TPU v7x, 512 devices: a whole 4x4x16 slice. The times are simulated.
512 devices in a mesh: pb: 128 (over z, x, core), vert: 4 (over y).
Axes of the slice: x: 4, y: 4, z: 16, core: 2. Of those that a mesh axis runs over, the one named last changes fastest.
Arguments:
- orbitals: bfloat16 [256, 32, 1024], P('pb', None, 'vert'), may hold values from -6 to 6
- transition: float32 [256, 256], P('pb'), may hold values from -0.9 to 0.9
- trial: float32 [8, 256, 256], P('vert', 'pb'), may hold values from -6 to 6
- screened: bfloat16 [256, 1024, 1024], P('pb', None, 'vert'), may hold values from -0.00030517578 to 0.00030517578
- bare: bfloat16 [1024, 1024], replicated, may hold values from -6.1035156e-05 to 6.1035156e-05
- cheb: float32 [3], replicated, may hold values from 0.5 to 1.5
- pair_k: int32 [384], P('pb'), may hold values from 0 to 255
- pair_slot: int32 [384], P('pb'), may hold values from 0 to 1
- k_order: int32 [256], replicated, may hold values from 0 to 255, each once
Outputs:
- filtered: float32 [8, 256, 256], P('vert', 'pb')
Inputs may be any that keep to these rules, and one draw needn't show every extreme that they name: The pair i lies with the owner of its momentum transfer 2 * (i // 3) + pair_slot[i]. `k_order`: A permutation of the k-points.
All inputs are finite; a program needn't handle non-finite values.
Results may differ from a plain program's by a relative error of at most 0.0075.
Values may be sent and summed in bfloat16 or wider, within the bound.
No kernel may reach another device: no remote copies, remote signals or barrier semaphores. Data moves between devices by JAX's collectives and lax.ppermute only.
A program may use at most 64 MiB of HBM per device.

v0:
```python
import jax
import jax.numpy as jnp
from jax import lax
from jax.sharding import Mesh
from jax.sharding import PartitionSpec as P

NV = 16
PB = ("pb_0", "pb_1", "pb_2")


def laid_out(blocks, dim):
    shape = list(blocks.shape[1:])
    shape[dim] *= blocks.shape[0]
    return jnp.moveaxis(blocks, 0, dim).reshape(shape)


def gather_in_order(shard, axes, turns):
    blocks = shard[None]
    for k in turns:
        blocks = lax.all_gather(blocks, axes[k], axis=0, tiled=True)
    block = [lax.axis_size(axes[k]) for k in reversed(turns)]
    blocks = blocks.reshape(*block, *shard.shape)
    turned = sorted(range(len(turns)), key=lambda place: turns[len(turns) - 1 - place])
    return blocks.transpose(*turned, *range(len(turns), blocks.ndim)).reshape(-1, *shard.shape)


def gather_axes(shard, axes, turns, dim):
    return laid_out(gather_in_order(shard, axes, turns), dim)


def copy_for_each(shard, axis):
    count = lax.axis_size(axis)
    return lax.all_to_all(
        jnp.broadcast_to(shard[None], (count, *shard.shape)), axis, 0, 0, tiled=True
    )


def collect(shard, axis, dim):
    return laid_out(copy_for_each(shard, axis), dim)


def of_everyone(shard, axis):
    return copy_for_each(shard, axis).sum(axis=0)


def gather_axes_2(shard, axes, dim):
    far, near = axes
    blocks = copy_for_each(copy_for_each(shard, far), near)
    return laid_out(blocks.swapaxes(0, 1).reshape(-1, *shard.shape), dim)


def split_up(shard, dim, count):
    before, after = (shard.shape[:dim], shard.shape[dim + 1 :])
    return jnp.moveaxis(shard.reshape(*before, count, -1, *after), dim, 0)


def summed_on_arrival(shard, axis, dim):
    count = lax.axis_size(axis)
    blocks = lax.all_to_all(split_up(shard, dim, count), axis, 0, 0, tiled=True)
    return jnp.sum(blocks, axis=0)


def sum_in_two_steps(shard, axes, dim):
    far, near = axes
    blocks = split_up(shard, dim, lax.axis_size(far))
    nearer = summed_on_arrival(blocks, near, dim + 1)
    arrived = lax.all_to_all(nearer, far, split_axis=0, concat_axis=0, tiled=True)
    return arrived.sum(axis=0)


def by_axis(shard, axes):
    far, near = axes
    nearer = of_everyone(shard, near)
    return of_everyone(nearer, far)


def body(orbitals, transition, trial, screened, bare, cheb, pair_k, pair_slot, k_order):
    kpoint_local = orbitals.shape[0]
    band_all = orbitals.shape[1]
    point_local = orbitals.shape[2]
    pair_count = pair_k.shape[0]
    kpoint_total = k_order.shape[0]
    valence = NV
    conduction = band_all - valence
    pair_width = valence * conduction
    end_count = 2 * pair_count
    hp = lax.Precision.HIGHEST
    position = lax.axis_index(PB)
    momentum = position * kpoint_local + pair_slot
    partner = jnp.mod(pair_k - momentum, kpoint_total)
    pair_ends = jnp.stack([pair_k, partner], axis=1).reshape(-1)
    owner_rows = jnp.arange(kpoint_total, dtype=jnp.int32)
    destination = jnp.sum(
        jnp.where(pair_ends[:, None] == k_order[None, :], owner_rows[None, :], 0), axis=1
    )
    shard_piece = gather_axes(orbitals, PB, (1, 0, 2), 0)
    row_count = shard_piece.shape[0]
    onehot = (destination[:, None] == jnp.arange(row_count, dtype=jnp.int32)[None, :]).astype(
        jnp.bfloat16
    )
    picked = jnp.dot(onehot, shard_piece.reshape(row_count, -1), preferred_element_type=jnp.float32)
    picked = picked.astype(jnp.bfloat16).reshape(end_count, band_all, point_local)
    val_points = collect(picked[:, :valence, :], "vert", 2)
    point_total = val_points.shape[2]
    val_pairs = val_points.reshape(pair_count, 2, valence, point_total)
    cond_pairs = picked[:, valence:, :].reshape(pair_count, 2, conduction, point_local)

    def build_block(pair_index):
        val_both = val_pairs[pair_index].astype(jnp.float32)
        cond_both = cond_pairs[pair_index].astype(jnp.float32)
        left_pair = (
            (val_both[0][:, None, :] * val_both[1][None, :, :])
            .reshape(valence * valence, point_total)
            .astype(jnp.bfloat16)
        )
        right_pair = (
            (cond_both[0][:, None, :] * cond_both[1][None, :, :])
            .reshape(conduction * conduction, point_local)
            .astype(jnp.bfloat16)
        )
        matrix = screened[pair_slot[pair_index]]
        half_product = jnp.dot(left_pair, matrix, preferred_element_type=jnp.float32).astype(
            jnp.bfloat16
        )
        block_part = lax.dot_general(
            half_product, right_pair, (((1,), (1,)), ((), ())), preferred_element_type=jnp.float32
        )
        return (
            block_part.reshape(valence, valence, conduction, conduction)
            .transpose(0, 2, 1, 3)
            .reshape(pair_width, pair_width)
        )

    block_parts = lax.map(build_block, jnp.arange(pair_count, dtype=jnp.int32))
    blocks = of_everyone(block_parts, "vert")
    gathered_own = collect(orbitals, "vert", 2).astype(jnp.float32)
    products = (
        (gathered_own[:, :valence, None, :] * gathered_own[:, None, valence:, :])
        .reshape(kpoint_local, pair_width, point_total)
        .astype(jnp.bfloat16)
    )

    def pick_trial(shard_piece):
        row_count = shard_piece.shape[1]
        onehot = (destination[:, None] == jnp.arange(row_count, dtype=jnp.int32)[None, :]).astype(
            jnp.bfloat16
        )
        return jnp.einsum("er,nrj->nej", onehot, shard_piece, preferred_element_type=jnp.float32)

    def apply_kernel(current):
        fetched = pick_trial(gather_axes_2(current, (("pb_0", "pb_1"), "pb_2"), 1)).astype(
            jnp.bfloat16
        )
        pair_view = fetched.astype(jnp.float32).reshape(fetched.shape[0], pair_count, 2, pair_width)
        toward_first = jnp.einsum("pij,npj->npi", blocks, pair_view[:, :, 1], precision=hp)
        toward_second = jnp.einsum("pij,npi->npj", blocks, pair_view[:, :, 0], precision=hp)
        results = jnp.stack([toward_first, toward_second], axis=2).reshape(
            fetched.shape[0], end_count, pair_width
        )
        onehot = (
            jnp.arange(kpoint_local * lax.axis_size(PB), dtype=jnp.int32)[:, None]
            == destination[None, :]
        ).astype(jnp.float32)
        screened_term = sum_in_two_steps(
            jnp.einsum("re,nej->rnj", onehot, results, precision=hp), (("pb_0", "pb_1"), "pb_2"), 0
        ).transpose(1, 0, 2)
        partial_density = jnp.einsum(
            "nkj,kjm->nm", current, products, preferred_element_type=jnp.float32
        )
        density = by_axis(partial_density, (("pb_0", "pb_1"), "pb_2")).astype(jnp.bfloat16)
        potential = jnp.einsum(
            "nv,mv->nm", density, bare, preferred_element_type=jnp.float32
        ).astype(jnp.bfloat16)
        bare_term = jnp.einsum(
            "kjm,nm->nkj", products, potential, preferred_element_type=jnp.float32
        )
        return transition[None] * current.astype(jnp.float32) + 2.0 * bare_term - screened_term

    first_step = apply_kernel(trial.astype(jnp.bfloat16))
    second_step = 2.0 * apply_kernel(first_step.astype(jnp.bfloat16)) - trial
    return cheb[0] * trial + cheb[1] * first_step + cheb[2] * second_step


def solution(mesh):
    split = Mesh(
        mesh.devices.reshape(16, 4, 2, mesh.shape["vert"]), ("pb_0", "pb_1", "pb_2", "vert")
    )
    in_specs = (
        P(PB, None, "vert"),
        P(PB, None),
        P("vert", PB, None),
        P(PB, None, "vert"),
        P(),
        P(),
        P(PB),
        P(PB),
        P(),
    )
    out_specs = P("vert", PB, None)
    return jax.shard_map(body, mesh=split, in_specs=in_specs, out_specs=out_specs, check_vma=False)
```

profile of v0, /device:TPU:4, one launch (start us, length us, event | category | flops | bytes accessed | tf_op | source)
XLA Modules:
  0.0 449.6 jit_solution(13693576423494758041)
XLA Ops:
  6.6 17.0 %all-gather = bf16[8,32,256]{2,1,0:T(8,128)(2,1)} all-gather(bf16[2,32,256]{2,1,0:T(8,128)(2,1)} %param.11), channel_id=2, replica_groups=mesh['pb_0'=16,'pb_1'=4,'pb_2'=2,'vert'=4] {'pb_1'}, dimensions={0}, use_global_device_ids=true | all-gather | bytes 163840 | tf_op jit(solution)/shard_map/all_gather | solution.py:20
  23.7 72.9 %all-gather.4.cloned.1.call-done = bf16[64,2,32,256]{3,2,1,0:T(8,128)(2,1)} async-done(((bf16[4,2,32,256]{3,2,1,0:T(8,128)(2,1)}), bf16[64,2,32,256]{3,2,1,0:T(8,128)(2,1)}) %all-gather.4.cloned.1.call-update) | async-done | bytes 2097168 | tf_op jit(solution)/shard_map/all_gather | solution.py:20
  97.3 4.3 all-to-all-start
  102.1 5.5 %all-to-all-done = bf16[4,2,32,256]{3,2,1,0:T(8,128)(2,1)S(1)} async-done(((bf16[4,2,32,256]{3,2,1,0:T(8,128)(2,1)}), bf16[4,2,32,256]{3,2,1,0:T(8,128)(2,1)S(1)}, u32[]{:S(2)}, u32[]{:S(2)}) %all-to-all-start) | async-done | bytes 131104 | tf_op jit(solution)/shard_map/all_to_all | solution.py:33
  108.3 11.3 %all-to-all-start.3 = ((bf16[64,2,2,256]{3,2,1,0:T(2,128)(2,1)}), bf16[64,2,2,256]{3,2,1,0:T(2,128)(2,1)S(1)}, u32[]{:S(2)}, u32[]{:S(2)}) async-start(bf16[64,2,2,256]{3,2,1,0:T(2,128)(2,1)} %broadcast_in_dim.50), calls=%async_computation.3 | async-start | bytes 262144 | tf_op jit(solution)/shard_map/all_to_all | solution.py:33
  119.9 2.6 copy.171
  122.5 4.3 copy.205
  128.2 5.8 %all-to-all-done.3 = bf16[64,2,2,256]{3,2,1,0:T(2,128)(2,1)S(1)} async-done(((bf16[64,2,2,256]{3,2,1,0:T(2,128)(2,1)}), bf16[64,2,2,256]{3,2,1,0:T(2,128)(2,1)S(1)}, u32[]{:S(2)}, u32[]{:S(2)}) %all-to-all-start.3) | async-done | bytes 131104 | tf_op jit(solution)/shard_map/all_to_all | solution.py:33
  134.6 3.4 all-to-all-start.5
  139.0 5.3 %all-to-all-done.5 = bf16[4,6,16,256]{3,2,1,0:T(8,128)(2,1)S(1)} async-done(((bf16[4,6,16,256]{3,2,1,0:T(8,128)(2,1)}), bf16[4,6,16,256]{3,2,1,0:T(8,128)(2,1)S(1)}, u32[]{:S(2)}, u32[]{:S(2)}) %all-to-all-start.5) | async-done | bytes 196640 | tf_op jit(solution)/shard_map/all_to_all | solution.py:33
  144.9 3.2 all-to-all-start.1
  149.7 43.2 %while.10 = (s32[]{:T(128)}, f32[3,256,256]{2,1,0:T(8,128)}, s32[3]{0:T(128)}, bf16[3,2,16,1024]{3,2,1,0:T(8,128)(2,1)}, s32[3]{0:T(128)}, /*index=5*/bf16[2,102...) while((s32[]{:T(128)}, f32[3,256,256]{2,1,0:T(8,128)}, ...), condition=%wide.region_4.5_spmd, body=%wide.region_3.4_spmd.sunk | while | flops 168534016 | bytes 3883733 | solution.py:134
  149.7 1.3 dynamic_slice.30
  152.9 1.3 dynamic_slice.31
  156.1 0.9 dynamic-slice_convert_fusion.4
  157.0 1.3 convolution_convert_fusion.7
  159.1 1.8 convolution_bitcast_fusion.10
  160.9 2.4 broadcast_in_dim.69
  164.1 1.3 dynamic_slice.30
  167.3 1.3 dynamic_slice.31
  170.4 0.9 dynamic-slice_convert_fusion.4
  171.4 1.3 convolution_convert_fusion.7
  173.5 1.8 convolution_bitcast_fusion.10
  175.3 2.4 broadcast_in_dim.69
  178.4 1.3 dynamic_slice.30
  181.6 1.3 dynamic_slice.31
  185.8 1.3 convolution_convert_fusion.7
  187.8 1.8 convolution_bitcast_fusion.10
  189.6 2.4 broadcast_in_dim.69
  193.0 3.9 all_to_all.75
  196.9 3.1 broadcast_in_dim.55
  200.0 5.0 %all-to-all-start.6 = ((f32[4,3,256,256]{3,2,1,0:T(8,128)}), f32[4,3,256,256]{3,2,1,0:T(8,128)}, u32[]{:S(2)}, u32[]{:S(2)}) async-start(f32[4,3,256,256]{3,2,1,0:T(8,128)} %broadcast_in_dim.55), calls=%async_computation.6 | async-start | bytes 6291456 | tf_op jit(solution)/shard_map/all_to_all | solution.py:33
  206.2 1.1 fusion.7
  207.4 35.7 %all-to-all-done.6 = f32[4,3,256,256]{3,2,1,0:T(8,128)} async-done(((f32[4,3,256,256]{3,2,1,0:T(8,128)}), f32[4,3,256,256]{3,2,1,0:T(8,128)}, u32[]{:S(2)}, u32[]{:S(2)}) %all-to-all-start.6) | async-done | bytes 3145760 | tf_op jit(solution)/shard_map/all_to_all | solution.py:33
  243.0 3.1 reduce_sum.93
  246.1 1.6 convolution_bitcast_fusion.8
  247.7 1.5 convolution_bitcast_fusion.7
  249.8 4.9 %all_to_all.76 = f32[2,64,2,2,256]{4,1,3,2,0:T(8,128)} all-to-all(f32[2,64,2,2,256]{4,1,3,2,0:T(8,128)S(1)} %convolution_bitcast_fusion.2), channel_id=1, replica_groups=mesh['pb_0'=16,'pb_1'=4,'pb_2'=2,'vert'=4] {'pb_2'}, dimensions={0} | all-to-all | bytes 1048576 | tf_op jit(solution)/shard_map/all_to_all | solution.py:59
  254.7 0.9 broadcast_in_dim.46
  255.6 11.1 %all-to-all-start.2 = ((f32[64,2,1024]{2,1,0:T(2,128)}), f32[64,2,1024]{2,1,0:T(2,128)}, u32[]{:S(2)}, u32[]{:S(2)}) async-start(f32[64,2,1024]{2,1,0:T(2,128)} %broadcast_in_dim.46), calls=%async_computation.2 | async-start | bytes 1048576 | tf_op jit(solution)/shard_map/all_to_all | solution.py:33
  266.7 1.1 reduce_sum.94
  267.8 0.9 copy.176
  268.7 30.9 %all-to-all-done.2 = f32[64,2,1024]{2,1,0:T(2,128)} async-done(((f32[64,2,1024]{2,1,0:T(2,128)}), f32[64,2,1024]{2,1,0:T(2,128)}, u32[]{:S(2)}, u32[]{:S(2)}) %all-to-all-start.2) | async-done | bytes 524320 | tf_op jit(solution)/shard_map/all_to_all | solution.py:33
  299.6 5.9 %all-to-all-start.8 = ((f32[64,2,2,256]{3,2,1,0:T(2,128)}), f32[64,2,2,256]{3,2,1,0:T(2,128)S(1)}, u32[]{:S(2)}, u32[]{:S(2)}) async-start(f32[64,2,2,256]{3,2,1,0:T(2,128)} %copy.176), calls=%async_computation.8 | async-start | bytes 524288 | tf_op jit(solution)/shard_map/all_to_all | solution.py:67
  305.6 1.2 reduce_sum.91
  306.8 19.7 %all-to-all-done.8 = f32[64,2,2,256]{3,2,1,0:T(2,128)S(1)} async-done(((f32[64,2,2,256]{3,2,1,0:T(2,128)}), f32[64,2,2,256]{3,2,1,0:T(2,128)S(1)}, u32[]{:S(2)}, u32[]{:S(2)}) %all-to-all-start.8) | async-done | bytes 262176 | tf_op jit(solution)/shard_map/all_to_all | solution.py:67
  326.6 0.9 fusion.44
  328.3 6.0 %all-to-all-start.11 = ((bf16[64,2,2,256]{3,2,1,0:T(2,128)(2,1)}), bf16[64,2,2,256]{3,2,1,0:T(2,128)(2,1)S(1)}, u32[]{:S(2)}, u32[]{:S(2)}) async-start(bf16[64,2,2,256]{3,2,1,0:T(2,128)(2,1)} %broadcast_in_dim.58), calls=%async_computation.11 | async-start | bytes 262144 | tf_op jit(solution)/shard_map/all_to_all | solution.py:33
  334.6 14.8 %all-to-all-done.11 = bf16[64,2,2,256]{3,2,1,0:T(2,128)(2,1)S(1)} async-done(((bf16[64,2,2,256]{3,2,1,0:T(2,128)(2,1)}), bf16[64,2,2,256]{3,2,1,0:T(2,128)(2,1)S(1)}, u32[]{:S(2)}, u32[]{:S(2)}) %all-to-all-start.11) | async-done | bytes 131104 | tf_op jit(solution)/shard_map/all_to_all | solution.py:33
  349.6 3.9 all_to_all.77
  354.7 1.1 fusion.8
  355.8 1.6 convolution_bitcast_fusion.6
  357.5 1.5 convolution_bitcast_fusion.5
  359.5 4.9 %all_to_all.78 = f32[2,64,2,2,256]{4,1,3,2,0:T(8,128)} all-to-all(f32[2,64,2,2,256]{4,1,3,2,0:T(8,128)S(1)} %convolution_bitcast_fusion.1), channel_id=1, replica_groups=mesh['pb_0'=16,'pb_1'=4,'pb_2'=2,'vert'=4] {'pb_2'}, dimensions={0} | all-to-all | bytes 1048576 | tf_op jit(solution)/shard_map/all_to_all | solution.py:59
  365.0 3.2 all-to-all-start.9
  368.3 1.1 reduce_sum.98
  369.4 0.9 copy.187
  370.3 6.0 %all-to-all-start.14 = ((f32[64,2,2,256]{3,2,1,0:T(2,128)}), f32[64,2,2,256]{3,2,1,0:T(2,128)S(1)}, u32[]{:S(2)}, u32[]{:S(2)}) async-start(f32[64,2,2,256]{3,2,1,0:T(2,128)} %copy.187), calls=%async_computation.14 | async-start | bytes 524288 | tf_op jit(solution)/shard_map/all_to_all | solution.py:67
  376.3 22.5 %all-to-all-done.14 = f32[64,2,2,256]{3,2,1,0:T(2,128)S(1)} async-done(((f32[64,2,2,256]{3,2,1,0:T(2,128)}), f32[64,2,2,256]{3,2,1,0:T(2,128)S(1)}, u32[]{:S(2)}, u32[]{:S(2)}) %all-to-all-start.14) | async-done | bytes 262176 | tf_op jit(solution)/shard_map/all_to_all | solution.py:67
  398.8 0.9 broadcast_in_dim.57
  399.7 6.2 %all-to-all-start.10 = ((f32[64,2,1024]{2,1,0:T(2,128)}), f32[64,2,1024]{2,1,0:T(2,128)}, u32[]{:S(2)}, u32[]{:S(2)}) async-start(f32[64,2,1024]{2,1,0:T(2,128)} %broadcast_in_dim.57), calls=%async_computation.10 | async-start | bytes 1048576 | tf_op jit(solution)/shard_map/all_to_all | solution.py:33
  406.6 31.5 %all-to-all-done.10 = f32[64,2,1024]{2,1,0:T(2,128)} async-done(((f32[64,2,1024]{2,1,0:T(2,128)}), f32[64,2,1024]{2,1,0:T(2,128)}, u32[]{:S(2)}, u32[]{:S(2)}) %all-to-all-start.10) | async-done | bytes 524320 | tf_op jit(solution)/shard_map/all_to_all | solution.py:33
  438.1 1.2 reduce_sum.97
  439.3 2.8 fusion.16
  (103 shorter events, 19.7 us)
Async XLA Ops:
  6.5 320.1 %copy-start = (bf16[1024,1024]{1,0:T(8,128)(2,1)S(1)}, bf16[1024,1024]{1,0:T(8,128)(2,1)}, u32[]{:S(2)}) copy-start(bf16[1024,1024]{1,0:T(8,128)(2,1)} %param.15) | copy-start | bytes 6291460
  6.5 90.1 %copy-start.2 = (bf16[2,32,256]{2,1,0:T(8,128)(2,1)S(1)}, bf16[2,32,256]{2,1,0:T(8,128)(2,1)}, u32[]{:S(2)}) copy-start(bf16[2,32,256]{2,1,0:T(8,128)(2,1)} %param.11) | copy-start | bytes 98308
  6.5 95.1 %copy-start.11 = (s32[3]{0:T(128)S(1)}, s32[3]{0:T(128)}, u32[]{:S(2)}) copy-start(s32[3]{0:T(128)} %param.17) | copy-start | bytes 40
  6.5 95.1 %copy-start.13 = (s32[3]{0:T(128)S(1)}, s32[3]{0:T(128)}, u32[]{:S(2)}) copy-start(s32[3]{0:T(128)} %param.18) | copy-start | bytes 40
  6.5 95.3 %copy-start.5 = (f32[2,2,256]{2,1,0:T(2,128)S(1)}, f32[2,2,256]{2,1,0:T(2,128)}, u32[]{:S(2)}) copy-start(f32[2,2,256]{2,1,0:T(2,128)} %param.13) | copy-start | bytes 12292
  6.6 95.3 %copy-start.12 = (s32[256]{0:T(256)S(1)}, s32[256]{0:T(256)}, u32[]{:S(2)}) copy-start(s32[256]{0:T(256)} %param.19) | copy-start | bytes 3076
  6.6 90.1 %all-gather.4.cloned.1.call-start = ((), (), s32[]{:S(2)}) async-start(), calls=%async_computation.15 | async-start | bytes 2228224 | tf_op jit(solution)/shard_map/all_gather | solution.py:20
  23.6 96.2 %all-gather.6.cloned.1.call-start = ((), (), s32[]{:S(2)}) async-start(), calls=%async_computation.16 | async-start | bytes 6291456 | tf_op jit(solution)/shard_map/all_gather | solution.py:20
  97.3 10.3 %all-to-all-start = ((bf16[4,2,32,256]{3,2,1,0:T(8,128)(2,1)}), bf16[4,2,32,256]{3,2,1,0:T(8,128)(2,1)S(1)}, u32[]{:S(2)}, u32[]{:S(2)}) async-start(bf16[4,2,32,256]{3,2,1,0:T(8,128)(2,1)} %broadcast_in_dim.44), calls=%async_computation | async-start | bytes 262144 | tf_op jit(solution)/shard_map/all_to_all | solution.py:33
  101.8 36.2 %copy-start.3 = (bf16[2,2,256]{2,0,1:T(2,128)(2,1)}, bf16[2,2,256]{2,0,1:T(2,128)(2,1)S(1)}, u32[]{:S(2)}) copy-start(bf16[2,2,256]{2,0,1:T(2,128)(2,1)S(1)} %copy.214) | copy-start | bytes 6148
  102.1 24.7 %copy-start.7 = (s32[6]{0:T(128)}, s32[6]{0:T(128)S(1)}, u32[]{:S(2)}) copy-start(s32[6]{0:T(128)S(1)} %select_reduce_fusion) | copy-start | bytes 76
  108.3 25.6 %all-to-all-start.3 = ((bf16[64,2,2,256]{3,2,1,0:T(2,128)(2,1)}), bf16[64,2,2,256]{3,2,1,0:T(2,128)(2,1)S(1)}, u32[]{:S(2)}, u32[]{:S(2)}) async-start(bf16[64,2,2,256]{3,2,1,0:T(2,128)(2,1)} %broadcast_in_dim.50), calls=%async_computation.3 | async-start | bytes 262144 | tf_op jit(solution)/shard_map/all_to_all | solution.py:33
  134.6 9.7 %all-to-all-start.5 = ((bf16[4,6,16,256]{3,2,1,0:T(8,128)(2,1)}), bf16[4,6,16,256]{3,2,1,0:T(8,128)(2,1)S(1)}, u32[]{:S(2)}, u32[]{:S(2)}) async-start(bf16[4,6,16,256]{3,2,1,0:T(8,128)(2,1)} %broadcast_in_dim.54), calls=%async_computation.5 | async-start | bytes 393216 | tf_op jit(solution)/shard_map/all_to_all | solution.py:33
  144.9 47.9 %all-to-all-start.1 = ((f32[2,2,1024]{2,1,0:T(2,128)}), f32[2,2,1024]{2,1,0:T(2,128)S(1)}, u32[]{:S(2)}, u32[]{:S(2)}) async-start(f32[2,2,1024]{2,1,0:T(2,128)} %broadcast_in_dim.45), calls=%async_computation.1 | async-start | bytes 32768 | tf_op jit(solution)/shard_map/all_to_all | solution.py:33
  149.7 43.2 %copy-start.1 = (bf16[64,2,2,256]{3,2,0,1:T(2,128)(2,1)S(1)}, bf16[64,2,2,256]{3,2,0,1:T(2,128)(2,1)}, u32[]{:S(2)}) copy-start(bf16[64,2,2,256]{3,2,0,1:T(2,128)(2,1)} %copy.166) | copy-start | bytes 393220
  200.0 6.2 %copy-start.8 = (s32[6]{0:T(128)S(1)}, s32[6]{0:T(128)}, u32[]{:S(2)}) copy-start(s32[6]{0:T(128)} %copy-done.7) | copy-start | bytes 76
  200.0 43.0 %all-to-all-start.6 = ((f32[4,3,256,256]{3,2,1,0:T(8,128)}), f32[4,3,256,256]{3,2,1,0:T(8,128)}, u32[]{:S(2)}, u32[]{:S(2)}) async-start(f32[4,3,256,256]{3,2,1,0:T(8,128)} %broadcast_in_dim.55), calls=%async_computation.6 | async-start | bytes 6291456 | tf_op jit(solution)/shard_map/all_to_all | solution.py:33
  254.7 71.9 %copy-start.4 = (bf16[2,2,256]{2,0,1:T(2,128)(2,1)S(1)}, bf16[2,2,256]{2,0,1:T(2,128)(2,1)}, u32[]{:S(2)}) copy-start(bf16[2,2,256]{2,0,1:T(2,128)(2,1)} %copy-done.3) | copy-start | bytes 6148
  254.7 71.9 %copy-start.9 = (f32[2,256]{1,0:T(2,128)S(1)}, f32[2,256]{1,0:T(2,128)}, u32[]{:S(2)}) copy-start(f32[2,256]{1,0:T(2,128)} %param.12) | copy-start | bytes 6148
  255.6 44.0 %all-to-all-start.2 = ((f32[64,2,1024]{2,1,0:T(2,128)}), f32[64,2,1024]{2,1,0:T(2,128)}, u32[]{:S(2)}, u32[]{:S(2)}) async-start(f32[64,2,1024]{2,1,0:T(2,128)} %broadcast_in_dim.46), calls=%async_computation.2 | async-start | bytes 1048576 | tf_op jit(solution)/shard_map/all_to_all | solution.py:33
  299.6 26.9 %all-to-all-start.8 = ((f32[64,2,2,256]{3,2,1,0:T(2,128)}), f32[64,2,2,256]{3,2,1,0:T(2,128)S(1)}, u32[]{:S(2)}, u32[]{:S(2)}) async-start(f32[64,2,2,256]{3,2,1,0:T(2,128)} %copy.176), calls=%async_computation.8 | async-start | bytes 524288 | tf_op jit(solution)/shard_map/all_to_all | solution.py:67
  328.3 21.1 %all-to-all-start.11 = ((bf16[64,2,2,256]{3,2,1,0:T(2,128)(2,1)}), bf16[64,2,2,256]{3,2,1,0:T(2,128)(2,1)S(1)}, u32[]{:S(2)}, u32[]{:S(2)}) async-start(bf16[64,2,2,256]{3,2,1,0:T(2,128)(2,1)} %broadcast_in_dim.58), calls=%async_computation.11 | async-start | bytes 262144 | tf_op jit(solution)/shard_map/all_to_all | solution.py:33
  359.5 46.3 %copy-start.10 = (f32[3]{0:T(128)S(1)}, f32[3]{0:T(128)}, u32[]{:S(2)}) copy-start(f32[3]{0:T(128)} %param.16) | copy-start | bytes 40
  365.0 5.3 %all-to-all-start.9 = ((f32[2,2,1024]{2,1,0:T(2,128)}), f32[2,2,1024]{2,1,0:T(2,128)S(1)}, u32[]{:S(2)}, u32[]{:S(2)}) async-start(f32[2,2,1024]{2,1,0:T(2,128)} %broadcast_in_dim.56), calls=%async_computation.9 | async-start | bytes 32768 | tf_op jit(solution)/shard_map/all_to_all | solution.py:33
  368.3 71.1 %copy-start.6 = (f32[2,2,256]{2,1,0:T(2,128)S(1)}, f32[2,2,256]{2,1,0:T(2,128)}, u32[]{:S(2)}) copy-start(f32[2,2,256]{2,1,0:T(2,128)} %param.13) | copy-start | bytes 12292
  370.3 28.5 %all-to-all-start.14 = ((f32[64,2,2,256]{3,2,1,0:T(2,128)}), f32[64,2,2,256]{3,2,1,0:T(2,128)S(1)}, u32[]{:S(2)}, u32[]{:S(2)}) async-start(f32[64,2,2,256]{3,2,1,0:T(2,128)} %copy.187), calls=%async_computation.14 | async-start | bytes 524288 | tf_op jit(solution)/shard_map/all_to_all | solution.py:67
  399.7 38.4 %all-to-all-start.10 = ((f32[64,2,1024]{2,1,0:T(2,128)}), f32[64,2,1024]{2,1,0:T(2,128)}, u32[]{:S(2)}, u32[]{:S(2)}) async-start(f32[64,2,1024]{2,1,0:T(2,128)} %broadcast_in_dim.57), calls=%async_computation.10 | async-start | bytes 1048576 | tf_op jit(solution)/shard_map/all_to_all | solution.py:33
Sparse Core Ops, SparseCore 0:
  23.8 72.8 all-gather.3
  98.7 21.0 all-gather.5
where the time goes:
time: 452 us; the launch traced here: 450 us
  waiting for transfers between devices  245 us (54%)
  starting transfers between devices  65.6 us (15%)
  local copies, waits for them, and re-layouts  42.1 us (9%)
  blocking collectives  34.7 us (8%)
  matrix products  23.8 us (5%)
  between operations  13.8 us (3%)
  other arithmetic  13.4 us (3%)
  loops' own time  11.5 us (3%)
    all_to_all x9, waiting for transfers between devices, copy_for_each(): lax.all_to_all(jnp.broadcast_to(shard[None], (count, *shard.shape)), axis...  129 us
    all_gather x2, waiting for transfers between devices, gather_in_order(): blocks = lax.all_gather(blocks, axes[k], axis=0, tiled=True)  73 us
    all_to_all x9, starting transfers between devices, copy_for_each(): lax.all_to_all(jnp.broadcast_to(shard[None], (count, *shard.shape)), axis...  53.6 us
    all_to_all x2, waiting for transfers between devices, sum_in_two_steps(): lax.all_to_all(nearer, far, split_axis=0, concat_axis=0, tiled=True)  42.2 us
    all_gather x1, blocking collectives, gather_in_order(): blocks = lax.all_gather(blocks, axes[k], axis=0, tiled=True)  17 us
    all_to_all x2, starting transfers between devices, sum_in_two_steps(): lax.all_to_all(nearer, far, split_axis=0, concat_axis=0, tiled=True)  11.9 us
    another operation x1, loops' own time, body(): block_parts = lax.map(build_block, jnp.arange(pair_count, dtype=jnp.int32))  11.5 us
    all_to_all x2, blocking collectives, summed_on_arrival(): blocks = lax.all_to_all(split_up(shard, dim, count), axis, 0, 0, tiled=True)  9.81 us
  transfers between devices with their start and end apart: 13, of which 10 were waited for; matrix products, arithmetic and copies ran while one was open for 12% of the time, Pallas kernels for 0%

commit v1 on v0

v1 whole, which is shorter than its diff:
```python
import functools

import jax
import jax.numpy as jnp
from jax import lax
from jax.experimental import pallas as pl
from jax.experimental.pallas import tpu as pltpu
from jax.sharding import Mesh
from jax.sharding import PartitionSpec as P

BF = jnp.bfloat16
F32 = jnp.float32
NV = 16
LAST = (((1,), (1,)), ((), ()))
PB = ("z", "x", "c")
PLANE = ("x", "c")
BLOCK = ("x", "c", "y")


def exchange(blocks, axis):
    return lax.all_to_all(blocks, axis, 0, 0, tiled=True)


def to_everyone(shard, axis):
    count = lax.axis_size(axis)
    return exchange(jnp.broadcast_to(shard[None], (count, *shard.shape)), axis)


def dot(a, b):
    return jnp.dot(a, b, preferred_element_type=F32)


def dot_t(a, b):
    return lax.dot_general(a, b, LAST, preferred_element_type=F32)


def call(kernel, outs, smem, scratch=()):
    def run(*args):
        specs = [
            pl.BlockSpec(memory_space=pltpu.SMEM if k in smem else pltpu.VMEM)
            for k in range(len(args))
        ]
        return pl.pallas_call(
            kernel,
            out_shape=[jax.ShapeDtypeStruct(s, d) for s, d in outs],
            in_specs=specs,
            out_specs=[pl.BlockSpec(memory_space=pltpu.VMEM) for _ in outs],
            scratch_shapes=list(scratch),
        )(*args)

    return run


def lanes(rows, width):
    return lax.broadcasted_iota(jnp.int32, (rows, width), 1)


def products_of(own_ref, s, part):
    val = own_ref[part, s, 0:16, :].astype(F32)
    cond = own_ref[part, s, 16:32, :].astype(F32)
    pieces = [(val[v : v + 1, :] * cond).astype(BF) for v in range(16)]
    return jnp.concatenate(pieces, axis=0)


def density_of(own_ref, rows_bf):
    parts = []
    for part in range(4):
        total = dot(rows_bf[0], products_of(own_ref, 0, part))
        total = total + dot(rows_bf[1], products_of(own_ref, 1, part))
        parts.append(total)
    return parts


def bare_of(own_ref, bare_ref, dens):
    pots = []
    for out in range(4):
        total = jnp.zeros((2, 256), F32)
        for part in range(4):
            total = total + dot_t(
                dens[part].astype(BF),
                bare_ref[out * 256 : (out + 1) * 256, part * 256 : (part + 1) * 256],
            )
        pots.append(total.astype(BF))
    terms = []
    for s in range(2):
        total = jnp.zeros((2, 256), F32)
        for part in range(4):
            total = total + dot_t(pots[part], products_of(own_ref, s, part))
        terms.append(total)
    return terms


def pack_kernel(info_ref, orb_ref, trial_ref, own_ref, out_ref, tail_ref):
    out_ref[0:64, :] = orb_ref[...].reshape(64, 256)
    rows = [trial_ref[:, s, :].astype(BF) for s in range(2)]
    parts = density_of(own_ref, rows)
    tail_ref[...] = jnp.zeros((16, 256), F32)
    for s in range(2):
        tail_ref[2 * s : 2 * s + 2, :] = rows[s].astype(F32)
    for part in range(4):
        tail_ref[4 + 2 * part : 6 + 2 * part, :] = parts[part]
    kind = lax.rem(lanes(1, 256), 16) // 2
    ids = jnp.zeros((1, 256), jnp.int32)
    for e in range(8):
        ids = jnp.where(kind == e, info_ref[e], ids)
    tail_ref[12:13, :] = ids.astype(F32)
    out_ref[64:80, :] = tail_ref[...].astype(BF)


def select_kernel(plane_ref, gat_ref, out_ref, pick_ref):
    lane = lanes(1, 256)
    pick_ref[...] = jnp.zeros((256, 256), F32)
    for peer in range(8):
        for e in range(6):
            row = plane_ref[peer * 8 + e]
            z = row // 16
            s = lax.rem(row, 2)
            for n in range(2):
                at = peer * 32 + 2 * e + n
                pick_ref[at : at + 1, :] = (lane == z * 16 + 2 * s + n).astype(F32)

            @pl.when(s == 0)
            def _():
                out_ref[peer, 32 * e : 32 * e + 32, :] = gat_ref[z, 0:32, :]

            @pl.when(s == 1)
            def _():
                out_ref[peer, 32 * e : 32 * e + 32, :] = gat_ref[z, 32:64, :]

        for d in range(8):
            at = peer * 32 + 16 + d
            pick_ref[at : at + 1, :] = (lax.rem(lane, 16) == 4 + d).astype(F32)
    tails = gat_ref[:, 64:80, :].reshape(256, 256)
    picked = dot(pick_ref[...].astype(BF), tails).astype(BF)
    out_ref[:, 192:224, :] = picked.reshape(8, 32, 256)


def accept_kernel(info_ref, got_ref, val_ref, cond_ref, dens_ref, tail_ref):
    for e in range(6):
        column = lax.rem(info_ref[e] // 2, 8)
        val_ref[16 * e : 16 * e + 16, :] = got_ref[column, 32 * e : 32 * e + 16, :]
        cond_ref[e] = got_ref[column, 32 * e + 16 : 32 * e + 32, :]
        part = got_ref[column, 192:208, :].astype(F32)
        tail_ref[2 * e : 2 * e + 2, :] = part[2 * e : 2 * e + 2, :]
    tail_ref[12:16, :] = jnp.zeros((4, 256), F32)
    val_ref[96:112, :] = tail_ref[...].astype(BF)
    total = got_ref[0, 208:224, :].astype(F32)
    for peer in range(1, 8):
        total = total + got_ref[peer, 208:224, :].astype(F32)
    dens_ref[...] = total[0:8, :]


def base_kernel(
    info_ref, plane_ref, dens_ref, gat_ref, own_ref, bare_ref, trans_ref, trial_ref,
    base_ref, route_ref, back_ref, base_s, route_s,
):
    dens = [dens_ref[2 * part : 2 * part + 2, :] for part in range(4)]
    terms = bare_of(own_ref, bare_ref, dens)
    for s in range(2):
        x = trial_ref[:, s, :].astype(BF).astype(F32)
        base_s[2 * s : 2 * s + 2, :] = trans_ref[s : s + 1, :] * x + 2.0 * terms[s]
    base_ref[...] = base_s[...]

    lane = lanes(1, 256)
    held = jnp.zeros((1, 256), F32)
    for z in range(16):
        row = gat_ref[z, 64:80, :].astype(F32)[12:13, :]
        held = jnp.where(lane // 16 == z, row, held)
    held = held.astype(jnp.int32)
    sign = jnp.where(lax.rem(lane, 16) < 12, -1.0, 1.0)
    parity = lax.rem(lane, 2)
    z_me = info_ref[8]
    q_me = info_ref[9]
    for peer in range(8):
        for k in range(8):
            row = plane_ref[peer * 8 + k] if k < 6 else z_me * 16 + peer * 2 + (k - 6)
            for n in range(2):
                at = peer * 16 + 2 * k + n
                hit = (held == row) & (parity == n)
                route_s[at : at + 1, :] = jnp.where(hit, sign, 0.0)
    route_ref[...] = route_s[...].astype(BF)

    wide = lanes(1, 512)
    sent = jnp.full((1, 512), -1, jnp.int32)
    for peer in range(8):
        for e in range(6):
            here = (wide // 64 == peer) & (lax.rem(wide, 16) // 2 == e)
            sent = jnp.where(here, plane_ref[peer * 8 + e], sent)
    row = lax.broadcasted_iota(jnp.int32, (64, 512), 0)
    target = (row // 4) * 16 + q_me * 2 + lax.rem(row, 4) // 2
    hit = (sent == target) & (lax.rem(row, 2) == lax.rem(lanes(64, 512), 2))
    back_ref[...] = jnp.where(hit, -1.0, 0.0).astype(BF)


def spread(x):
    rows = jnp.concatenate([x] * 16, axis=0)
    group = lax.broadcasted_iota(jnp.int32, (128, 256), 0) // 8
    return jnp.where(group == lanes(128, 256) // 16, rows, 0.0).astype(BF)


def gathered(full):
    group = lax.broadcasted_iota(jnp.int32, (128, 256), 0) // 8
    kept = jnp.where(group == lanes(128, 256) // 16, full, 0.0)
    total = kept[0:8, :]
    for v in range(1, 16):
        total = total + kept[8 * v : 8 * v + 8, :]
    return total


def apply_pair(i, half_ref, cond_ref, xs_ref, ys_ref, t_ref, u_ref):
    tile_a = jnp.concatenate([cond_ref[2 * i]] * 16, axis=0)
    tile_c = jnp.concatenate([cond_ref[2 * i + 1]] * 16, axis=0)
    t_ref[0] = dot(spread(xs_ref[2 * i]), tile_a)
    t_ref[1] = dot(spread(xs_ref[2 * i + 1]), tile_c)
    u_ref[1] = jnp.zeros((128, 256), F32)

    def over_first(v, carry):
        at = pl.multiple_of(v * 8, 8)
        t_a = t_ref[0, pl.ds(at, 8), :]
        total = jnp.zeros((8, 256), F32)
        for w in range(16):
            h = jnp.broadcast_to(half_ref[i, pl.ds(v * 16 + w, 1), :], (8, 256))
            total = total + h * t_ref[1, 8 * w : 8 * w + 8, :]
            u_ref[1, 8 * w : 8 * w + 8, :] += h * t_a
        u_ref[0, pl.ds(at, 8), :] = total
        return carry

    lax.fori_loop(0, 16, over_first, 0)
    ys_ref[2 * i] = gathered(dot_t(u_ref[0].astype(BF), tile_a))
    ys_ref[2 * i + 1] = gathered(dot_t(u_ref[1].astype(BF), tile_c))


def first_kernel(
    info_ref, wide_ref, cond_ref, scr_ref, base_ref, half_ref, res_ref,
    xs_ref, ys_ref, t_ref, u_ref, rs_ref,
):
    for part in range(4):
        tail = wide_ref[part, 96:112, :].astype(F32)
        for e in range(6):
            xs_ref[e, 2 * part : 2 * part + 2, :] = tail[2 * e : 2 * e + 2, :]

    def one(i, carry):
        slot = info_ref[11 + i]
        total = jnp.zeros((256, 256), F32)
        for part in range(4):
            at = pl.multiple_of(i * 32, 16)
            a = wide_ref[part, pl.ds(at, 16), :].astype(F32)
            b = wide_ref[part, pl.ds(at + 16, 16), :].astype(F32)
            left = jnp.concatenate(
                [(a[v : v + 1, :] * b).astype(BF) for v in range(16)], axis=0
            )
            total = total + dot(left, scr_ref[slot, part * 256 : (part + 1) * 256, :])
        half_ref[i] = total.astype(BF).astype(F32)
        apply_pair(i, half_ref, cond_ref, xs_ref, ys_ref, t_ref, u_ref)
        return carry

    lax.fori_loop(0, 3, one, 0)
    for part in range(4):
        for e in range(6):
            rs_ref[part, 2 * e : 2 * e + 2, :] = ys_ref[e, 2 * part : 2 * part + 2, :]
        mine = (info_ref[10] == part).astype(F32)
        rs_ref[part, 12:16, :] = base_ref[...] * mine
    res_ref[...] = rs_ref[...].astype(BF)


def middle_kernel(route_ref, col_ref, out_ref):
    full = dot(route_ref[...], col_ref[...].reshape(256, 256)).astype(BF)
    for peer in range(8):
        for part in range(4):
            out_ref[4 * peer + part] = full[16 * peer : 16 * peer + 16, :]


def second_kernel(
    info_ref, got_ref, half_ref, cond_ref, own_ref, out_ref, own_x_ref,
    xs_ref, ys_ref, t_ref, u_ref, rs_ref, ds_ref,
):
    for part in range(4):
        total = got_ref[part].astype(F32)
        for peer in range(1, 8):
            total = total + got_ref[4 * peer + part].astype(F32)
        for e in range(6):
            xs_ref[e, 2 * part : 2 * part + 2, :] = total[2 * e : 2 * e + 2, :]
    y_me = info_ref[10]
    total = got_ref[y_me].astype(F32)
    for peer in range(1, 8):
        total = total + got_ref[4 * peer + y_me].astype(F32)
    own_x_ref[...] = total[12:16, :]
    rows = [total[12 + 2 * s : 14 + 2 * s, :].astype(BF) for s in range(2)]
    parts = density_of(own_ref, rows)
    for part in range(4):
        for h in range(2):
            at = 4 * part + 2 * h
            ds_ref[at : at + 2, :] = parts[part][:, 128 * h : 128 * h + 128]

    def one(i, carry):
        apply_pair(i, half_ref, cond_ref, xs_ref, ys_ref, t_ref, u_ref)
        return carry

    lax.fori_loop(0, 3, one, 0)
    rs_ref[...] = jnp.zeros((4, 16, 256), F32)
    for part in range(4):
        for e in range(6):
            rs_ref[part, 2 * e : 2 * e + 2, :] = ys_ref[e, 2 * part : 2 * part + 2, :]
    for peer in range(8):
        for part in range(4):
            out_ref[4 * peer + part, :, 0:256] = rs_ref[part].astype(BF)
            out_ref[4 * peer + part, :, 256:384] = ds_ref[...].astype(BF)


def return_kernel(info_ref, back_ref, got_ref, out_ref, buf_ref):
    full = dot(back_ref[...], got_ref[:, :, 0:256].reshape(512, 256))
    y_me = info_ref[10]
    total = got_ref[y_me, :, 256:384].astype(F32)
    for peer in range(1, 8):
        total = total + got_ref[4 * peer + y_me, :, 256:384].astype(F32)
    buf_ref[...] = jnp.zeros((16, 16, 256), F32)
    for part in range(4):
        for h in range(2):
            at = 4 * part + 2 * h
            buf_ref[0, 4 + 2 * part : 6 + 2 * part, 128 * h : 128 * h + 128] = total[at : at + 2, :]
    for z in range(16):
        if z:
            buf_ref[z, 4:12, :] = buf_ref[0, 4:12, :]
        buf_ref[z, 0:4, :] = full[4 * z : 4 * z + 4, :]
    out_ref[...] = buf_ref[...].astype(BF)


def last_kernel(cheb_ref, got_ref, own_ref, bare_ref, trans_ref, trial_ref, own_x_ref, out_ref):
    total = got_ref[0].astype(F32)
    for z in range(1, 16):
        total = total + got_ref[z].astype(F32)
    dens = [total[4 + 2 * part : 6 + 2 * part, :] for part in range(4)]
    terms = bare_of(own_ref, bare_ref, dens)
    for s in range(2):
        x = own_x_ref[2 * s : 2 * s + 2, :]
        t = trial_ref[:, s, :]
        applied = (
            trans_ref[s : s + 1, :] * x.astype(BF).astype(F32)
            + 2.0 * terms[s]
            + total[2 * s : 2 * s + 2, :]
        )
        second = 2.0 * applied - t
        out_ref[:, s, :] = cheb_ref[0] * t + cheb_ref[1] * x + cheb_ref[2] * second


def body(orbitals, transition, trial, screened, bare, cheb, pair_k, pair_slot, k_order):
    k_total = k_order.shape[0]
    position = lax.axis_index(PB)
    momentum = position * 2 + pair_slot
    partner = jnp.mod(pair_k - momentum, k_total)
    ends = jnp.stack([pair_k, partner], axis=1).reshape(-1)
    rows = jnp.arange(k_total, dtype=jnp.int32)
    dest = jnp.sum(jnp.where(ends[:, None] == k_order[None, :], rows[None, :], 0), axis=1)
    own_rows = position * 2 + jnp.arange(2, dtype=jnp.int32)
    where = jnp.stack([lax.axis_index("z"), lax.axis_index(PLANE), lax.axis_index("y")])
    info = jnp.concatenate([dest, own_rows, where, pair_slot, jnp.zeros((2,), jnp.int32)])

    plane = to_everyone(info[0:8], PLANE).reshape(64)
    own = to_everyone(orbitals, "y")
    (packed,) = call(pack_kernel, [((80, 256), BF)], (0,), [pltpu.VMEM((16, 256), F32)])(
        info, orbitals, trial, own
    )
    gat = lax.all_gather(packed, "z")
    (chosen,) = call(select_kernel, [((8, 224, 256), BF)], (0,), [pltpu.VMEM((256, 256), F32)])(
        plane, gat
    )
    got = exchange(chosen, PLANE)
    val, cond, dens = call(
        accept_kernel,
        [((112, 256), BF), ((6, 16, 256), BF), ((8, 256), F32)],
        (0,),
        [pltpu.VMEM((16, 256), F32)],
    )(info, got)
    wide = to_everyone(val, "y")
    base, route, back = call(
        base_kernel,
        [((4, 256), F32), ((128, 256), BF), ((64, 512), BF)],
        (0, 1),
        [pltpu.VMEM((4, 256), F32), pltpu.VMEM((128, 256), F32)],
    )(info, plane, dens, gat, own, bare, transition, trial)
    work = [
        pltpu.VMEM((6, 8, 256), F32),
        pltpu.VMEM((6, 8, 256), F32),
        pltpu.VMEM((2, 128, 256), F32),
        pltpu.VMEM((2, 128, 256), F32),
        pltpu.VMEM((4, 16, 256), F32),
    ]
    half, res = call(
        first_kernel, [((3, 256, 256), F32), ((4, 16, 256), BF)], (0,), work
    )(info, wide, cond, screened, base)
    parts = exchange(res, "y")
    column = jnp.sum(parts.astype(F32), axis=0).astype(BF)
    columns = to_everyone(column, "z")
    (middle,) = call(middle_kernel, [((32, 16, 256), BF)], ())(route, columns)
    arrived = exchange(middle, BLOCK)
    out2, own_x = call(
        second_kernel,
        [((32, 16, 384), BF), ((4, 256), F32)],
        (0,),
        work + [pltpu.VMEM((16, 128), F32)],
    )(info, arrived, half, cond, own)
    returned = exchange(out2, BLOCK)
    (final,) = call(
        return_kernel, [((16, 16, 256), BF)], (0,), [pltpu.VMEM((16, 16, 256), F32)]
    )(info, back, returned)
    last = exchange(final, "z")
    (result,) = call(last_kernel, [(trial.shape, F32)], (0,))(
        cheb, last, own, bare, transition, trial, own_x
    )
    return result


def solution(mesh):
    split = Mesh(mesh.devices.reshape(16, 4, 2, mesh.shape["vert"]), ("z", "x", "c", "y"))
    in_specs = (
        P(PB, None, "y"),
        P(PB, None),
        P("y", PB, None),
        P(PB, None, "y"),
        P(),
        P(),
        P(PB),
        P(PB),
        P(),
    )
    out_specs = P("y", PB, None)
    return jax.shard_map(body, mesh=split, in_specs=in_specs, out_specs=out_specs, check_vma=False)
```

time: 452 us -> 199 us (0.44)
  the two profiles are of different devices: /device:TPU:4 before, /device:TPU:32 now
where the time goes in v1:
time: 199 us; the launch traced here: 198 us
  blocking collectives  145 us (73%)
  Pallas kernels  28.6 us (14%)
  starting transfers between devices  7.85 us (4%)
  local copies, waits for them, and re-layouts  6.89 us (3%)
  waiting for transfers between devices  5.86 us (3%)
  other arithmetic  2.96 us (1%)
    all_to_all x7, blocking collectives, exchange(): return lax.all_to_all(blocks, axis, 0, 0, tiled=True)  106 us
    all_gather x1, blocking collectives, body(): gat = lax.all_gather(packed, 'z')  39.6 us
    pallas_call x9, Pallas kernels, run(): pl.pallas_call(kernel, out_shape=[jax.ShapeDtypeStruct(s, d) for s, d in...  28.6 us
    all_to_all x2, starting transfers between devices, exchange(): return lax.all_to_all(blocks, axis, 0, 0, tiled=True)  7.85 us
    all_to_all x2, waiting for transfers between devices, exchange(): return lax.all_to_all(blocks, axis, 0, 0, tiled=True)  5.86 us
  transfers between devices with their start and end apart: 2, of which 2 were waited for; matrix products, arithmetic and copies ran while one was open for 2% of the time, Pallas kernels for 2%

profile of v1, /device:TPU:32, one launch (start us, length us, event | category | flops | bytes accessed | tf_op | source)
XLA Modules:
  0.0 197.6 jit_solution(13315110892528551257)
XLA Ops:
  0.0 0.7 fusion
  0.7 0.7 pad_add_fusion
  1.4 0.1 copy.13
  1.4 0.1 eq.17
  1.5 0.9 select_reduce_fusion
  2.4 0.1 pad_add_fusion.1
  2.5 9.4 %all_to_all.46 = s32[8,1,8]{2,1,0:T(1,128)S(1)} all-to-all(s32[8,1,8]{2,1,0:T(1,128)S(1)} %broadcast_in_dim.22), channel_id=1, replica_groups=mesh['z'=16,'x'=4,'c'=2,'y'=4] {'x','c'}, dimensions={0} | all-to-all | bytes 512 | tf_op jit(solution)/shard_map/all_to_all | solution.py:21
  11.9 1.4 broadcast_in_dim.23
  13.3 4.5 %all-to-all-start.1 = ((bf16[4,2,32,256]{3,2,1,0:T(8,128)(2,1)}), bf16[4,2,32,256]{3,2,1,0:T(8,128)(2,1)S(1)}, u32[]{:S(2)}, u32[]{:S(2)}) async-start(bf16[4,2,32,256]{3,2,1,0:T(8,128)(2,1)} %broadcast_in_dim.23), calls=%async_computation.1 | async-start | bytes 262144 | tf_op jit(solution)/shard_map/all_to_all | solution.py:21
  17.7 1.2 concatenate.6.info_ref
  19.0 0.5 broadcast.22
  19.5 0.7 reduce.4
  20.1 0.7 reshape.15.plane_ref
  20.8 2.9 %all-to-all-done.1.own_ref = bf16[4,2,32,256]{3,2,1,0:T(8,128)(2,1)S(1)} async-done(((bf16[4,2,32,256]{3,2,1,0:T(8,128)(2,1)}), bf16[4,2,32,256]{3,2,1,0:T(8,128)(2,1)S(1)}, u32[]{:S(2)}, u32[]{:S(2)}) %all-to-all-start.1) | async-done | bytes 131104 | tf_op jit(solution)/shard_map/all_to_all | solution.py:21
  23.7 0.0 copy-start
  23.7 0.7 copy-done
  24.4 1.8 shard_map.91
  26.2 39.6 %all-gather = bf16[1280,256]{1,0:T(8,128)(2,1)} all-gather(bf16[80,256]{1,0:T(8,128)(2,1)} %shard_map.91), channel_id=2, replica_groups=mesh['z'=16,'x'=4,'c'=2,'y'=4] {'z'}, dimensions={0}, use_global_device_ids=true | all-gather | bytes 696320 | tf_op jit(solution)/shard_map/all_gather | solution.py:363
  65.8 3.3 %shard_map.92 = bf16[8,224,256]{2,1,0:T(8,128)(2,1)} custom-call(s32[64]{0:T(128)} %reshape.15.plane_ref, bf16[16,80,256]{2,1,0:T(8,128)(2,1)} %bitcast.7), custom_call_target="tpu_custom_call" | custom-call | tf_op jit(solution)/shard_map/pallas_call | solution.py:43
  69.1 18.8 %all_to_all.47.got_ref = bf16[8,224,256]{2,1,0:T(8,128)(2,1)} all-to-all(bf16[8,224,256]{2,1,0:T(8,128)(2,1)} %shard_map.92), channel_id=1, replica_groups=mesh['z'=16,'x'=4,'c'=2,'y'=4] {'x','c'}, dimensions={0} | all-to-all | bytes 1835008 | tf_op jit(solution)/shard_map/all_to_all | solution.py:21
  87.8 1.9 shard_map.93
  89.7 1.5 broadcast_in_dim.24
  91.2 3.4 %all-to-all-start.3 = ((bf16[4,112,256]{2,1,0:T(8,128)(2,1)}), bf16[4,112,256]{2,1,0:T(8,128)(2,1)S(1)}, u32[]{:S(2)}, u32[]{:S(2)}) async-start(bf16[4,112,256]{2,1,0:T(8,128)(2,1)} %broadcast_in_dim.24), calls=%async_computation.3 | async-start | bytes 458752 | tf_op jit(solution)/shard_map/all_to_all | solution.py:21
  94.6 3.5 %shard_map.94 = (f32[4,256]{1,0:T(4,128)}, bf16[128,256]{1,0:T(8,128)(2,1)}, bf16[64,512]{1,0:T(8,128)(2,1)}) custom-call(s32[16]{0:T(128)} %concatenate.6.info_ref, s32[64]{0:T(128)} %reshape.15.plane_ref, f32[8,256]{1,0:T(8,128)} %get-tuple-element.15.dens_ref, bf16[16,80,256]{2,1,0:T(8,128)(2,1)} %bitcast.8, bf16[4,2,32,256]{3,2,1,0:T(8,128)(2,1)} %copy-done, ...), custom_call_target="tpu_custom_call" | custom-call | tf_op jit(solution)/shard_map/pallas_call | solution.py:43
  98.1 3.0 %all-to-all-done.3.wide_ref = bf16[4,112,256]{2,1,0:T(8,128)(2,1)S(1)} async-done(((bf16[4,112,256]{2,1,0:T(8,128)(2,1)}), bf16[4,112,256]{2,1,0:T(8,128)(2,1)S(1)}, u32[]{:S(2)}, u32[]{:S(2)}) %all-to-all-start.3) | async-done | bytes 229408 | tf_op jit(solution)/shard_map/all_to_all | solution.py:21
  101.1 0.0 copy-start.1
  101.1 0.7 copy-done.1
  101.8 5.8 %shard_map.95 = (f32[3,256,256]{2,1,0:T(8,128)}, bf16[4,16,256]{2,1,0:T(8,128)(2,1)}) custom-call(s32[16]{0:T(128)} %concatenate.6.info_ref, bf16[4,112,256]{2,1,0:T(8,128)(2,1)} %copy-done.1, bf16[6,16,256]{2,1,0:T(8,128)(2,1)} %get-tuple-element.19.cond_ref, bf16[2,1024,256]{2,1,0:T(8,128)(2,1)} %scr_ref.1, f32[4,256]{1,0:T(4,128)} %get-tuple-element.20.base_ref), custom_call_target="tpu_custom_call" | custom-call | tf_op jit(solution)/shard_map/pallas_call | solution.py:43
  107.6 8.7 %all_to_all.48 = bf16[4,16,256]{2,1,0:T(8,128)(2,1)S(1)} all-to-all(bf16[4,16,256]{2,1,0:T(8,128)(2,1)} %get-tuple-element.21), channel_id=1, replica_groups=mesh['z'=16,'x'=4,'c'=2,'y'=4] {'y'}, dimensions={0} | all-to-all | bytes 65536 | tf_op jit(solution)/shard_map/all_to_all | solution.py:21
  116.3 21.6 %all_to_all.49.col_ref = bf16[16,16,256]{2,1,0:T(8,128)(2,1)} all-to-all(bf16[16,16,256]{2,1,0:T(8,128)(2,1)S(1)} %broadcast_in_dim.25), channel_id=1, replica_groups=mesh['z'=16,'x'=4,'c'=2,'y'=4] {'z'}, dimensions={0} | all-to-all | bytes 262144 | tf_op jit(solution)/shard_map/all_to_all | solution.py:21
  137.9 1.8 shard_map.96
  139.7 13.7 %all_to_all.50.got_ref = bf16[32,16,256]{2,1,0:T(8,128)(2,1)} all-to-all(bf16[32,16,256]{2,1,0:T(8,128)(2,1)} %shard_map.96), channel_id=1, replica_groups=mesh['z'=16,'x'=4,'c'=2,'y'=4] {'x','c','y'}, dimensions={0} | all-to-all | bytes 524288 | tf_op jit(solution)/shard_map/all_to_all | solution.py:21
  153.4 5.3 %shard_map.97 = (bf16[32,16,384]{2,1,0:T(8,128)(2,1)}, f32[4,256]{1,0:T(4,128)}) custom-call(s32[16]{0:T(128)} %concatenate.6.info_ref, bf16[32,16,256]{2,1,0:T(8,128)(2,1)} %all_to_all.50.got_ref, f32[3,256,256]{2,1,0:T(8,128)} %get-tuple-element.22.half_ref, bf16[6,16,256]{2,1,0:T(8,128)(2,1)} %get-tuple-element.19.cond_ref, bf16[4,2,32,256]{3,2,1,0:T(8,128)(2,1)} %copy-done), custom_call_target="tpu_custom_call" | custom-call | tf_op jit(solution)/shard_map/pallas_call | solution.py:43
  158.7 15.1 %all_to_all.51.got_ref = bf16[32,16,384]{2,1,0:T(8,128)(2,1)} all-to-all(bf16[32,16,384]{2,1,0:T(8,128)(2,1)} %get-tuple-element.23), channel_id=1, replica_groups=mesh['z'=16,'x'=4,'c'=2,'y'=4] {'x','c','y'}, dimensions={0} | all-to-all | bytes 786432 | tf_op jit(solution)/shard_map/all_to_all | solution.py:21
  173.8 1.9 shard_map.98
  175.7 18.7 %all_to_all.52.got_ref = bf16[16,16,256]{2,1,0:T(8,128)(2,1)} all-to-all(bf16[16,16,256]{2,1,0:T(8,128)(2,1)} %shard_map.98), channel_id=1, replica_groups=mesh['z'=16,'x'=4,'c'=2,'y'=4] {'z'}, dimensions={0} | all-to-all | bytes 262144 | tf_op jit(solution)/shard_map/all_to_all | solution.py:21
  194.3 3.3 %shard_map.99 = f32[2,2,256]{2,1,0:T(2,128)} custom-call(f32[3]{0:T(128)} %cheb_ref.1, bf16[16,16,256]{2,1,0:T(8,128)(2,1)} %all_to_all.52.got_ref, bf16[4,2,32,256]{3,2,1,0:T(8,128)(2,1)} %copy-done, bf16[1024,1024]{1,0:T(8,128)(2,1)} %bare_ref.3, f32[2,256]{1,0:T(2,128)} %trans_ref.3, f32[2,2,256]{2,1,0:T(2,128)} %trial_ref.5, ...), custom_call_target="tpu_custom_call" | custom-call | tf_op jit(solution)/shard_map/pallas_call | solution.py:43
  (5 shorter events, 0.0 us)
Async XLA Ops:
  13.3 10.4 %all-to-all-start.1 = ((bf16[4,2,32,256]{3,2,1,0:T(8,128)(2,1)}), bf16[4,2,32,256]{3,2,1,0:T(8,128)(2,1)S(1)}, u32[]{:S(2)}, u32[]{:S(2)}) async-start(bf16[4,2,32,256]{3,2,1,0:T(8,128)(2,1)} %broadcast_in_dim.23), calls=%async_computation.1 | async-start | bytes 262144 | tf_op jit(solution)/shard_map/all_to_all | solution.py:21
  23.7 0.7 copy-start
  91.2 9.9 %all-to-all-start.3 = ((bf16[4,112,256]{2,1,0:T(8,128)(2,1)}), bf16[4,112,256]{2,1,0:T(8,128)(2,1)S(1)}, u32[]{:S(2)}, u32[]{:S(2)}) async-start(bf16[4,112,256]{2,1,0:T(8,128)(2,1)} %broadcast_in_dim.24), calls=%async_computation.3 | async-start | bytes 458752 | tf_op jit(solution)/shard_map/all_to_all | solution.py:21
  101.1 0.7 copy-start.1

commit v2 on v1

--- a/solution.py
+++ b/solution.py
@@ -15,15 +15,11 @@
 PB = ("z", "x", "c")
 PLANE = ("x", "c")
 BLOCK = ("x", "c", "y")
+LIMIT = 12 << 20
 
 
 def exchange(blocks, axis):
     return lax.all_to_all(blocks, axis, 0, 0, tiled=True)
-
-
-def to_everyone(shard, axis):
-    count = lax.axis_size(axis)
-    return exchange(jnp.broadcast_to(shard[None], (count, *shard.shape)), axis)
 
 
 def dot(a, b):
@@ -44,8 +40,13 @@
             kernel,
             out_shape=[jax.ShapeDtypeStruct(s, d) for s, d in outs],
             in_specs=specs,
-            out_specs=[pl.BlockSpec(memory_space=pltpu.VMEM) for _ in outs],
+            out_specs=[
+                pl.BlockSpec(memory_space=pltpu.SMEM if len(s) == 1 else pltpu.VMEM)
+                for s, _ in outs
+            ],
             scratch_shapes=list(scratch),
+            name=kernel.__name__,
+            compiler_params=pltpu.CompilerParams(vmem_limit_bytes=LIMIT),
         )(*args)
 
     return run
@@ -90,6 +91,34 @@
     return terms
 
 
+def info_kernel(pair_ref, slot_ref, order_ref, orb_ref, info_ref, ids_ref, own_ref):
+    position = lax.axis_index(PB)
+    lane = lanes(1, 256)
+    short = lanes(1, 128)
+    order = order_ref[...]
+    ids = jnp.where(short == 6, position * 2, jnp.where(short == 7, position * 2 + 1, 0))
+    for i in range(3):
+        first = pair_ref[i]
+        second = first - position * 2 - slot_ref[i]
+        second = jnp.where(second < 0, second + 256, second)
+        for h, k in enumerate((first, second)):
+            row = jnp.sum(jnp.where(order == k, lane, 0))
+            info_ref[2 * i + h] = row
+            ids = jnp.where(short == 2 * i + h, row, ids)
+        info_ref[11 + i] = slot_ref[i]
+    info_ref[6] = position * 2
+    info_ref[7] = position * 2 + 1
+    info_ref[8] = lax.axis_index("z")
+    info_ref[9] = lax.axis_index(PLANE)
+    info_ref[10] = lax.axis_index("y")
+    info_ref[14] = 0
+    info_ref[15] = 0
+    for peer in range(8):
+        ids_ref[peer] = ids
+    for part in range(4):
+        own_ref[part] = orb_ref[...]
+
+
 def pack_kernel(info_ref, orb_ref, trial_ref, own_ref, out_ref, tail_ref):
     out_ref[0:64, :] = orb_ref[...].reshape(64, 256)
     rows = [trial_ref[:, s, :].astype(BF) for s in range(2)]
@@ -112,20 +141,14 @@
     pick_ref[...] = jnp.zeros((256, 256), F32)
     for peer in range(8):
         for e in range(6):
-            row = plane_ref[peer * 8 + e]
+            row = plane_ref[peer, 0, e]
             z = row // 16
             s = lax.rem(row, 2)
             for n in range(2):
                 at = peer * 32 + 2 * e + n
                 pick_ref[at : at + 1, :] = (lane == z * 16 + 2 * s + n).astype(F32)
-
-            @pl.when(s == 0)
-            def _():
-                out_ref[peer, 32 * e : 32 * e + 32, :] = gat_ref[z, 0:32, :]
-
-            @pl.when(s == 1)
-            def _():
-                out_ref[peer, 32 * e : 32 * e + 32, :] = gat_ref[z, 32:64, :]
+            at = pl.multiple_of(s * 32, 32)
+            out_ref[peer, 32 * e : 32 * e + 32, :] = gat_ref[z, pl.ds(at, 32), :]
 
         for d in range(8):
             at = peer * 32 + 16 + d
@@ -138,12 +161,15 @@
 def accept_kernel(info_ref, got_ref, val_ref, cond_ref, dens_ref, tail_ref):
     for e in range(6):
         column = lax.rem(info_ref[e] // 2, 8)
-        val_ref[16 * e : 16 * e + 16, :] = got_ref[column, 32 * e : 32 * e + 16, :]
+        val = got_ref[column, 32 * e : 32 * e + 16, :]
+        for part in range(4):
+            val_ref[part, 16 * e : 16 * e + 16, :] = val
         cond_ref[e] = got_ref[column, 32 * e + 16 : 32 * e + 32, :]
         part = got_ref[column, 192:208, :].astype(F32)
         tail_ref[2 * e : 2 * e + 2, :] = part[2 * e : 2 * e + 2, :]
     tail_ref[12:16, :] = jnp.zeros((4, 256), F32)
-    val_ref[96:112, :] = tail_ref[...].astype(BF)
+    for part in range(4):
+        val_ref[part, 96:112, :] = tail_ref[...].astype(BF)
     total = got_ref[0, 208:224, :].astype(F32)
     for peer in range(1, 8):
         total = total + got_ref[peer, 208:224, :].astype(F32)
@@ -173,7 +199,7 @@
     q_me = info_ref[9]
     for peer in range(8):
         for k in range(8):
-            row = plane_ref[peer * 8 + k] if k < 6 else z_me * 16 + peer * 2 + (k - 6)
+            row = plane_ref[peer, 0, k] if k < 6 else z_me * 16 + peer * 2 + (k - 6)
             for n in range(2):
                 at = peer * 16 + 2 * k + n
                 hit = (held == row) & (parity == n)
@@ -185,7 +211,7 @@
     for peer in range(8):
         for e in range(6):
             here = (wide // 64 == peer) & (lax.rem(wide, 16) // 2 == e)
-            sent = jnp.where(here, plane_ref[peer * 8 + e], sent)
+            sent = jnp.where(here, plane_ref[peer, 0, e], sent)
     row = lax.broadcasted_iota(jnp.int32, (64, 512), 0)
     target = (row // 4) * 16 + q_me * 2 + lax.rem(row, 4) // 2
     hit = (sent == target) & (lax.rem(row, 2) == lax.rem(lanes(64, 512), 2))
@@ -212,20 +238,25 @@
     tile_c = jnp.concatenate([cond_ref[2 * i + 1]] * 16, axis=0)
     t_ref[0] = dot(spread(xs_ref[2 * i]), tile_a)
     t_ref[1] = dot(spread(xs_ref[2 * i + 1]), tile_c)
-    u_ref[1] = jnp.zeros((128, 256), F32)
-
-    def over_first(v, carry):
-        at = pl.multiple_of(v * 8, 8)
-        t_a = t_ref[0, pl.ds(at, 8), :]
-        total = jnp.zeros((8, 256), F32)
+    for part in range(2):
+        at = slice(128 * part, 128 * part + 128)
+        t_c = [t_ref[1, 8 * w : 8 * w + 8, at] for w in range(16)]
+
+        def over_first(v, u_c):
+            row = pl.multiple_of(v * 8, 8)
+            t_a = t_ref[0, pl.ds(row, 8), at]
+            sums = [jnp.zeros((8, 128), F32)] * 2
+            new = []
+            for w in range(16):
+                h = jnp.broadcast_to(half_ref[2 * i + part, pl.ds(v * 16 + w, 1), :], (8, 128))
+                sums[w % 2] = sums[w % 2] + h * t_c[w]
+                new.append(u_c[w] + h * t_a)
+            u_ref[0, pl.ds(row, 8), at] = sums[0] + sums[1]
+            return tuple(new)
+
+        u_c = lax.fori_loop(0, 16, over_first, (jnp.zeros((8, 128), F32),) * 16)
         for w in range(16):
-            h = jnp.broadcast_to(half_ref[i, pl.ds(v * 16 + w, 1), :], (8, 256))
-            total = total + h * t_ref[1, 8 * w : 8 * w + 8, :]
-            u_ref[1, 8 * w : 8 * w + 8, :] += h * t_a
-        u_ref[0, pl.ds(at, 8), :] = total
-        return carry
-
-    lax.fori_loop(0, 16, over_first, 0)
+            u_ref[1, 8 * w : 8 * w + 8, at] = u_c[w]
     ys_ref[2 * i] = gathered(dot_t(u_ref[0].astype(BF), tile_a))
     ys_ref[2 * i + 1] = gathered(dot_t(u_ref[1].astype(BF), tile_c))
 
@@ -250,7 +281,9 @@
                 [(a[v : v + 1, :] * b).astype(BF) for v in range(16)], axis=0
             )
             total = total + dot(left, scr_ref[slot, part * 256 : (part + 1) * 256, :])
-        half_ref[i] = total.astype(BF).astype(F32)
+        total = total.astype(BF).astype(F32)
+        half_ref[2 * i] = total[:, 0:128]
+        half_ref[2 * i + 1] = total[:, 128:256]
         apply_pair(i, half_ref, cond_ref, xs_ref, ys_ref, t_ref, u_ref)
         return carry
 
@@ -261,6 +294,14 @@
         mine = (info_ref[10] == part).astype(F32)
         rs_ref[part, 12:16, :] = base_ref[...] * mine
     res_ref[...] = rs_ref[...].astype(BF)
+
+
+def column_kernel(got_ref, out_ref):
+    total = got_ref[0].astype(F32)
+    for part in range(1, 4):
+        total = total + got_ref[part].astype(F32)
+    for z in range(16):
+        out_ref[z] = total.astype(BF)
 
 
 def middle_kernel(route_ref, col_ref, out_ref):
@@ -344,19 +385,13 @@
 
 
 def body(orbitals, transition, trial, screened, bare, cheb, pair_k, pair_slot, k_order):
-    k_total = k_order.shape[0]
-    position = lax.axis_index(PB)
-    momentum = position * 2 + pair_slot
-    partner = jnp.mod(pair_k - momentum, k_total)
-    ends = jnp.stack([pair_k, partner], axis=1).reshape(-1)
-    rows = jnp.arange(k_total, dtype=jnp.int32)
-    dest = jnp.sum(jnp.where(ends[:, None] == k_order[None, :], rows[None, :], 0), axis=1)
-    own_rows = position * 2 + jnp.arange(2, dtype=jnp.int32)
-    where = jnp.stack([lax.axis_index("z"), lax.axis_index(PLANE), lax.axis_index("y")])
-    info = jnp.concatenate([dest, own_rows, where, pair_slot, jnp.zeros((2,), jnp.int32)])
-
-    plane = to_everyone(info[0:8], PLANE).reshape(64)
-    own = to_everyone(orbitals, "y")
+    info, ids, copies = call(
+        info_kernel,
+        [((16,), jnp.int32), ((8, 1, 128), jnp.int32), ((4, 2, 32, 256), BF)],
+        (0, 1),
+    )(pair_k, pair_slot, k_order.reshape(1, -1), orbitals)
+    own = exchange(copies, "y")
+    plane = exchange(ids, PLANE)
     (packed,) = call(pack_kernel, [((80, 256), BF)], (0,), [pltpu.VMEM((16, 256), F32)])(
         info, orbitals, trial, own
     )
@@ -367,11 +402,11 @@
     got = exchange(chosen, PLANE)
     val, cond, dens = call(
         accept_kernel,
-        [((112, 256), BF), ((6, 16, 256), BF), ((8, 256), F32)],
+        [((4, 112, 256), BF), ((6, 16, 256), BF), ((8, 256), F32)],
         (0,),
         [pltpu.VMEM((16, 256), F32)],
     )(info, got)
-    wide = to_everyone(val, "y")
+    wide = exchange(val, "y")
     base, route, back = call(
         base_kernel,
         [((4, 256), F32), ((128, 256), BF), ((64, 512), BF)],
@@ -386,11 +421,11 @@
         pltpu.VMEM((4, 16, 256), F32),
     ]
     half, res = call(
-        first_kernel, [((3, 256, 256), F32), ((4, 16, 256), BF)], (0,), work
+        first_kernel, [((6, 256, 128), F32), ((4, 16, 256), BF)], (0,), work
     )(info, wide, cond, screened, base)
     parts = exchange(res, "y")
-    column = jnp.sum(parts.astype(F32), axis=0).astype(BF)
-    columns = to_everyone(column, "z")
+    (column,) = call(column_kernel, [((16, 16, 256), BF)], ())(parts)
+    columns = exchange(column, "z")
     (middle,) = call(middle_kernel, [((32, 16, 256), BF)], ())(route, columns)
     arrived = exchange(middle, BLOCK)
     out2, own_x = call(

time: 199 us -> 177 us (0.89)
  Pallas kernels: 28.6 us -> 16.9 us
  blocking collectives: 145 us -> 141 us
  other arithmetic: 2.96 us -> 0 us
    pallas_call x9 -> x11, Pallas kernels: 28.6 us -> 16.9 us  [run(): pl.pallas_call(kernel, out_shape=[jax.ShapeDtypeStruct(s, d) for s, d in...]
    unnamed x4 -> x22, local copies, waits for them, and re-layouts: 1.36 us -> 5.43 us
    broadcast_in_dim x4 -> x0, local copies, waits for them, and re-layouts: 2.93 us -> none  [to_everyone(): return exchange(jnp.broadcast_to(shard[None], (count, *shard.shape)), axis)]
    all_gather x1, blocking collectives: 39.6 us -> 36.9 us  [body(): gat = lax.all_gather(packed, 'z')]
  transfers between devices with their start and end apart: 2 -> 2, of which waited for: 2 -> 1; matrix products, arithmetic and copies ran while one was open for 2% -> 0% of each run, Pallas kernels for 2% -> 1%
where the time goes in v2:
time: 177 us; the launch traced here: 176 us
  blocking collectives  141 us (80%)
  Pallas kernels  16.9 us (10%)
  starting transfers between devices  7.69 us (4%)
  local copies, waits for them, and re-layouts  5.43 us (3%)
  waiting for transfers between devices  4.77 us (3%)
    all_to_all x7, blocking collectives, exchange(): return lax.all_to_all(blocks, axis, 0, 0, tiled=True)  104 us
    all_gather x1, blocking collectives, body(): gat = lax.all_gather(packed, 'z')  36.9 us
    pallas_call x11, Pallas kernels, run(): pl.pallas_call(kernel, out_shape=[jax.ShapeDtypeStruct(s, d) for s, d in...  16.9 us
    all_to_all x2, starting transfers between devices, exchange(): return lax.all_to_all(blocks, axis, 0, 0, tiled=True)  7.69 us
    unnamed x22, local copies, waits for them, and re-layouts  5.43 us
    all_to_all x2, waiting for transfers between devices, exchange(): return lax.all_to_all(blocks, axis, 0, 0, tiled=True)  4.77 us
  transfers between devices with their start and end apart: 2, of which 1 were waited for; matrix products, arithmetic and copies ran while one was open for 0% of the time, Pallas kernels for 1%

profile of v2, /device:TPU:32, one launch (start us, length us, event | category | flops | bytes accessed | tf_op | source)
XLA Modules:
  0.0 175.9 jit_solution(9525676678096911746)
XLA Ops:
  0.0 0.0 copy-start.2
  0.0 0.8 copy-done.2
  0.8 0.0 copy-start.7
  0.8 0.7 copy-done.7
  1.4 0.0 copy-start.8
  1.4 0.7 copy-done.8
  2.1 0.0 copy-start.9
  2.1 0.7 copy-done.9
  2.8 1.3 info_kernel.1
  4.1 10.2 %all_to_all.45.own_ref = bf16[4,2,32,256]{3,2,1,0:T(8,128)(2,1)S(1)} all-to-all(bf16[4,2,32,256]{3,2,1,0:T(8,128)(2,1)S(1)} %get-tuple-element.20), channel_id=1, replica_groups=mesh['z'=16,'x'=4,'c'=2,'y'=4] {'y'}, dimensions={0} | all-to-all | bytes 262144 | tf_op jit(solution)/shard_map/all_to_all | solution.py:22
  14.3 4.3 %all-to-all-start = ((s32[8,1,128]{2,1,0:T(1,128)}), s32[8,1,128]{2,1,0:T(1,128)S(1)}, u32[]{:S(2)}, u32[]{:S(2)}) async-start(s32[8,1,128]{2,1,0:T(1,128)} %get-tuple-element.19), calls=%async_computation | async-start | bytes 8192 | tf_op jit(solution)/shard_map/all_to_all | solution.py:22
  18.6 0.0 copy-start.3
  18.6 0.8 copy-done.3
  19.4 0.0 copy-start.4
  19.4 0.7 copy-done.4
  20.0 0.8 pack_kernel.1
  20.9 36.9 %all-gather = bf16[1280,256]{1,0:T(8,128)(2,1)S(1)} all-gather(bf16[80,256]{1,0:T(8,128)(2,1)S(1)} %pack_kernel.1), channel_id=2, replica_groups=mesh['z'=16,'x'=4,'c'=2,'y'=4] {'z'}, dimensions={0}, use_global_device_ids=true | all-gather | bytes 696320 | tf_op jit(solution)/shard_map/all_gather | solution.py:398
  57.8 0.0 all-to-all-done.plane_ref
  57.8 0.0 copy-start
  57.8 0.0 copy-start.5
  57.8 0.0 copy-start.6
  57.8 1.1 select_kernel.1
  58.9 19.3 %all_to_all.46.got_ref = bf16[8,224,256]{2,1,0:T(8,128)(2,1)S(1)} all-to-all(bf16[8,224,256]{2,1,0:T(8,128)(2,1)S(1)} %select_kernel.1), channel_id=1, replica_groups=mesh['z'=16,'x'=4,'c'=2,'y'=4] {'x','c'}, dimensions={0} | all-to-all | bytes 1835008 | tf_op jit(solution)/shard_map/all_to_all | solution.py:22
  78.2 1.3 accept_kernel.1
  79.5 3.4 %all-to-all-start.3 = ((bf16[4,112,256]{2,1,0:T(8,128)(2,1)}), bf16[4,112,256]{2,1,0:T(8,128)(2,1)S(1)}, u32[]{:S(2)}, u32[]{:S(2)}) async-start(bf16[4,112,256]{2,1,0:T(8,128)(2,1)} %get-tuple-element.24), calls=%async_computation.3 | async-start | bytes 458752 | tf_op jit(solution)/shard_map/all_to_all | solution.py:22
  82.9 0.0 copy-done
  82.9 0.0 copy-done.5
  82.9 0.0 copy-done.6
  82.9 1.7 base_kernel.1
  84.6 4.8 %all-to-all-done.3.wide_ref = bf16[4,112,256]{2,1,0:T(8,128)(2,1)S(1)} async-done(((bf16[4,112,256]{2,1,0:T(8,128)(2,1)}), bf16[4,112,256]{2,1,0:T(8,128)(2,1)S(1)}, u32[]{:S(2)}, u32[]{:S(2)}) %all-to-all-start.3) | async-done | bytes 229408 | tf_op jit(solution)/shard_map/all_to_all | solution.py:22
  89.4 0.0 copy-start.1
  89.4 1.2 copy-done.1
  90.6 4.1 %first_kernel.1 = (f32[6,256,128]{2,1,0:T(8,128)S(1)}, bf16[4,16,256]{2,1,0:T(8,128)(2,1)S(1)}) custom-call(s32[16]{0:T(128)S(1)} %get-tuple-element.18.info_ref, bf16[4,112,256]{2,1,0:T(8,128)(2,1)S(1)} %all-to-all-done.3.wide_ref, bf16[6,16,256]{2,1,0:T(8,128)(2,1)S(1)} %get-tuple-element.25.cond_ref, bf16[2,1024,256]{2,1,0:T(8,128)(2,1)S(1)} %copy-done.1, ...), custom_call_target="tpu_custom_call" | custom-call | tf_op jit(solution)/shard_map/first_kernel/pallas_call | solution.py:39
  94.7 7.8 %all_to_all.47.got_ref = bf16[4,16,256]{2,1,0:T(8,128)(2,1)S(1)} all-to-all(bf16[4,16,256]{2,1,0:T(8,128)(2,1)S(1)} %get-tuple-element.27), channel_id=1, replica_groups=mesh['z'=16,'x'=4,'c'=2,'y'=4] {'y'}, dimensions={0} | all-to-all | bytes 65536 | tf_op jit(solution)/shard_map/all_to_all | solution.py:22
  102.5 0.0 copy-start.10
  102.6 21.8 %all_to_all.48.col_ref = bf16[16,16,256]{2,1,0:T(8,128)(2,1)S(1)} all-to-all(bf16[16,16,256]{2,1,0:T(8,128)(2,1)S(1)} %column_kernel.1), channel_id=1, replica_groups=mesh['z'=16,'x'=4,'c'=2,'y'=4] {'z'}, dimensions={0} | all-to-all | bytes 262144 | tf_op jit(solution)/shard_map/all_to_all | solution.py:22
  124.3 0.2 middle_kernel.1
  124.5 12.4 %all_to_all.49.got_ref = bf16[32,16,256]{2,1,0:T(8,128)(2,1)S(1)} all-to-all(bf16[32,16,256]{2,1,0:T(8,128)(2,1)S(1)} %middle_kernel.1), channel_id=1, replica_groups=mesh['z'=16,'x'=4,'c'=2,'y'=4] {'x','c','y'}, dimensions={0} | all-to-all | bytes 524288 | tf_op jit(solution)/shard_map/all_to_all | solution.py:22
  136.9 3.6 %second_kernel.1 = (bf16[32,16,384]{2,1,0:T(8,128)(2,1)S(1)}, f32[4,256]{1,0:T(4,128)S(1)}) custom-call(s32[16]{0:T(128)S(1)} %get-tuple-element.18.info_ref, bf16[32,16,256]{2,1,0:T(8,128)(2,1)S(1)} %all_to_all.49.got_ref, f32[6,256,128]{2,1,0:T(8,128)S(1)} %get-tuple-element.28.half_ref, bf16[6,16,256]{2,1,0:T(8,128)(2,1)S(1)} %get-tuple-element.25.cond_ref, ...), custom_call_target="tpu_custom_call" | custom-call | tf_op jit(solution)/shard_map/second_kernel/pallas_call | solution.py:39
  140.5 14.1 %all_to_all.50.got_ref = bf16[32,16,384]{2,1,0:T(8,128)(2,1)S(1)} all-to-all(bf16[32,16,384]{2,1,0:T(8,128)(2,1)S(1)} %get-tuple-element.29), channel_id=1, replica_groups=mesh['z'=16,'x'=4,'c'=2,'y'=4] {'x','c','y'}, dimensions={0} | all-to-all | bytes 786432 | tf_op jit(solution)/shard_map/all_to_all | solution.py:22
  154.6 0.7 return_kernel.1
  155.3 18.5 %all_to_all.51.got_ref = bf16[16,16,256]{2,1,0:T(8,128)(2,1)S(1)} all-to-all(bf16[16,16,256]{2,1,0:T(8,128)(2,1)S(1)} %return_kernel.1), channel_id=1, replica_groups=mesh['z'=16,'x'=4,'c'=2,'y'=4] {'z'}, dimensions={0} | all-to-all | bytes 262144 | tf_op jit(solution)/shard_map/all_to_all | solution.py:22
  173.8 0.0 copy-done.10
  173.8 2.1 %last_kernel.1 = f32[2,2,256]{2,1,0:T(2,128)} custom-call(f32[3]{0:T(128)S(1)} %copy-done.10, bf16[16,16,256]{2,1,0:T(8,128)(2,1)S(1)} %all_to_all.51.got_ref, bf16[4,2,32,256]{3,2,1,0:T(8,128)(2,1)S(1)} %all_to_all.45.own_ref, bf16[1024,1024]{1,0:T(8,128)(2,1)S(1)} %copy-done, f32[2,256]{1,0:T(2,128)S(1)} %copy-done.6, f32[2,2,256]{2,1,0:T(2,128)S(1)} %copy-done.5, ...), custom_call_target="tpu_custom_call" | custom-call | tf_op jit(solution)/shard_map/last_kernel/pallas_call | solution.py:39
  (1 shorter events, 0.0 us)
Async XLA Ops:
  0.0 0.8 copy-start.2
  0.8 0.7 copy-start.7
  1.4 0.7 copy-start.8
  2.1 0.7 copy-start.9
  14.3 43.5 %all-to-all-start = ((s32[8,1,128]{2,1,0:T(1,128)}), s32[8,1,128]{2,1,0:T(1,128)S(1)}, u32[]{:S(2)}, u32[]{:S(2)}) async-start(s32[8,1,128]{2,1,0:T(1,128)} %get-tuple-element.19), calls=%async_computation | async-start | bytes 8192 | tf_op jit(solution)/shard_map/all_to_all | solution.py:22
  18.6 0.8 copy-start.3
  19.4 0.7 copy-start.4
  57.8 25.1 %copy-start = (bf16[1024,1024]{1,0:T(8,128)(2,1)S(1)}, bf16[1024,1024]{1,0:T(8,128)(2,1)}, u32[]{:S(2)}) copy-start(bf16[1024,1024]{1,0:T(8,128)(2,1)} %bare_ref.3) | copy-start | bytes 6291460
  57.8 25.1 %copy-start.5 = (f32[2,2,256]{2,1,0:T(2,128)S(1)}, f32[2,2,256]{2,1,0:T(2,128)}, u32[]{:S(2)}) copy-start(f32[2,2,256]{2,1,0:T(2,128)} %trial_ref.5) | copy-start | bytes 12292
  57.8 25.1 %copy-start.6 = (f32[2,256]{1,0:T(2,128)S(1)}, f32[2,256]{1,0:T(2,128)}, u32[]{:S(2)}) copy-start(f32[2,256]{1,0:T(2,128)} %trans_ref.3) | copy-start | bytes 6148
  79.5 9.9 %all-to-all-start.3 = ((bf16[4,112,256]{2,1,0:T(8,128)(2,1)}), bf16[4,112,256]{2,1,0:T(8,128)(2,1)S(1)}, u32[]{:S(2)}, u32[]{:S(2)}) async-start(bf16[4,112,256]{2,1,0:T(8,128)(2,1)} %get-tuple-element.24), calls=%async_computation.3 | async-start | bytes 458752 | tf_op jit(solution)/shard_map/all_to_all | solution.py:22
  89.4 1.2 copy-start.1
  102.5 71.3 %copy-start.10 = (f32[3]{0:T(128)S(1)}, f32[3]{0:T(128)}, u32[]{:S(2)}) copy-start(f32[3]{0:T(128)} %cheb_ref.1) | copy-start | bytes 40

commit v3 on v2

--- a/solution.py
+++ b/solution.py
@@ -1,5 +1,3 @@
-import functools
-
 import jax
 import jax.numpy as jnp
 from jax import lax
@@ -8,13 +6,14 @@
 from jax.sharding import Mesh
 from jax.sharding import PartitionSpec as P
 
+
 BF = jnp.bfloat16
 F32 = jnp.float32
-NV = 16
 LAST = (((1,), (1,)), ((), ()))
 PB = ("z", "x", "c")
 PLANE = ("x", "c")
 BLOCK = ("x", "c", "y")
+SHEET = ("x", "y")
 LIMIT = 12 << 20
 
 
@@ -22,6 +21,10 @@
     return lax.all_to_all(blocks, axis, 0, 0, tiled=True)
 
 
+def swap(shard):
+    return lax.ppermute(shard, "c", [(0, 1), (1, 0)])
+
+
 def dot(a, b):
     return jnp.dot(a, b, preferred_element_type=F32)
 
@@ -30,12 +33,12 @@
     return lax.dot_general(a, b, LAST, preferred_element_type=F32)
 
 
-def call(kernel, outs, smem, scratch=()):
+def call(kernel, outs, smem, scratch=(), far=(), limit=LIMIT):
+    def space(k):
+        return pltpu.SMEM if k in smem else pltpu.HBM if k in far else pltpu.VMEM
+
     def run(*args):
-        specs = [
-            pl.BlockSpec(memory_space=pltpu.SMEM if k in smem else pltpu.VMEM)
-            for k in range(len(args))
-        ]
+        specs = [pl.BlockSpec(memory_space=space(k)) for k in range(len(args))]
         return pl.pallas_call(
             kernel,
             out_shape=[jax.ShapeDtypeStruct(s, d) for s, d in outs],
@@ -45,8 +48,8 @@
                 for s, _ in outs
             ],
             scratch_shapes=list(scratch),
-            name=kernel.__name__,
-            compiler_params=pltpu.CompilerParams(vmem_limit_bytes=LIMIT),
+            compiler_params=pltpu.CompilerParams(vmem_limit_bytes=limit),
+            cost_estimate=pl.CostEstimate(flops=0, transcendentals=0, bytes_accessed=4 << 20),
         )(*args)
 
     return run
@@ -91,7 +94,19 @@
     return terms
 
 
-def info_kernel(pair_ref, slot_ref, order_ref, orb_ref, info_ref, ids_ref, own_ref):
+def info_kernel(
+    pair_hbm, slot_hbm, order_hbm, orb_hbm, trial_hbm, trans_hbm,
+    info_ref, ids_ref, own_ref, held_ref, pair_ref, slot_ref, order_ref, trial_ref, trans_ref, sem,
+):
+    moves = [
+        (pair_hbm, pair_ref), (slot_hbm, slot_ref), (order_hbm, order_ref),
+        (trial_hbm, trial_ref), (trans_hbm, trans_ref),
+    ] + [(orb_hbm, own_ref.at[part]) for part in range(4)]
+    copies = [pltpu.make_async_copy(a, b, sem.at[k]) for k, (a, b) in enumerate(moves)]
+    for copy in copies:
+        copy.start()
+    for copy in copies[:3]:
+        copy.wait()
     position = lax.axis_index(PB)
     lane = lanes(1, 256)
     short = lanes(1, 128)
@@ -115,13 +130,17 @@
     info_ref[15] = 0
     for peer in range(8):
         ids_ref[peer] = ids
-    for part in range(4):
-        own_ref[part] = orb_ref[...]
-
-
-def pack_kernel(info_ref, orb_ref, trial_ref, own_ref, out_ref, tail_ref):
-    out_ref[0:64, :] = orb_ref[...].reshape(64, 256)
-    rows = [trial_ref[:, s, :].astype(BF) for s in range(2)]
+    for copy in copies[3:]:
+        copy.wait()
+    held_ref[...] = jnp.zeros((8, 256), F32)
+    for s in range(2):
+        held_ref[2 * s : 2 * s + 2, :] = trial_ref[:, s, :]
+    held_ref[4:6, :] = trans_ref[...]
+
+
+def pack_kernel(info_ref, held_ref, own_ref, out_ref, tail_ref):
+    out_ref[0:64, :] = own_ref[info_ref[10]].reshape(64, 256)
+    rows = [held_ref[2 * s : 2 * s + 2, :].astype(BF) for s in range(2)]
     parts = density_of(own_ref, rows)
     tail_ref[...] = jnp.zeros((16, 256), F32)
     for s in range(2):
@@ -136,31 +155,42 @@
     out_ref[64:80, :] = tail_ref[...].astype(BF)
 
 
-def select_kernel(plane_ref, gat_ref, out_ref, pick_ref):
-    lane = lanes(1, 256)
-    pick_ref[...] = jnp.zeros((256, 256), F32)
-    for peer in range(8):
+def select_kernel(info_ref, plane_ref, gat_ref, twin_ref, out_ref, pick_ref):
+    lane = lanes(1, 512)
+    core = lax.rem(info_ref[9], 2)
+    pick_ref[...] = jnp.zeros((128, 512), F32)
+    for peer in range(4):
         for e in range(6):
-            row = plane_ref[peer, 0, e]
+            row = plane_ref[2 * peer + core, 0, e]
             z = row // 16
             s = lax.rem(row, 2)
+            ours = lax.rem(row // 2, 2) == core
+            first = z * 16 + 2 * s + jnp.where(ours, 0, 256)
             for n in range(2):
                 at = peer * 32 + 2 * e + n
-                pick_ref[at : at + 1, :] = (lane == z * 16 + 2 * s + n).astype(F32)
+                pick_ref[at : at + 1, :] = (lane == first + n).astype(F32)
             at = pl.multiple_of(s * 32, 32)
-            out_ref[peer, 32 * e : 32 * e + 32, :] = gat_ref[z, pl.ds(at, 32), :]
+
+            @pl.when(ours)
+            def _():
+                out_ref[peer, 32 * e : 32 * e + 32, :] = gat_ref[z, pl.ds(at, 32), :]
+
+            @pl.when(jnp.logical_not(ours))
+            def _():
+                out_ref[peer, 32 * e : 32 * e + 32, :] = twin_ref[z, pl.ds(at, 32), :]
 
         for d in range(8):
             at = peer * 32 + 16 + d
             pick_ref[at : at + 1, :] = (lax.rem(lane, 16) == 4 + d).astype(F32)
-    tails = gat_ref[:, 64:80, :].reshape(256, 256)
-    picked = dot(pick_ref[...].astype(BF), tails).astype(BF)
-    out_ref[:, 192:224, :] = picked.reshape(8, 32, 256)
+    pick = pick_ref[...].astype(BF)
+    picked = dot(pick[:, 0:256], gat_ref[:, 64:80, :].reshape(256, 256))
+    picked = picked + dot(pick[:, 256:512], twin_ref[:, 64:80, :].reshape(256, 256))
+    out_ref[:, 192:224, :] = picked.astype(BF).reshape(4, 32, 256)
 
 
 def accept_kernel(info_ref, got_ref, val_ref, cond_ref, dens_ref, tail_ref):
     for e in range(6):
-        column = lax.rem(info_ref[e] // 2, 8)
+        column = lax.rem(info_ref[e] // 4, 4)
         val = got_ref[column, 32 * e : 32 * e + 16, :]
         for part in range(4):
             val_ref[part, 16 * e : 16 * e + 16, :] = val
@@ -171,20 +201,20 @@
     for part in range(4):
         val_ref[part, 96:112, :] = tail_ref[...].astype(BF)
     total = got_ref[0, 208:224, :].astype(F32)
-    for peer in range(1, 8):
+    for peer in range(1, 4):
         total = total + got_ref[peer, 208:224, :].astype(F32)
     dens_ref[...] = total[0:8, :]
 
 
 def base_kernel(
-    info_ref, plane_ref, dens_ref, gat_ref, own_ref, bare_ref, trans_ref, trial_ref,
+    info_ref, plane_ref, dens_ref, gat_ref, own_ref, bare_ref, held_ref,
     base_ref, route_ref, back_ref, base_s, route_s,
 ):
     dens = [dens_ref[2 * part : 2 * part + 2, :] for part in range(4)]
     terms = bare_of(own_ref, bare_ref, dens)
     for s in range(2):
-        x = trial_ref[:, s, :].astype(BF).astype(F32)
-        base_s[2 * s : 2 * s + 2, :] = trans_ref[s : s + 1, :] * x + 2.0 * terms[s]
+        x = held_ref[2 * s : 2 * s + 2, :].astype(BF).astype(F32)
+        base_s[2 * s : 2 * s + 2, :] = held_ref[4 + s : 5 + s, :] * x + 2.0 * terms[s]
     base_ref[...] = base_s[...]
 
     lane = lanes(1, 256)
@@ -206,15 +236,15 @@
                 route_s[at : at + 1, :] = jnp.where(hit, sign, 0.0)
     route_ref[...] = route_s[...].astype(BF)
 
-    wide = lanes(1, 512)
-    sent = jnp.full((1, 512), -1, jnp.int32)
-    for peer in range(8):
+    sent = jnp.full((1, 256), -1, jnp.int32)
+    core = lax.rem(q_me, 2)
+    for peer in range(4):
         for e in range(6):
-            here = (wide // 64 == peer) & (lax.rem(wide, 16) // 2 == e)
-            sent = jnp.where(here, plane_ref[peer, 0, e], sent)
-    row = lax.broadcasted_iota(jnp.int32, (64, 512), 0)
-    target = (row // 4) * 16 + q_me * 2 + lax.rem(row, 4) // 2
-    hit = (sent == target) & (lax.rem(row, 2) == lax.rem(lanes(64, 512), 2))
+            here = (lane // 64 == peer) & (lax.rem(lane, 16) // 2 == e)
+            sent = jnp.where(here, plane_ref[2 * peer + core, 0, e], sent)
+    row = lax.broadcasted_iota(jnp.int32, (128, 256), 0)
+    target = (row // 8) * 16 + (q_me // 2) * 4 + lax.rem(row, 8) // 2
+    hit = (sent == target) & (lax.rem(row, 2) == lax.rem(lanes(128, 256), 2))
     back_ref[...] = jnp.where(hit, -1.0, 0.0).astype(BF)
 
 
@@ -342,41 +372,49 @@
     for part in range(4):
         for e in range(6):
             rs_ref[part, 2 * e : 2 * e + 2, :] = ys_ref[e, 2 * part : 2 * part + 2, :]
-    for peer in range(8):
+    for peer in range(4):
         for part in range(4):
             out_ref[4 * peer + part, :, 0:256] = rs_ref[part].astype(BF)
             out_ref[4 * peer + part, :, 256:384] = ds_ref[...].astype(BF)
 
 
 def return_kernel(info_ref, back_ref, got_ref, out_ref, buf_ref):
-    full = dot(back_ref[...], got_ref[:, :, 0:256].reshape(512, 256))
+    full = dot(back_ref[...], got_ref[:, :, 0:256].reshape(256, 256))
     y_me = info_ref[10]
     total = got_ref[y_me, :, 256:384].astype(F32)
-    for peer in range(1, 8):
+    for peer in range(1, 4):
         total = total + got_ref[4 * peer + y_me, :, 256:384].astype(F32)
-    buf_ref[...] = jnp.zeros((16, 16, 256), F32)
     for part in range(4):
         for h in range(2):
             at = 4 * part + 2 * h
-            buf_ref[0, 4 + 2 * part : 6 + 2 * part, 128 * h : 128 * h + 128] = total[at : at + 2, :]
+            buf_ref[2 * part : 2 * part + 2, 128 * h : 128 * h + 128] = total[at : at + 2, :]
     for z in range(16):
-        if z:
-            buf_ref[z, 4:12, :] = buf_ref[0, 4:12, :]
-        buf_ref[z, 0:4, :] = full[4 * z : 4 * z + 4, :]
-    out_ref[...] = buf_ref[...].astype(BF)
-
-
-def last_kernel(cheb_ref, got_ref, own_ref, bare_ref, trans_ref, trial_ref, own_x_ref, out_ref):
+        rows = jnp.concatenate([full[8 * z : 8 * z + 8, :], buf_ref[...]], axis=0)
+        out_ref[z] = rows.astype(BF)
+
+
+def cross_kernel(info_ref, got_ref, keep_ref, send_ref, buf_ref):
     total = got_ref[0].astype(F32)
     for z in range(1, 16):
         total = total + got_ref[z].astype(F32)
+    mine = lax.rem(info_ref[9], 2) == 0
+    buf_ref[0:4, :] = jnp.where(mine, total[0:4, :], total[4:8, :])
+    buf_ref[4:12, :] = total[8:16, :]
+    buf_ref[12:16, :] = jnp.zeros((4, 256), F32)
+    keep_ref[...] = buf_ref[...]
+    buf_ref[0:4, :] = jnp.where(mine, total[4:8, :], total[0:4, :])
+    send_ref[...] = buf_ref[...].astype(BF)
+
+
+def last_kernel(cheb_ref, keep_ref, got_ref, own_ref, bare_ref, held_ref, own_x_ref, out_ref):
+    total = keep_ref[...] + got_ref[...].astype(F32)
     dens = [total[4 + 2 * part : 6 + 2 * part, :] for part in range(4)]
     terms = bare_of(own_ref, bare_ref, dens)
     for s in range(2):
         x = own_x_ref[2 * s : 2 * s + 2, :]
-        t = trial_ref[:, s, :]
+        t = held_ref[2 * s : 2 * s + 2, :]
         applied = (
-            trans_ref[s : s + 1, :] * x.astype(BF).astype(F32)
+            held_ref[4 + s : 5 + s, :] * x.astype(BF).astype(F32)
             + 2.0 * terms[s]
             + total[2 * s : 2 * s + 2, :]
         )
@@ -385,21 +423,34 @@
 
 
 def body(orbitals, transition, trial, screened, bare, cheb, pair_k, pair_slot, k_order):
-    info, ids, copies = call(
+    info, ids, copies, held = call(
         info_kernel,
-        [((16,), jnp.int32), ((8, 1, 128), jnp.int32), ((4, 2, 32, 256), BF)],
-        (0, 1),
-    )(pair_k, pair_slot, k_order.reshape(1, -1), orbitals)
+        [
+            ((16,), jnp.int32), ((8, 1, 128), jnp.int32), ((4, 2, 32, 256), BF), ((8, 256), F32),
+        ],
+        (),
+        [
+            pltpu.SMEM((3,), jnp.int32),
+            pltpu.SMEM((3,), jnp.int32),
+            pltpu.VMEM((1, 256), jnp.int32),
+            pltpu.VMEM((2, 2, 256), F32),
+            pltpu.VMEM((2, 256), F32),
+            pltpu.SemaphoreType.DMA((9,)),
+        ],
+        range(6),
+        66600000,
+    )(pair_k, pair_slot, k_order.reshape(1, -1), orbitals, trial, transition)
     own = exchange(copies, "y")
     plane = exchange(ids, PLANE)
     (packed,) = call(pack_kernel, [((80, 256), BF)], (0,), [pltpu.VMEM((16, 256), F32)])(
-        info, orbitals, trial, own
+        info, held, own
     )
     gat = lax.all_gather(packed, "z")
-    (chosen,) = call(select_kernel, [((8, 224, 256), BF)], (0,), [pltpu.VMEM((256, 256), F32)])(
-        plane, gat
+    twin = swap(gat)
+    (chosen,) = call(select_kernel, [((4, 224, 256), BF)], (0, 1), [pltpu.VMEM((128, 512), F32)])(
+        info, plane, gat, twin
     )
-    got = exchange(chosen, PLANE)
+    got = exchange(chosen, "x")
     val, cond, dens = call(
         accept_kernel,
         [((4, 112, 256), BF), ((6, 16, 256), BF), ((8, 256), F32)],
@@ -409,10 +460,10 @@
     wide = exchange(val, "y")
     base, route, back = call(
         base_kernel,
-        [((4, 256), F32), ((128, 256), BF), ((64, 512), BF)],
+        [((4, 256), F32), ((128, 256), BF), ((128, 256), BF)],
         (0, 1),
         [pltpu.VMEM((4, 256), F32), pltpu.VMEM((128, 256), F32)],
-    )(info, plane, dens, gat, own, bare, transition, trial)
+    )(info, plane, dens, gat, own, bare, held)
     work = [
         pltpu.VMEM((6, 8, 256), F32),
         pltpu.VMEM((6, 8, 256), F32),
@@ -430,17 +481,19 @@
     arrived = exchange(middle, BLOCK)
     out2, own_x = call(
         second_kernel,
-        [((32, 16, 384), BF), ((4, 256), F32)],
+        [((16, 16, 384), BF), ((4, 256), F32)],
         (0,),
         work + [pltpu.VMEM((16, 128), F32)],
     )(info, arrived, half, cond, own)
-    returned = exchange(out2, BLOCK)
-    (final,) = call(
-        return_kernel, [((16, 16, 256), BF)], (0,), [pltpu.VMEM((16, 16, 256), F32)]
-    )(info, back, returned)
-    last = exchange(final, "z")
+    returned = exchange(out2, SHEET)
+    (final,) = call(return_kernel, [((16, 16, 256), BF)], (0,), [pltpu.VMEM((8, 256), F32)])(
+        info, back, returned
+    )
+    keep, send = call(
+        cross_kernel, [((16, 256), F32), ((16, 256), BF)], (0,), [pltpu.VMEM((16, 256), F32)]
+    )(info, exchange(final, "z"))
     (result,) = call(last_kernel, [(trial.shape, F32)], (0,))(
-        cheb, last, own, bare, transition, trial, own_x
+        cheb, keep, swap(send), own, bare, held, own_x
     )
     return result
 

time: 177 us -> 176 us (level)
  the two profiles are of different devices: /device:TPU:32 before, /device:TPU:1 now
where the time goes in v3:
time: 176 us; the launch traced here: 175 us
  blocking collectives  130 us (74%)
  starting transfers between devices  19.7 us (11%)
  Pallas kernels  18.2 us (10%)
  waiting for transfers between devices  4.43 us (3%)
  local copies, waits for them, and re-layouts  2.62 us (1%)
    all_to_all x8, blocking collectives, exchange(): return lax.all_to_all(blocks, axis, 0, 0, tiled=True)  96.7 us
    all_gather x1, blocking collectives, body(): gat = lax.all_gather(packed, 'z')  33.1 us
    pallas_call x12, Pallas kernels, run(): pl.pallas_call(kernel, out_shape=[jax.ShapeDtypeStruct(s, d) for s, d in...  18.2 us
    ppermute x2, starting transfers between devices, swap(): return lax.ppermute(shard, 'c', [(0, 1), (1, 0)])  16.3 us
    all_to_all x1, waiting for transfers between devices, exchange(): return lax.all_to_all(blocks, axis, 0, 0, tiled=True)  3.63 us
  transfers between devices with their start and end apart: 3, of which 2 were waited for; matrix products, arithmetic and copies ran while one was open for 0% of the time, Pallas kernels for 1%

profile of v3, /device:TPU:1, one launch (start us, length us, event | category | flops | bytes accessed | tf_op | source)
XLA Modules:
  0.0 174.8 jit_solution(10365684148106795768)
XLA Ops:
  0.0 1.6 shard_map.91
  1.7 9.8 %all_to_all.45.own_ref = bf16[4,2,32,256]{3,2,1,0:T(8,128)(2,1)S(1)} all-to-all(bf16[4,2,32,256]{3,2,1,0:T(8,128)(2,1)} %get-tuple-element.24), channel_id=1, replica_groups=mesh['z'=16,'x'=4,'c'=2,'y'=4] {'y'}, dimensions={0} | all-to-all | bytes 262144 | tf_op jit(solution)/shard_map/all_to_all | solution.py:21
  11.5 0.0 copy-start.2
  11.5 0.7 copy-done.2
  12.2 0.0 copy-start.4
  12.2 0.7 copy-done.4
  12.9 0.8 shard_map.92
  13.7 0.0 copy-start
  13.7 0.0 copy-start.3
  13.7 0.0 copy-start.5
  13.7 33.1 %all-gather = bf16[1280,256]{1,0:T(8,128)(2,1)S(1)} all-gather(bf16[80,256]{1,0:T(8,128)(2,1)S(1)} %shard_map.92), channel_id=2, replica_groups=mesh['z'=16,'x'=4,'c'=2,'y'=4] {'z'}, dimensions={0}, use_global_device_ids=true | all-gather | bytes 696320 | tf_op jit(solution)/shard_map/all_gather | solution.py:448
  46.8 10.4 %collective-permute-start = (bf16[16,80,256]{2,1,0:T(8,128)(2,1)S(1)}, bf16[16,80,256]{2,1,0:T(8,128)(2,1)S(1)}, u32[]{:S(2)}, u32[]{:S(2)}) collective-permute-start(bf16[16,80,256]{2,1,0:T(8,128)(2,1)S(1)} %bitcast.2), channel_id=1, source_target_pairs={{0,4},{4,0},{1,5},{5,1},{2,6},{6,2},{3,7},{7,3},{8,12},{12,8},{9,1... | collective-permute-start | bytes 1966088 | tf_op jit(solution)/shard_map/ppermute | solution.py:25
  57.1 8.9 %all_to_all.46.plane_ref = s32[8,1,128]{2,1,0:T(1,128)S(1)} all-to-all(s32[8,1,128]{2,1,0:T(1,128)} %get-tuple-element.22), channel_id=1, replica_groups=mesh['z'=16,'x'=4,'c'=2,'y'=4] {'x','c'}, dimensions={0} | all-to-all | bytes 8192 | tf_op jit(solution)/shard_map/all_to_all | solution.py:21
  66.1 0.0 collective-permute-done.twin_ref
  66.1 1.5 shard_map.93
  67.6 10.5 %all_to_all.47.got_ref = bf16[4,224,256]{2,1,0:T(8,128)(2,1)S(1)} all-to-all(bf16[4,224,256]{2,1,0:T(8,128)(2,1)S(1)} %shard_map.93), channel_id=1, replica_groups=mesh['z'=16,'x'=4,'c'=2,'y'=4] {'x'}, dimensions={0} | all-to-all | bytes 917504 | tf_op jit(solution)/shard_map/all_to_all | solution.py:21
  78.2 1.3 shard_map.94
  79.5 3.4 %all-to-all-start.3 = ((bf16[4,112,256]{2,1,0:T(8,128)(2,1)}), bf16[4,112,256]{2,1,0:T(8,128)(2,1)S(1)}, u32[]{:S(2)}, u32[]{:S(2)}) async-start(bf16[4,112,256]{2,1,0:T(8,128)(2,1)} %get-tuple-element.28), calls=%async_computation.3 | async-start | bytes 458752 | tf_op jit(solution)/shard_map/all_to_all | solution.py:21
  82.8 0.0 copy-done
  82.9 0.0 copy-done.3
  82.9 0.0 copy-done.5
  82.9 1.7 shard_map.95
  84.5 3.6 %all-to-all-done.3.wide_ref = bf16[4,112,256]{2,1,0:T(8,128)(2,1)S(1)} async-done(((bf16[4,112,256]{2,1,0:T(8,128)(2,1)}), bf16[4,112,256]{2,1,0:T(8,128)(2,1)S(1)}, u32[]{:S(2)}, u32[]{:S(2)}) %all-to-all-start.3) | async-done | bytes 229408 | tf_op jit(solution)/shard_map/all_to_all | solution.py:21
  88.2 0.0 copy-start.1
  88.2 1.2 copy-done.1
  89.4 4.1 %shard_map.96 = (f32[6,256,128]{2,1,0:T(8,128)S(1)}, bf16[4,16,256]{2,1,0:T(8,128)(2,1)S(1)}) custom-call(s32[16]{0:T(128)S(1)} %copy-done.5, bf16[4,112,256]{2,1,0:T(8,128)(2,1)S(1)} %all-to-all-done.3.wide_ref, bf16[6,16,256]{2,1,0:T(8,128)(2,1)S(1)} %get-tuple-element.29.cond_ref, bf16[2,1024,256]{2,1,0:T(8,128)(2,1)S(1)} %copy-done.1, ...), custom_call_target="tpu_custom_call" | custom-call | bytes 4194304 | tf_op jit(solution)/shard_map/pallas_call | solution.py:42
  93.5 0.0 copy-start.6
  93.5 6.7 %all_to_all.48.got_ref = bf16[4,16,256]{2,1,0:T(8,128)(2,1)S(1)} all-to-all(bf16[4,16,256]{2,1,0:T(8,128)(2,1)S(1)} %get-tuple-element.31), channel_id=1, replica_groups=mesh['z'=16,'x'=4,'c'=2,'y'=4] {'y'}, dimensions={0} | all-to-all | bytes 65536 | tf_op jit(solution)/shard_map/all_to_all | solution.py:21
  100.2 18.5 %all_to_all.49.col_ref = bf16[16,16,256]{2,1,0:T(8,128)(2,1)S(1)} all-to-all(bf16[16,16,256]{2,1,0:T(8,128)(2,1)S(1)} %shard_map.97), channel_id=1, replica_groups=mesh['z'=16,'x'=4,'c'=2,'y'=4] {'z'}, dimensions={0} | all-to-all | bytes 262144 | tf_op jit(solution)/shard_map/all_to_all | solution.py:21
  118.7 0.2 shard_map.98
  118.9 17.1 %all_to_all.50.got_ref = bf16[32,16,256]{2,1,0:T(8,128)(2,1)S(1)} all-to-all(bf16[32,16,256]{2,1,0:T(8,128)(2,1)S(1)} %shard_map.98), channel_id=1, replica_groups=mesh['z'=16,'x'=4,'c'=2,'y'=4] {'x','c','y'}, dimensions={0} | all-to-all | bytes 524288 | tf_op jit(solution)/shard_map/all_to_all | solution.py:21
  136.0 3.6 %shard_map.99 = (bf16[16,16,384]{2,1,0:T(8,128)(2,1)S(1)}, f32[4,256]{1,0:T(4,128)S(1)}) custom-call(s32[16]{0:T(128)S(1)} %copy-done.5, bf16[32,16,256]{2,1,0:T(8,128)(2,1)S(1)} %all_to_all.50.got_ref, f32[6,256,128]{2,1,0:T(8,128)S(1)} %get-tuple-element.32.half_ref, bf16[6,16,256]{2,1,0:T(8,128)(2,1)S(1)} %get-tuple-element.29.cond_ref, ...), custom_call_target="tpu_custom_call" | custom-call | bytes 4194304 | tf_op jit(solution)/shard_map/pallas_call | solution.py:42
  139.6 9.5 %all_to_all.51.got_ref = bf16[16,16,384]{2,1,0:T(8,128)(2,1)S(1)} all-to-all(bf16[16,16,384]{2,1,0:T(8,128)(2,1)S(1)} %get-tuple-element.33), channel_id=1, replica_groups=mesh['z'=16,'x'=4,'c'=2,'y'=4] {'x','y'}, dimensions={0} | all-to-all | bytes 393216 | tf_op jit(solution)/shard_map/all_to_all | solution.py:21
  149.1 0.7 shard_map.100
  149.8 15.6 %all_to_all.52.got_ref = bf16[16,16,256]{2,1,0:T(8,128)(2,1)S(1)} all-to-all(bf16[16,16,256]{2,1,0:T(8,128)(2,1)S(1)} %shard_map.100), channel_id=1, replica_groups=mesh['z'=16,'x'=4,'c'=2,'y'=4] {'z'}, dimensions={0} | all-to-all | bytes 262144 | tf_op jit(solution)/shard_map/all_to_all | solution.py:21
  165.4 0.6 shard_map.101
  166.0 5.9 %collective-permute-start.1 = (bf16[16,256]{1,0:T(8,128)(2,1)S(1)}, bf16[16,256]{1,0:T(8,128)(2,1)S(1)}, u32[]{:S(2)}, u32[]{:S(2)}) collective-permute-start(bf16[16,256]{1,0:T(8,128)(2,1)S(1)} %get-tuple-element.35), channel_id=1, source_target_pairs={{0,4},{4,0},{1,5},{5,1},{2,6},{6,2},{3,7},{7,3},{8,12},{12,8},{9,1... | collective-permute-start | bytes 24584 | tf_op jit(solution)/shard_map/ppermute | solution.py:25
  172.0 0.8 collective-permute-done.1.got_ref
  172.8 0.0 copy-done.6
  172.8 2.1 %shard_map.102 = f32[2,2,256]{2,1,0:T(2,128)} custom-call(f32[3]{0:T(128)S(1)} %copy-done.6, f32[16,256]{1,0:T(8,128)S(1)} %get-tuple-element.34.keep_ref, bf16[16,256]{1,0:T(8,128)(2,1)S(1)} %collective-permute-done.1.got_ref, bf16[4,2,32,256]{3,2,1,0:T(8,128)(2,1)S(1)} %all_to_all.45.own_ref, bf16[1024,1024]{1,0:T(8,128)(2,1)S(1)} %copy-done, ...), custom_call_target="tpu_custom_call" | custom-call | bytes 4194304 | tf_op jit(solution)/shard_map/pallas_call | solution.py:42
  (1 shorter events, 0.0 us)
Async XLA Ops:
  11.5 0.7 copy-start.2
  12.2 0.7 copy-start.4
  13.7 69.2 %copy-start = (bf16[1024,1024]{1,0:T(8,128)(2,1)S(1)}, bf16[1024,1024]{1,0:T(8,128)(2,1)}, u32[]{:S(2)}) copy-start(bf16[1024,1024]{1,0:T(8,128)(2,1)} %bare_ref.3) | copy-start | bytes 6291460
  13.7 69.2 %copy-start.3 = (f32[8,256]{1,0:T(8,128)S(1)}, f32[8,256]{1,0:T(8,128)}, u32[]{:S(2)}) copy-start(f32[8,256]{1,0:T(8,128)} %get-tuple-element.23.held_ref) | copy-start | bytes 24580
  13.7 69.2 %copy-start.5 = (s32[16]{0:T(128)S(1)}, s32[16]{0:T(128)}, u32[]{:S(2)}) copy-start(s32[16]{0:T(128)} %get-tuple-element.21.info_ref) | copy-start | bytes 196
  46.8 19.3 %collective-permute-start = (bf16[16,80,256]{2,1,0:T(8,128)(2,1)S(1)}, bf16[16,80,256]{2,1,0:T(8,128)(2,1)S(1)}, u32[]{:S(2)}, u32[]{:S(2)}) collective-permute-start(bf16[16,80,256]{2,1,0:T(8,128)(2,1)S(1)} %bitcast.2), channel_id=1, source_target_pairs={{0,4},{4,0},{1,5},{5,1},{2,6},{6,2},{3,7},{7,3},{8,12},{12,8},{9,1... | collective-permute-start | bytes 1966088 | tf_op jit(solution)/shard_map/ppermute | solution.py:25
  79.5 8.7 %all-to-all-start.3 = ((bf16[4,112,256]{2,1,0:T(8,128)(2,1)}), bf16[4,112,256]{2,1,0:T(8,128)(2,1)S(1)}, u32[]{:S(2)}, u32[]{:S(2)}) async-start(bf16[4,112,256]{2,1,0:T(8,128)(2,1)} %get-tuple-element.28), calls=%async_computation.3 | async-start | bytes 458752 | tf_op jit(solution)/shard_map/all_to_all | solution.py:21
  88.2 1.2 copy-start.1
  93.5 79.3 %copy-start.6 = (f32[3]{0:T(128)S(1)}, f32[3]{0:T(128)}, u32[]{:S(2)}) copy-start(f32[3]{0:T(128)} %cheb_ref.1) | copy-start | bytes 40
  166.0 6.8 %collective-permute-start.1 = (bf16[16,256]{1,0:T(8,128)(2,1)S(1)}, bf16[16,256]{1,0:T(8,128)(2,1)S(1)}, u32[]{:S(2)}, u32[]{:S(2)}) collective-permute-start(bf16[16,256]{1,0:T(8,128)(2,1)S(1)} %get-tuple-element.35), channel_id=1, source_target_pairs={{0,4},{4,0},{1,5},{5,1},{2,6},{6,2},{3,7},{7,3},{8,12},{12,8},{9,1... | collective-permute-start | bytes 24584 | tf_op jit(solution)/shard_map/ppermute | solution.py:25

commit v4 on v3

--- a/solution.py
+++ b/solution.py
@@ -13,7 +13,6 @@
 PB = ("z", "x", "c")
 PLANE = ("x", "c")
 BLOCK = ("x", "c", "y")
-SHEET = ("x", "y")
 LIMIT = 12 << 20
 
 
@@ -223,7 +222,6 @@
         row = gat_ref[z, 64:80, :].astype(F32)[12:13, :]
         held = jnp.where(lane // 16 == z, row, held)
     held = held.astype(jnp.int32)
-    sign = jnp.where(lax.rem(lane, 16) < 12, -1.0, 1.0)
     parity = lax.rem(lane, 2)
     z_me = info_ref[8]
     q_me = info_ref[9]
@@ -233,18 +231,18 @@
             for n in range(2):
                 at = peer * 16 + 2 * k + n
                 hit = (held == row) & (parity == n)
-                route_s[at : at + 1, :] = jnp.where(hit, sign, 0.0)
-    route_ref[...] = route_s[...].astype(BF)
-
-    sent = jnp.full((1, 256), -1, jnp.int32)
-    core = lax.rem(q_me, 2)
-    for peer in range(4):
+                route_s[at : at + 1, :] = jnp.where(hit, -1.0 if k < 6 else 1.0, 0.0)
+    route_ref[...] = jnp.transpose(route_s[...]).astype(BF)
+
+    wide = lanes(1, 512)
+    sent = jnp.full((1, 512), -1, jnp.int32)
+    for peer in range(8):
         for e in range(6):
-            here = (lane // 64 == peer) & (lax.rem(lane, 16) // 2 == e)
-            sent = jnp.where(here, plane_ref[2 * peer + core, 0, e], sent)
-    row = lax.broadcasted_iota(jnp.int32, (128, 256), 0)
-    target = (row // 8) * 16 + (q_me // 2) * 4 + lax.rem(row, 8) // 2
-    hit = (sent == target) & (lax.rem(row, 2) == lax.rem(lanes(128, 256), 2))
+            here = (wide // 64 == peer) & (lax.rem(wide, 16) // 2 == e)
+            sent = jnp.where(here, plane_ref[peer, 0, e], sent)
+    row = lax.broadcasted_iota(jnp.int32, (64, 512), 0)
+    target = (row // 4) * 16 + q_me * 2 + lax.rem(row, 4) // 2
+    hit = (sent == target) & (lax.rem(row, 2) == lax.rem(lanes(64, 512), 2))
     back_ref[...] = jnp.where(hit, -1.0, 0.0).astype(BF)
 
 
@@ -271,20 +269,17 @@
     for part in range(2):
         at = slice(128 * part, 128 * part + 128)
         t_c = [t_ref[1, 8 * w : 8 * w + 8, at] for w in range(16)]
-
-        def over_first(v, u_c):
-            row = pl.multiple_of(v * 8, 8)
-            t_a = t_ref[0, pl.ds(row, 8), at]
-            sums = [jnp.zeros((8, 128), F32)] * 2
-            new = []
+        u_c = [None] * 16
+        for v in range(16):
+            t_a = t_ref[0, 8 * v : 8 * v + 8, at]
+            sums = [None] * 2
             for w in range(16):
-                h = jnp.broadcast_to(half_ref[2 * i + part, pl.ds(v * 16 + w, 1), :], (8, 128))
-                sums[w % 2] = sums[w % 2] + h * t_c[w]
-                new.append(u_c[w] + h * t_a)
-            u_ref[0, pl.ds(row, 8), at] = sums[0] + sums[1]
-            return tuple(new)
-
-        u_c = lax.fori_loop(0, 16, over_first, (jnp.zeros((8, 128), F32),) * 16)
+                row = 16 * v + w
+                h = jnp.broadcast_to(half_ref[2 * i + part, row : row + 1, :], (8, 128))
+                one, two = h * t_c[w], h * t_a
+                sums[w % 2] = one if w < 2 else sums[w % 2] + one
+                u_c[w] = two if v == 0 else u_c[w] + two
+            u_ref[0, 8 * v : 8 * v + 8, at] = sums[0] + sums[1]
         for w in range(16):
             u_ref[1, 8 * w : 8 * w + 8, at] = u_c[w]
     ys_ref[2 * i] = gathered(dot_t(u_ref[0].astype(BF), tile_a))
@@ -323,45 +318,48 @@
             rs_ref[part, 2 * e : 2 * e + 2, :] = ys_ref[e, 2 * part : 2 * part + 2, :]
         mine = (info_ref[10] == part).astype(F32)
         rs_ref[part, 12:16, :] = base_ref[...] * mine
-    res_ref[...] = rs_ref[...].astype(BF)
-
-
-def column_kernel(got_ref, out_ref):
-    total = got_ref[0].astype(F32)
-    for part in range(1, 4):
-        total = total + got_ref[part].astype(F32)
-    for z in range(16):
-        out_ref[z] = total.astype(BF)
-
-
-def middle_kernel(route_ref, col_ref, out_ref):
-    full = dot(route_ref[...], col_ref[...].reshape(256, 256)).astype(BF)
     for peer in range(8):
         for part in range(4):
-            out_ref[4 * peer + part] = full[16 * peer : 16 * peer + 16, :]
-
-
-def second_kernel(
-    info_ref, got_ref, half_ref, cond_ref, own_ref, out_ref, own_x_ref,
-    xs_ref, ys_ref, t_ref, u_ref, rs_ref, ds_ref,
-):
-    for part in range(4):
-        total = got_ref[part].astype(F32)
-        for peer in range(1, 8):
+            res_ref[4 * peer + part] = rs_ref[part].astype(BF)
+
+
+def middle_kernel(route_ref, got_ref, out_ref):
+    peers = []
+    for peer in range(8):
+        total = got_ref[4 * peer].astype(F32)
+        for part in range(1, 4):
             total = total + got_ref[4 * peer + part].astype(F32)
-        for e in range(6):
-            xs_ref[e, 2 * part : 2 * part + 2, :] = total[2 * e : 2 * e + 2, :]
-    y_me = info_ref[10]
-    total = got_ref[y_me].astype(F32)
-    for peer in range(1, 8):
-        total = total + got_ref[4 * peer + y_me].astype(F32)
+        peers.append(total.astype(BF))
+    full = dot(route_ref[...], jnp.concatenate(peers, axis=0))
+    out_ref[...] = full.astype(BF).reshape(16, 16, 256)
+
+
+def step_kernel(got_ref, out_ref, own_x_ref):
+    total = got_ref[0].astype(F32)
+    for z in range(1, 16):
+        total = total + got_ref[z].astype(F32)
     own_x_ref[...] = total[12:16, :]
-    rows = [total[12 + 2 * s : 14 + 2 * s, :].astype(BF) for s in range(2)]
+    for part in range(4):
+        out_ref[part] = total.astype(BF)
+
+
+def density_kernel(own_x_ref, own_ref, out_ref, ds_ref):
+    rows = [own_x_ref[2 * s : 2 * s + 2, :].astype(BF) for s in range(2)]
     parts = density_of(own_ref, rows)
     for part in range(4):
         for h in range(2):
             at = 4 * part + 2 * h
             ds_ref[at : at + 2, :] = parts[part][:, 128 * h : 128 * h + 128]
+    out_ref[...] = ds_ref[...].astype(BF)
+
+
+def second_kernel(
+    got_ref, ds_ref, half_ref, cond_ref, out_ref, xs_ref, ys_ref, t_ref, u_ref, rs_ref,
+):
+    for part in range(4):
+        total = got_ref[part].astype(F32)
+        for e in range(6):
+            xs_ref[e, 2 * part : 2 * part + 2, :] = total[2 * e : 2 * e + 2, :]
 
     def one(i, carry):
         apply_pair(i, half_ref, cond_ref, xs_ref, ys_ref, t_ref, u_ref)
@@ -372,42 +370,34 @@
     for part in range(4):
         for e in range(6):
             rs_ref[part, 2 * e : 2 * e + 2, :] = ys_ref[e, 2 * part : 2 * part + 2, :]
-    for peer in range(4):
+    for peer in range(8):
         for part in range(4):
             out_ref[4 * peer + part, :, 0:256] = rs_ref[part].astype(BF)
-            out_ref[4 * peer + part, :, 256:384] = ds_ref[...].astype(BF)
+            out_ref[4 * peer + part, :, 256:384] = ds_ref[...]
 
 
 def return_kernel(info_ref, back_ref, got_ref, out_ref, buf_ref):
-    full = dot(back_ref[...], got_ref[:, :, 0:256].reshape(256, 256))
+    full = dot(back_ref[...], got_ref[:, :, 0:256].reshape(512, 256))
     y_me = info_ref[10]
     total = got_ref[y_me, :, 256:384].astype(F32)
-    for peer in range(1, 4):
+    for peer in range(1, 8):
         total = total + got_ref[4 * peer + y_me, :, 256:384].astype(F32)
+    buf_ref[...] = jnp.zeros((16, 16, 256), F32)
     for part in range(4):
         for h in range(2):
             at = 4 * part + 2 * h
-            buf_ref[2 * part : 2 * part + 2, 128 * h : 128 * h + 128] = total[at : at + 2, :]
+            buf_ref[0, 4 + 2 * part : 6 + 2 * part, 128 * h : 128 * h + 128] = total[at : at + 2, :]
     for z in range(16):
-        rows = jnp.concatenate([full[8 * z : 8 * z + 8, :], buf_ref[...]], axis=0)
-        out_ref[z] = rows.astype(BF)
-
-
-def cross_kernel(info_ref, got_ref, keep_ref, send_ref, buf_ref):
+        if z:
+            buf_ref[z, 4:12, :] = buf_ref[0, 4:12, :]
+        buf_ref[z, 0:4, :] = full[4 * z : 4 * z + 4, :]
+    out_ref[...] = buf_ref[...].astype(BF)
+
+
+def last_kernel(cheb_ref, got_ref, own_ref, bare_ref, held_ref, own_x_ref, out_ref):
     total = got_ref[0].astype(F32)
     for z in range(1, 16):
         total = total + got_ref[z].astype(F32)
-    mine = lax.rem(info_ref[9], 2) == 0
-    buf_ref[0:4, :] = jnp.where(mine, total[0:4, :], total[4:8, :])
-    buf_ref[4:12, :] = total[8:16, :]
-    buf_ref[12:16, :] = jnp.zeros((4, 256), F32)
-    keep_ref[...] = buf_ref[...]
-    buf_ref[0:4, :] = jnp.where(mine, total[4:8, :], total[0:4, :])
-    send_ref[...] = buf_ref[...].astype(BF)
-
-
-def last_kernel(cheb_ref, keep_ref, got_ref, own_ref, bare_ref, held_ref, own_x_ref, out_ref):
-    total = keep_ref[...] + got_ref[...].astype(F32)
     dens = [total[4 + 2 * part : 6 + 2 * part, :] for part in range(4)]
     terms = bare_of(own_ref, bare_ref, dens)
     for s in range(2):
@@ -460,7 +450,7 @@
     wide = exchange(val, "y")
     base, route, back = call(
         base_kernel,
-        [((4, 256), F32), ((128, 256), BF), ((128, 256), BF)],
+        [((4, 256), F32), ((256, 128), BF), ((64, 512), BF)],
         (0, 1),
         [pltpu.VMEM((4, 256), F32), pltpu.VMEM((128, 256), F32)],
     )(info, plane, dens, gat, own, bare, held)
@@ -472,28 +462,24 @@
         pltpu.VMEM((4, 16, 256), F32),
     ]
     half, res = call(
-        first_kernel, [((6, 256, 128), F32), ((4, 16, 256), BF)], (0,), work
+        first_kernel, [((6, 256, 128), F32), ((32, 16, 256), BF)], (0,), work
     )(info, wide, cond, screened, base)
-    parts = exchange(res, "y")
-    (column,) = call(column_kernel, [((16, 16, 256), BF)], ())(parts)
-    columns = exchange(column, "z")
-    (middle,) = call(middle_kernel, [((32, 16, 256), BF)], ())(route, columns)
-    arrived = exchange(middle, BLOCK)
-    out2, own_x = call(
-        second_kernel,
-        [((16, 16, 384), BF), ((4, 256), F32)],
-        (0,),
-        work + [pltpu.VMEM((16, 128), F32)],
-    )(info, arrived, half, cond, own)
-    returned = exchange(out2, SHEET)
-    (final,) = call(return_kernel, [((16, 16, 256), BF)], (0,), [pltpu.VMEM((8, 256), F32)])(
-        info, back, returned
-    )
-    keep, send = call(
-        cross_kernel, [((16, 256), F32), ((16, 256), BF)], (0,), [pltpu.VMEM((16, 256), F32)]
-    )(info, exchange(final, "z"))
+    (middle,) = call(middle_kernel, [((16, 16, 256), BF)], ())(route, exchange(res, BLOCK))
+    step, own_x = call(step_kernel, [((4, 16, 256), BF), ((4, 256), F32)], ())(
+        exchange(middle, "z")
+    )
+    (dens2,) = call(density_kernel, [((16, 128), BF)], (), [pltpu.VMEM((16, 128), F32)])(
+        own_x, own
+    )
+    (out2,) = call(second_kernel, [((32, 16, 384), BF)], (), work)(
+        exchange(step, "y"), dens2, half, cond
+    )
+    (final,) = call(
+        return_kernel, [((16, 16, 256), BF)], (0,), [pltpu.VMEM((16, 16, 256), F32)]
+    )(info, back, exchange(out2, BLOCK))
+    last = exchange(final, "z")
     (result,) = call(last_kernel, [(trial.shape, F32)], (0,))(
-        cheb, keep, swap(send), own, bare, held, own_x
+        cheb, last, own, bare, held, own_x
     )
     return result
 

time: 176 us -> 176 us (level)
  the two profiles are of different devices: /device:TPU:1 before, /device:TPU:32 now
where the time goes in v4:
time: 176 us; the launch traced here: 175 us
  blocking collectives  137 us (78%)
  Pallas kernels  15.6 us (9%)
  waiting for transfers between devices  9.92 us (6%)
  starting transfers between devices  8.56 us (5%)
  local copies, waits for them, and re-layouts  3.74 us (2%)
    all_to_all x7, blocking collectives, exchange(): return lax.all_to_all(blocks, axis, 0, 0, tiled=True)  99.2 us
    all_gather x1, blocking collectives, body(): gat = lax.all_gather(packed, 'z')  37.6 us
    pallas_call x12, Pallas kernels, run(): pl.pallas_call(kernel, out_shape=[jax.ShapeDtypeStruct(s, d) for s, d in...  15.6 us
    all_to_all x2, waiting for transfers between devices, exchange(): return lax.all_to_all(blocks, axis, 0, 0, tiled=True)  9.92 us
    all_to_all x2, starting transfers between devices, exchange(): return lax.all_to_all(blocks, axis, 0, 0, tiled=True)  6.65 us
    unnamed x18, local copies, waits for them, and re-layouts  3.74 us
  transfers between devices with their start and end apart: 3, of which 2 were waited for; matrix products, arithmetic and copies ran while one was open for 0% of the time, Pallas kernels for 1%

profile of v4, /device:TPU:32, one launch (start us, length us, event | category | flops | bytes accessed | tf_op | source)
XLA Modules:
  0.0 174.8 jit_solution(8008366309929173320)
XLA Ops:
  0.0 1.7 shard_map.91
  1.7 10.5 %all_to_all.45.own_ref = bf16[4,2,32,256]{3,2,1,0:T(8,128)(2,1)S(1)} all-to-all(bf16[4,2,32,256]{3,2,1,0:T(8,128)(2,1)} %get-tuple-element.22), channel_id=1, replica_groups=mesh['z'=16,'x'=4,'c'=2,'y'=4] {'y'}, dimensions={0} | all-to-all | bytes 262144 | tf_op jit(solution)/shard_map/all_to_all | solution.py:20
  12.1 0.0 copy-start.4
  12.1 0.7 copy-done.4
  12.8 0.0 copy-start.6
  12.8 0.7 copy-done.6
  13.5 0.8 shard_map.92
  14.3 0.0 copy-start
  14.3 0.0 copy-start.5
  14.3 0.0 copy-start.7
  14.3 37.6 %all-gather = bf16[1280,256]{1,0:T(8,128)(2,1)S(1)} all-gather(bf16[80,256]{1,0:T(8,128)(2,1)S(1)} %shard_map.92), channel_id=2, replica_groups=mesh['z'=16,'x'=4,'c'=2,'y'=4] {'z'}, dimensions={0}, use_global_device_ids=true | all-gather | bytes 696320 | tf_op jit(solution)/shard_map/all_gather | solution.py:438
  51.9 1.9 %collective-permute-start = (bf16[16,80,256]{2,1,0:T(8,128)(2,1)S(1)}, bf16[16,80,256]{2,1,0:T(8,128)(2,1)S(1)}, u32[]{:S(2)}, u32[]{:S(2)}) collective-permute-start(bf16[16,80,256]{2,1,0:T(8,128)(2,1)S(1)} %bitcast.2), channel_id=1, source_target_pairs={{0,4},{4,0},{1,5},{5,1},{2,6},{6,2},{3,7},{7,3},{8,12},{12,8},{9,1... | collective-permute-start | bytes 1966088 | tf_op jit(solution)/shard_map/ppermute | solution.py:24
  53.9 9.6 %all_to_all.46.plane_ref = s32[8,1,128]{2,1,0:T(1,128)S(1)} all-to-all(s32[8,1,128]{2,1,0:T(1,128)} %get-tuple-element.20), channel_id=1, replica_groups=mesh['z'=16,'x'=4,'c'=2,'y'=4] {'x','c'}, dimensions={0} | all-to-all | bytes 8192 | tf_op jit(solution)/shard_map/all_to_all | solution.py:20
  63.5 0.0 collective-permute-done.twin_ref
  63.5 1.5 shard_map.93
  65.0 11.4 %all_to_all.47.got_ref = bf16[4,224,256]{2,1,0:T(8,128)(2,1)S(1)} all-to-all(bf16[4,224,256]{2,1,0:T(8,128)(2,1)S(1)} %shard_map.93), channel_id=1, replica_groups=mesh['z'=16,'x'=4,'c'=2,'y'=4] {'x'}, dimensions={0} | all-to-all | bytes 917504 | tf_op jit(solution)/shard_map/all_to_all | solution.py:20
  76.4 1.3 shard_map.94
  77.7 3.4 %all-to-all-start.3 = ((bf16[4,112,256]{2,1,0:T(8,128)(2,1)}), bf16[4,112,256]{2,1,0:T(8,128)(2,1)S(1)}, u32[]{:S(2)}, u32[]{:S(2)}) async-start(bf16[4,112,256]{2,1,0:T(8,128)(2,1)} %get-tuple-element.26), calls=%async_computation.3 | async-start | bytes 458752 | tf_op jit(solution)/shard_map/all_to_all | solution.py:20
  81.1 0.0 copy-done
  81.1 0.0 copy-done.5
  81.1 0.0 copy-done.7
  81.1 1.7 shard_map.95
  82.8 4.8 %all-to-all-done.3.wide_ref = bf16[4,112,256]{2,1,0:T(8,128)(2,1)S(1)} async-done(((bf16[4,112,256]{2,1,0:T(8,128)(2,1)}), bf16[4,112,256]{2,1,0:T(8,128)(2,1)S(1)}, u32[]{:S(2)}, u32[]{:S(2)}) %all-to-all-start.3) | async-done | bytes 229408 | tf_op jit(solution)/shard_map/all_to_all | solution.py:20
  87.6 0.0 copy-start.1
  87.6 1.2 copy-done.1
  88.8 3.0 %shard_map.96 = (f32[6,256,128]{2,1,0:T(8,128)S(1)}, bf16[32,16,256]{2,1,0:T(8,128)(2,1)S(1)}) custom-call(s32[16]{0:T(128)S(1)} %copy-done.7, bf16[4,112,256]{2,1,0:T(8,128)(2,1)S(1)} %all-to-all-done.3.wide_ref, bf16[6,16,256]{2,1,0:T(8,128)(2,1)S(1)} %get-tuple-element.27.cond_ref, bf16[2,1024,256]{2,1,0:T(8,128)(2,1)S(1)} %copy-done.1, ...), custom_call_target="tpu_custom_call" | custom-call | bytes 4194304 | tf_op jit(solution)/shard_map/pallas_call | solution.py:41
  91.8 0.0 copy-start.2
  91.9 12.4 %all_to_all.48.got_ref = bf16[32,16,256]{2,1,0:T(8,128)(2,1)S(1)} all-to-all(bf16[32,16,256]{2,1,0:T(8,128)(2,1)S(1)} %get-tuple-element.29), channel_id=1, replica_groups=mesh['z'=16,'x'=4,'c'=2,'y'=4] {'x','c','y'}, dimensions={0} | all-to-all | bytes 524288 | tf_op jit(solution)/shard_map/all_to_all | solution.py:20
  104.2 0.0 copy-start.8
  104.2 0.2 shard_map.97
  104.4 0.0 copy-done.2
  104.4 23.2 %all_to_all.49.got_ref = bf16[16,16,256]{2,1,0:T(8,128)(2,1)S(1)} all-to-all(bf16[16,16,256]{2,1,0:T(8,128)(2,1)S(1)} %shard_map.97), channel_id=1, replica_groups=mesh['z'=16,'x'=4,'c'=2,'y'=4] {'z'}, dimensions={0} | all-to-all | bytes 262144 | tf_op jit(solution)/shard_map/all_to_all | solution.py:20
  127.6 0.6 shard_map.98
  128.3 3.3 %all-to-all-start.6 = ((bf16[4,16,256]{2,1,0:T(8,128)(2,1)}), bf16[4,16,256]{2,1,0:T(8,128)(2,1)S(1)}, u32[]{:S(2)}, u32[]{:S(2)}) async-start(bf16[4,16,256]{2,1,0:T(8,128)(2,1)} %get-tuple-element.30), calls=%async_computation.6 | async-start | bytes 65536 | tf_op jit(solution)/shard_map/all_to_all | solution.py:20
  131.5 0.3 shard_map.99.ds_ref
  131.8 5.1 %all-to-all-done.6.got_ref = bf16[4,16,256]{2,1,0:T(8,128)(2,1)S(1)} async-done(((bf16[4,16,256]{2,1,0:T(8,128)(2,1)}), bf16[4,16,256]{2,1,0:T(8,128)(2,1)S(1)}, u32[]{:S(2)}, u32[]{:S(2)}) %all-to-all-start.6) | async-done | bytes 32800 | tf_op jit(solution)/shard_map/all_to_all | solution.py:20
  137.0 0.0 copy-start.3
  137.0 1.1 copy-done.3
  138.1 1.7 shard_map.100
  139.8 13.5 %all_to_all.50.got_ref = bf16[32,16,384]{2,1,0:T(8,128)(2,1)S(1)} all-to-all(bf16[32,16,384]{2,1,0:T(8,128)(2,1)S(1)} %shard_map.100), channel_id=1, replica_groups=mesh['z'=16,'x'=4,'c'=2,'y'=4] {'x','c','y'}, dimensions={0} | all-to-all | bytes 786432 | tf_op jit(solution)/shard_map/all_to_all | solution.py:20
  153.3 0.7 shard_map.101
  154.1 18.6 %all_to_all.51.got_ref = bf16[16,16,256]{2,1,0:T(8,128)(2,1)S(1)} all-to-all(bf16[16,16,256]{2,1,0:T(8,128)(2,1)S(1)} %shard_map.101), channel_id=1, replica_groups=mesh['z'=16,'x'=4,'c'=2,'y'=4] {'z'}, dimensions={0} | all-to-all | bytes 262144 | tf_op jit(solution)/shard_map/all_to_all | solution.py:20
  172.7 0.0 copy-done.8
  172.7 2.1 %shard_map.102 = f32[2,2,256]{2,1,0:T(2,128)} custom-call(f32[3]{0:T(128)S(1)} %copy-done.8, bf16[16,16,256]{2,1,0:T(8,128)(2,1)S(1)} %all_to_all.51.got_ref, bf16[4,2,32,256]{3,2,1,0:T(8,128)(2,1)S(1)} %all_to_all.45.own_ref, bf16[1024,1024]{1,0:T(8,128)(2,1)S(1)} %copy-done, f32[8,256]{1,0:T(8,128)S(1)} %copy-done.5, f32[4,256]{1,0:T(4,128)S(1)} %get-tuple-element.31.own_x_ref), custom_call_target="tpu_custom_call" | custom-call | bytes 4194304 | tf_op jit(solution)/shard_map/pallas_call | solution.py:41
Async XLA Ops:
  12.1 0.7 copy-start.4
  12.8 0.7 copy-start.6
  14.3 66.8 %copy-start = (bf16[1024,1024]{1,0:T(8,128)(2,1)S(1)}, bf16[1024,1024]{1,0:T(8,128)(2,1)}, u32[]{:S(2)}) copy-start(bf16[1024,1024]{1,0:T(8,128)(2,1)} %bare_ref.3) | copy-start | bytes 6291460
  14.3 66.8 %copy-start.5 = (f32[8,256]{1,0:T(8,128)S(1)}, f32[8,256]{1,0:T(8,128)}, u32[]{:S(2)}) copy-start(f32[8,256]{1,0:T(8,128)} %get-tuple-element.21.held_ref) | copy-start | bytes 24580
  14.3 66.8 %copy-start.7 = (s32[16]{0:T(128)S(1)}, s32[16]{0:T(128)}, u32[]{:S(2)}) copy-start(s32[16]{0:T(128)} %get-tuple-element.19.info_ref) | copy-start | bytes 196
  51.9 11.5 %collective-permute-start = (bf16[16,80,256]{2,1,0:T(8,128)(2,1)S(1)}, bf16[16,80,256]{2,1,0:T(8,128)(2,1)S(1)}, u32[]{:S(2)}, u32[]{:S(2)}) collective-permute-start(bf16[16,80,256]{2,1,0:T(8,128)(2,1)S(1)} %bitcast.2), channel_id=1, source_target_pairs={{0,4},{4,0},{1,5},{5,1},{2,6},{6,2},{3,7},{7,3},{8,12},{12,8},{9,1... | collective-permute-start | bytes 1966088 | tf_op jit(solution)/shard_map/ppermute | solution.py:24
  77.7 9.9 %all-to-all-start.3 = ((bf16[4,112,256]{2,1,0:T(8,128)(2,1)}), bf16[4,112,256]{2,1,0:T(8,128)(2,1)S(1)}, u32[]{:S(2)}, u32[]{:S(2)}) async-start(bf16[4,112,256]{2,1,0:T(8,128)(2,1)} %get-tuple-element.26), calls=%async_computation.3 | async-start | bytes 458752 | tf_op jit(solution)/shard_map/all_to_all | solution.py:20
  87.6 1.2 copy-start.1
  91.8 12.6 %copy-start.2 = (f32[6,256,128]{2,1,0:T(8,128)}, f32[6,256,128]{2,1,0:T(8,128)S(1)}, u32[]{:S(2)}) copy-start(f32[6,256,128]{2,1,0:T(8,128)S(1)} %get-tuple-element.32.half_ref) | copy-start | bytes 2359300
  104.2 68.5 %copy-start.8 = (f32[3]{0:T(128)S(1)}, f32[3]{0:T(128)}, u32[]{:S(2)}) copy-start(f32[3]{0:T(128)} %cheb_ref.1) | copy-start | bytes 40
  128.3 8.7 %all-to-all-start.6 = ((bf16[4,16,256]{2,1,0:T(8,128)(2,1)}), bf16[4,16,256]{2,1,0:T(8,128)(2,1)S(1)}, u32[]{:S(2)}, u32[]{:S(2)}) async-start(bf16[4,16,256]{2,1,0:T(8,128)(2,1)} %get-tuple-element.30), calls=%async_computation.6 | async-start | bytes 65536 | tf_op jit(solution)/shard_map/all_to_all | solution.py:20
  137.0 1.1 copy-start.3

commit v5 on v4

--- a/solution.py
+++ b/solution.py
@@ -22,6 +22,11 @@
 
 def swap(shard):
     return lax.ppermute(shard, "c", [(0, 1), (1, 0)])
+
+
+def shift(shard, by):
+    count = lax.axis_size("y")
+    return lax.ppermute(shard, "y", [(k, (k + by) % count) for k in range(count)])
 
 
 def dot(a, b):
@@ -234,15 +239,15 @@
                 route_s[at : at + 1, :] = jnp.where(hit, -1.0 if k < 6 else 1.0, 0.0)
     route_ref[...] = jnp.transpose(route_s[...]).astype(BF)
 
-    wide = lanes(1, 512)
-    sent = jnp.full((1, 512), -1, jnp.int32)
+    wide = lanes(1, 128)
+    sent = jnp.full((1, 128), -1, jnp.int32)
     for peer in range(8):
         for e in range(6):
-            here = (wide // 64 == peer) & (lax.rem(wide, 16) // 2 == e)
+            here = (wide // 16 == peer) & (lax.rem(wide, 16) // 2 == e)
             sent = jnp.where(here, plane_ref[peer, 0, e], sent)
-    row = lax.broadcasted_iota(jnp.int32, (64, 512), 0)
+    row = lax.broadcasted_iota(jnp.int32, (64, 128), 0)
     target = (row // 4) * 16 + q_me * 2 + lax.rem(row, 4) // 2
-    hit = (sent == target) & (lax.rem(row, 2) == lax.rem(lanes(64, 512), 2))
+    hit = (sent == target) & (lax.rem(row, 2) == lax.rem(lanes(64, 128), 2))
     back_ref[...] = jnp.where(hit, -1.0, 0.0).astype(BF)
 
 
@@ -287,9 +292,12 @@
 
 
 def first_kernel(
-    info_ref, wide_ref, cond_ref, scr_ref, base_ref, half_ref, res_ref,
-    xs_ref, ys_ref, t_ref, u_ref, rs_ref,
+    info_ref, wide_ref, cond_ref, scr_ref, base_ref, op_ref, res_ref,
+    xs_ref, ys_ref, t_ref, u_ref, rs_ref, half_ref,
 ):
+    for e in range(6):
+        op_ref[0, 768 + 16 * e : 784 + 16 * e, :] = cond_ref[e, :, 0:128]
+        op_ref[1, 768 + 16 * e : 784 + 16 * e, :] = cond_ref[e, :, 128:256]
     for part in range(4):
         tail = wide_ref[part, 96:112, :].astype(F32)
         for e in range(6):
@@ -306,7 +314,11 @@
                 [(a[v : v + 1, :] * b).astype(BF) for v in range(16)], axis=0
             )
             total = total + dot(left, scr_ref[slot, part * 256 : (part + 1) * 256, :])
-        total = total.astype(BF).astype(F32)
+        total = total.astype(BF)
+        at = pl.multiple_of(i * 256, 256)
+        op_ref[0, pl.ds(at, 256), :] = total[:, 0:128]
+        op_ref[1, pl.ds(at, 256), :] = total[:, 128:256]
+        total = total.astype(F32)
         half_ref[2 * i] = total[:, 0:128]
         half_ref[2 * i + 1] = total[:, 128:256]
         apply_pair(i, half_ref, cond_ref, xs_ref, ys_ref, t_ref, u_ref)
@@ -334,54 +346,77 @@
     out_ref[...] = full.astype(BF).reshape(16, 16, 256)
 
 
-def step_kernel(got_ref, out_ref, own_x_ref):
+def picker(rows, columns):
+    row = lax.broadcasted_iota(jnp.int32, (rows, columns), 0)
+    return (lax.rem(row, 16) == lax.rem(lanes(rows, columns), 16)).astype(BF)
+
+
+def second_kernel(
+    got_ref, own_ref, op_ref, left_ref, right_ref, far_ref, out_ref, own_x_ref,
+    x_ref, y_ref, t_ref, ua_ref, uc_ref, rs_ref, ds_ref,
+):
     total = got_ref[0].astype(F32)
     for z in range(1, 16):
         total = total + got_ref[z].astype(F32)
     own_x_ref[...] = total[12:16, :]
-    for part in range(4):
-        out_ref[part] = total.astype(BF)
-
-
-def density_kernel(own_x_ref, own_ref, out_ref, ds_ref):
-    rows = [own_x_ref[2 * s : 2 * s + 2, :].astype(BF) for s in range(2)]
-    parts = density_of(own_ref, rows)
+    parts = density_of(own_ref, [total[12 + 2 * s : 14 + 2 * s, :].astype(BF) for s in range(2)])
     for part in range(4):
         for h in range(2):
             at = 4 * part + 2 * h
             ds_ref[at : at + 2, :] = parts[part][:, 128 * h : 128 * h + 128]
-    out_ref[...] = ds_ref[...].astype(BF)
-
-
-def second_kernel(
-    got_ref, ds_ref, half_ref, cond_ref, out_ref, xs_ref, ys_ref, t_ref, u_ref, rs_ref,
-):
-    for part in range(4):
-        total = got_ref[part].astype(F32)
-        for e in range(6):
-            xs_ref[e, 2 * part : 2 * part + 2, :] = total[2 * e : 2 * e + 2, :]
-
-    def one(i, carry):
-        apply_pair(i, half_ref, cond_ref, xs_ref, ys_ref, t_ref, u_ref)
+
+    here = lanes(16, 256) // 16 == lax.broadcasted_iota(jnp.int32, (16, 256), 0)
+    rows = [jnp.where(here, total[k : k + 1, :], 0.0).astype(BF) for k in range(12)]
+    x_ref[...] = dot(jnp.concatenate(rows, axis=0), picker(256, 16)).astype(BF)
+
+    chunks = [(ref, h) for ref in (op_ref, left_ref, right_ref, far_ref) for h in range(2)]
+
+    def one(p, carry):
+        at = pl.multiple_of(p * 64, 64)
+        conds = []
+        for end in range(2):
+            row = pl.multiple_of(768 + p * 32 + end * 16, 16)
+            conds.append(
+                jnp.concatenate([ref[h, pl.ds(row, 16), :] for ref, h in chunks], axis=1)
+            )
+            t_ref[end] = dot(x_ref[pl.ds(pl.multiple_of(at + 32 * end, 32), 32), :], conds[end])
+        for k, (ref, h) in enumerate(chunks):
+            span = slice(128 * k, 128 * k + 128)
+            t_c = [t_ref[1, 8 * g : 8 * g + 8, span] for g in range(4)]
+            sums = [None] * 4
+            for v in range(16):
+                tile = ref[h, pl.ds(pl.multiple_of(p * 256 + 16 * v, 16), 16), :].astype(F32)
+                lo, hi = tile[0:8, :], tile[8:16, :]
+                for n in range(2):
+                    ua_ref[128 * n + 8 * v : 128 * n + 8 * v + 8, span] = (
+                        lo * t_c[2 * n] + hi * t_c[2 * n + 1]
+                    )
+                    t_a = jnp.broadcast_to(
+                        t_ref[0, 16 * n + v : 16 * n + v + 1, span], (8, 128)
+                    )
+                    for g, part in ((2 * n, lo * t_a), (2 * n + 1, hi * t_a)):
+                        sums[g] = part if v == 0 else sums[g] + part
+            for g in range(4):
+                uc_ref[8 * g : 8 * g + 8, span] = sums[g]
+        first = dot_t(ua_ref[...].astype(BF), conds[0])
+        y_ref[pl.ds(at, 32), :] = jnp.sum(first.reshape(32, 8, 16), axis=1)
+        y_ref[pl.ds(pl.multiple_of(at + 32, 32), 32), :] = dot_t(uc_ref[...].astype(BF), conds[1])
         return carry
 
     lax.fori_loop(0, 3, one, 0)
-    rs_ref[...] = jnp.zeros((4, 16, 256), F32)
-    for part in range(4):
-        for e in range(6):
-            rs_ref[part, 2 * e : 2 * e + 2, :] = ys_ref[e, 2 * part : 2 * part + 2, :]
+    full = dot(y_ref[...].astype(BF), picker(16, 256)).reshape(12, 16, 256)
+    rs_ref[0:12, :] = jnp.sum(jnp.where(here[None], full, 0.0), axis=1)
+    rs_ref[12:16, :] = jnp.zeros((4, 256), F32)
     for peer in range(8):
-        for part in range(4):
-            out_ref[4 * peer + part, :, 0:256] = rs_ref[part].astype(BF)
-            out_ref[4 * peer + part, :, 256:384] = ds_ref[...]
-
-
-def return_kernel(info_ref, back_ref, got_ref, out_ref, buf_ref):
-    full = dot(back_ref[...], got_ref[:, :, 0:256].reshape(512, 256))
-    y_me = info_ref[10]
-    total = got_ref[y_me, :, 256:384].astype(F32)
+        out_ref[peer, :, 0:256] = rs_ref[...].astype(BF)
+        out_ref[peer, :, 256:384] = ds_ref[...].astype(BF)
+
+
+def return_kernel(back_ref, got_ref, out_ref, buf_ref):
+    full = dot(back_ref[...], got_ref[:, :, 0:256].reshape(128, 256))
+    total = got_ref[0, :, 256:384].astype(F32)
     for peer in range(1, 8):
-        total = total + got_ref[4 * peer + y_me, :, 256:384].astype(F32)
+        total = total + got_ref[peer, :, 256:384].astype(F32)
     buf_ref[...] = jnp.zeros((16, 16, 256), F32)
     for part in range(4):
         for h in range(2):
@@ -450,7 +485,7 @@
     wide = exchange(val, "y")
     base, route, back = call(
         base_kernel,
-        [((4, 256), F32), ((256, 128), BF), ((64, 512), BF)],
+        [((4, 256), F32), ((256, 128), BF), ((64, 128), BF)],
         (0, 1),
         [pltpu.VMEM((4, 256), F32), pltpu.VMEM((128, 256), F32)],
     )(info, plane, dens, gat, own, bare, held)
@@ -461,22 +496,35 @@
         pltpu.VMEM((2, 128, 256), F32),
         pltpu.VMEM((4, 16, 256), F32),
     ]
-    half, res = call(
-        first_kernel, [((6, 256, 128), F32), ((32, 16, 256), BF)], (0,), work
+    op, res = call(
+        first_kernel,
+        [((2, 864, 128), BF), ((32, 16, 256), BF)],
+        (0,),
+        work + [pltpu.VMEM((6, 256, 128), F32)],
     )(info, wide, cond, screened, base)
-    (middle,) = call(middle_kernel, [((16, 16, 256), BF)], ())(route, exchange(res, BLOCK))
-    step, own_x = call(step_kernel, [((4, 16, 256), BF), ((4, 256), F32)], ())(
-        exchange(middle, "z")
+    mixed = exchange(res, BLOCK)
+    left = shift(op, 1)
+    right = shift(op, -1)
+    (middle,) = call(middle_kernel, [((16, 16, 256), BF)], ())(route, mixed)
+    step = exchange(middle, "z")
+    far = shift(left, 1)
+    out2, own_x = call(
+        second_kernel,
+        [((8, 16, 384), BF), ((4, 256), F32)],
+        (),
+        [
+            pltpu.VMEM((192, 16), BF),
+            pltpu.VMEM((192, 16), F32),
+            pltpu.VMEM((2, 32, 1024), F32),
+            pltpu.VMEM((256, 1024), F32),
+            pltpu.VMEM((32, 1024), F32),
+            pltpu.VMEM((16, 256), F32),
+            pltpu.VMEM((16, 128), F32),
+        ],
+    )(step, own, op, left, right, far)
+    (final,) = call(return_kernel, [((16, 16, 256), BF)], (), [pltpu.VMEM((16, 16, 256), F32)])(
+        back, exchange(out2, PLANE)
     )
-    (dens2,) = call(density_kernel, [((16, 128), BF)], (), [pltpu.VMEM((16, 128), F32)])(
-        own_x, own
-    )
-    (out2,) = call(second_kernel, [((32, 16, 384), BF)], (), work)(
-        exchange(step, "y"), dens2, half, cond
-    )
-    (final,) = call(
-        return_kernel, [((16, 16, 256), BF)], (0,), [pltpu.VMEM((16, 16, 256), F32)]
-    )(info, back, exchange(out2, BLOCK))
     last = exchange(final, "z")
     (result,) = call(last_kernel, [(trial.shape, F32)], (0,))(
         cheb, last, own, bare, held, own_x

time: 176 us -> 177 us (level)
  blocking collectives: 137 us -> 117 us
  starting transfers between devices: 8.56 us -> 22.5 us
  waiting for transfers between devices: 9.92 us -> 15.6 us
    all_to_all x7 -> x6, blocking collectives: 99.2 us -> 79.3 us  [exchange(): return lax.all_to_all(blocks, axis, 0, 0, tiled=True)]
    ppermute x0 -> x3, waiting for transfers between devices: none -> 10.3 us  [shift(): lax.ppermute(shard, 'y', [(k, (k + by) % count) for k in range(count)])]
    ppermute x0 -> x3, starting transfers between devices: none -> 8.31 us  [shift(): lax.ppermute(shard, 'y', [(k, (k + by) % count) for k in range(count)])]
    all_to_all x2, starting transfers between devices: 6.65 us -> 12.2 us  [exchange(): return lax.all_to_all(blocks, axis, 0, 0, tiled=True)]
    all_to_all x2, waiting for transfers between devices: 9.92 us -> 5.3 us  [exchange(): return lax.all_to_all(blocks, axis, 0, 0, tiled=True)]
    pallas_call x12 -> x10, Pallas kernels: 15.6 us -> 16.1 us  [run(): pl.pallas_call(kernel, out_shape=[jax.ShapeDtypeStruct(s, d) for s, d in...]
  transfers between devices with their start and end apart: 3 -> 6, of which waited for: 2 -> 4; matrix products, arithmetic and copies ran while one was open for 0% -> 0% of each run, Pallas kernels for 1% -> 1%
where the time goes in v5:
time: 177 us; the launch traced here: 176 us
  blocking collectives  117 us (66%)
  starting transfers between devices  22.5 us (13%)
  Pallas kernels  16.1 us (9%)
  waiting for transfers between devices  15.6 us (9%)
  local copies, waits for them, and re-layouts  4.37 us (2%)
    all_to_all x6, blocking collectives, exchange(): return lax.all_to_all(blocks, axis, 0, 0, tiled=True)  79.3 us
    all_gather x1, blocking collectives, body(): gat = lax.all_gather(packed, 'z')  37.6 us
    pallas_call x10, Pallas kernels, run(): pl.pallas_call(kernel, out_shape=[jax.ShapeDtypeStruct(s, d) for s, d in...  16.1 us
    all_to_all x2, starting transfers between devices, exchange(): return lax.all_to_all(blocks, axis, 0, 0, tiled=True)  12.2 us
    ppermute x3, waiting for transfers between devices, shift(): lax.ppermute(shard, 'y', [(k, (k + by) % count) for k in range(count)])  10.3 us
    ppermute x3, starting transfers between devices, shift(): lax.ppermute(shard, 'y', [(k, (k + by) % count) for k in range(count)])  8.31 us
    all_to_all x2, waiting for transfers between devices, exchange(): return lax.all_to_all(blocks, axis, 0, 0, tiled=True)  5.3 us
    unnamed x18, local copies, waits for them, and re-layouts  4.37 us
  transfers between devices with their start and end apart: 6, of which 4 were waited for; matrix products, arithmetic and copies ran while one was open for 0% of the time, Pallas kernels for 1%

profile of v5, /device:TPU:32, one launch (start us, length us, event | category | flops | bytes accessed | tf_op | source)
XLA Modules:
  0.0 175.6 jit_solution(9096835729653430915)
XLA Ops:
  0.0 1.6 shard_map.91
  1.6 10.5 %all_to_all.40.own_ref = bf16[4,2,32,256]{3,2,1,0:T(8,128)(2,1)S(1)} all-to-all(bf16[4,2,32,256]{3,2,1,0:T(8,128)(2,1)} %get-tuple-element.22), channel_id=1, replica_groups=mesh['z'=16,'x'=4,'c'=2,'y'=4] {'y'}, dimensions={0} | all-to-all | bytes 262144 | tf_op jit(solution)/shard_map/all_to_all | solution.py:20
  12.1 0.0 copy-start.4
  12.1 0.7 copy-done.4
  12.8 0.0 copy-start.6
  12.8 0.7 copy-done.6
  13.5 0.8 shard_map.92
  14.3 0.0 copy-start
  14.3 0.0 copy-start.5
  14.3 0.0 copy-start.7
  14.3 37.6 %all-gather = bf16[1280,256]{1,0:T(8,128)(2,1)S(1)} all-gather(bf16[80,256]{1,0:T(8,128)(2,1)S(1)} %shard_map.92), channel_id=2, replica_groups=mesh['z'=16,'x'=4,'c'=2,'y'=4] {'z'}, dimensions={0}, use_global_device_ids=true | all-gather | bytes 696320 | tf_op jit(solution)/shard_map/all_gather | solution.py:473
  51.9 1.9 %collective-permute-start = (bf16[16,80,256]{2,1,0:T(8,128)(2,1)S(1)}, bf16[16,80,256]{2,1,0:T(8,128)(2,1)S(1)}, u32[]{:S(2)}, u32[]{:S(2)}) collective-permute-start(bf16[16,80,256]{2,1,0:T(8,128)(2,1)S(1)} %bitcast.2), channel_id=1, source_target_pairs={{0,4},{4,0},{1,5},{5,1},{2,6},{6,2},{3,7},{7,3},{8,12},{12,8},{9,1... | collective-permute-start | bytes 1966088 | tf_op jit(solution)/shard_map/ppermute | solution.py:24
  53.8 9.6 %all_to_all.41.plane_ref = s32[8,1,128]{2,1,0:T(1,128)S(1)} all-to-all(s32[8,1,128]{2,1,0:T(1,128)} %get-tuple-element.20), channel_id=1, replica_groups=mesh['z'=16,'x'=4,'c'=2,'y'=4] {'x','c'}, dimensions={0} | all-to-all | bytes 8192 | tf_op jit(solution)/shard_map/all_to_all | solution.py:20
  63.4 0.0 collective-permute-done.twin_ref
  63.5 1.5 shard_map.93
  65.0 11.4 %all_to_all.42.got_ref = bf16[4,224,256]{2,1,0:T(8,128)(2,1)S(1)} all-to-all(bf16[4,224,256]{2,1,0:T(8,128)(2,1)S(1)} %shard_map.93), channel_id=1, replica_groups=mesh['z'=16,'x'=4,'c'=2,'y'=4] {'x'}, dimensions={0} | all-to-all | bytes 917504 | tf_op jit(solution)/shard_map/all_to_all | solution.py:20
  76.4 1.3 shard_map.94
  77.7 3.4 %all-to-all-start.3 = ((bf16[4,112,256]{2,1,0:T(8,128)(2,1)}), bf16[4,112,256]{2,1,0:T(8,128)(2,1)S(1)}, u32[]{:S(2)}, u32[]{:S(2)}) async-start(bf16[4,112,256]{2,1,0:T(8,128)(2,1)} %get-tuple-element.26), calls=%async_computation.3 | async-start | bytes 458752 | tf_op jit(solution)/shard_map/all_to_all | solution.py:20
  81.1 0.0 copy-done
  81.1 0.0 copy-done.5
  81.1 0.0 copy-done.7
  81.1 1.6 shard_map.95
  82.7 4.8 %all-to-all-done.3.wide_ref = bf16[4,112,256]{2,1,0:T(8,128)(2,1)S(1)} async-done(((bf16[4,112,256]{2,1,0:T(8,128)(2,1)}), bf16[4,112,256]{2,1,0:T(8,128)(2,1)S(1)}, u32[]{:S(2)}, u32[]{:S(2)}) %all-to-all-start.3) | async-done | bytes 229408 | tf_op jit(solution)/shard_map/all_to_all | solution.py:20
  87.5 0.0 copy-start.1
  87.5 1.2 copy-done.1
  88.8 2.9 %shard_map.96 = (bf16[2,864,128]{2,1,0:T(8,128)(2,1)S(1)}, bf16[32,16,256]{2,1,0:T(8,128)(2,1)S(1)}) custom-call(s32[16]{0:T(128)S(1)} %copy-done.7, bf16[4,112,256]{2,1,0:T(8,128)(2,1)S(1)} %all-to-all-done.3.wide_ref, bf16[6,16,256]{2,1,0:T(8,128)(2,1)S(1)} %get-tuple-element.27.cond_ref, bf16[2,1024,256]{2,1,0:T(8,128)(2,1)S(1)} %copy-done.1, ...), custom_call_target="tpu_custom_call" | custom-call | bytes 4194304 | tf_op jit(solution)/shard_map/pallas_call | solution.py:46
  91.7 0.0 copy-start.8
  91.7 2.5 %collective-permute-start.1 = (bf16[2,864,128]{2,1,0:T(8,128)(2,1)S(1)}, bf16[2,864,128]{2,1,0:T(8,128)(2,1)S(1)}, u32[]{:S(2)}, u32[]{:S(2)}) collective-permute-start(bf16[2,864,128]{2,1,0:T(8,128)(2,1)S(1)} %get-tuple-element.30.op_ref), channel_id=1, source_target_pairs={{0,1},{1,2},{2,3},{3,0},{4,5},{5,6},{6,7},{7,4},{8,9},{9,10},{10,1... | collective-permute-start | bytes 1327112 | tf_op jit(solution)/shard_map/ppermute | solution.py:29
  94.2 13.9 %all_to_all.43.got_ref = bf16[32,16,256]{2,1,0:T(8,128)(2,1)S(1)} all-to-all(bf16[32,16,256]{2,1,0:T(8,128)(2,1)S(1)} %get-tuple-element.29), channel_id=1, replica_groups=mesh['z'=16,'x'=4,'c'=2,'y'=4] {'x','c','y'}, dimensions={0} | all-to-all | bytes 524288 | tf_op jit(solution)/shard_map/all_to_all | solution.py:20
  108.1 0.8 shard_map.97
  108.9 8.9 %all-to-all-start.5 = ((bf16[16,16,256]{2,1,0:T(8,128)(2,1)}), bf16[16,16,256]{2,1,0:T(8,128)(2,1)S(1)}, u32[]{:S(2)}, u32[]{:S(2)}) async-start(bf16[16,16,256]{2,1,0:T(8,128)(2,1)} %shard_map.97), calls=%async_computation.5 | async-start | bytes 262144 | tf_op jit(solution)/shard_map/all_to_all | solution.py:20
  117.7 3.2 %collective-permute-start.2 = (bf16[2,864,128]{2,1,0:T(8,128)(2,1)S(1)}, bf16[2,864,128]{2,1,0:T(8,128)(2,1)S(1)}, u32[]{:S(2)}, u32[]{:S(2)}) collective-permute-start(bf16[2,864,128]{2,1,0:T(8,128)(2,1)S(1)} %get-tuple-element.30.op_ref), channel_id=1, source_target_pairs={{0,3},{1,0},{2,1},{3,2},{4,7},{5,4},{6,5},{7,6},{8,11},{9,8},{10,9... | collective-permute-start | bytes 1327112 | tf_op jit(solution)/shard_map/ppermute | solution.py:29
  120.9 0.0 collective-permute-done.1.left_ref
  120.9 2.7 %collective-permute-start.3 = (bf16[2,864,128]{2,1,0:T(8,128)(2,1)S(1)}, bf16[2,864,128]{2,1,0:T(8,128)(2,1)}, u32[]{:S(2)}, u32[]{:S(2)}) collective-permute-start(bf16[2,864,128]{2,1,0:T(8,128)(2,1)S(1)} %collective-permute-done.1.left_ref), channel_id=1, source_target_pairs={{0,1},{1,2},{2,3},{3,0},{4,5},{5,6},{6,7},{7,4},{8,9},{9,10},{10,1... | collective-permute-start | bytes 1327112 | tf_op jit(solution)/shard_map/ppermute | solution.py:29
  123.6 7.5 %collective-permute-done.2.right_ref = bf16[2,864,128]{2,1,0:T(8,128)(2,1)S(1)} collective-permute-done((bf16[2,864,128]{2,1,0:T(8,128)(2,1)S(1)}, bf16[2,864,128]{2,1,0:T(8,128)(2,1)S(1)}, u32[]{:S(2)}, u32[]{:S(2)}) %collective-permute-start.2) | collective-permute-done | bytes 442400 | tf_op jit(solution)/shard_map/ppermute | solution.py:29
  131.1 0.0 copy-start.2
  131.1 0.8 copy-done.2
  131.8 0.5 all-to-all-done.5.got_ref
  132.3 2.8 %collective-permute-done.3.far_ref = bf16[2,864,128]{2,1,0:T(8,128)(2,1)} collective-permute-done((bf16[2,864,128]{2,1,0:T(8,128)(2,1)S(1)}, bf16[2,864,128]{2,1,0:T(8,128)(2,1)}, u32[]{:S(2)}, u32[]{:S(2)}) %collective-permute-start.3) | collective-permute-done | bytes 442400 | tf_op jit(solution)/shard_map/ppermute | solution.py:29
  135.2 0.0 copy-start.3
  135.2 1.0 copy-done.3
  136.2 3.2 %shard_map.98 = (bf16[8,16,384]{2,1,0:T(8,128)(2,1)S(1)}, f32[4,256]{1,0:T(4,128)S(1)}) custom-call(bf16[16,16,256]{2,1,0:T(8,128)(2,1)S(1)} %all-to-all-done.5.got_ref, bf16[4,2,32,256]{3,2,1,0:T(8,128)(2,1)S(1)} %all_to_all.40.own_ref, bf16[2,864,128]{2,1,0:T(8,128)(2,1)S(1)} %get-tuple-element.30.op_ref, ...), custom_call_target="tpu_custom_call" | custom-call | bytes 4194304 | tf_op jit(solution)/shard_map/pallas_call | solution.py:46
  139.4 8.2 %all_to_all.44.got_ref = bf16[8,16,384]{2,1,0:T(8,128)(2,1)S(1)} all-to-all(bf16[8,16,384]{2,1,0:T(8,128)(2,1)S(1)} %get-tuple-element.31), channel_id=1, replica_groups=mesh['z'=16,'x'=4,'c'=2,'y'=4] {'x','c'}, dimensions={0} | all-to-all | bytes 196608 | tf_op jit(solution)/shard_map/all_to_all | solution.py:20
  147.6 0.1 shard_map.99
  147.7 25.8 %all_to_all.45.got_ref = bf16[16,16,256]{2,1,0:T(8,128)(2,1)S(1)} all-to-all(bf16[16,16,256]{2,1,0:T(8,128)(2,1)S(1)} %shard_map.99), channel_id=1, replica_groups=mesh['z'=16,'x'=4,'c'=2,'y'=4] {'z'}, dimensions={0} | all-to-all | bytes 262144 | tf_op jit(solution)/shard_map/all_to_all | solution.py:20
  173.5 0.0 copy-done.8
  173.5 2.1 %shard_map.100 = f32[2,2,256]{2,1,0:T(2,128)} custom-call(f32[3]{0:T(128)S(1)} %copy-done.8, bf16[16,16,256]{2,1,0:T(8,128)(2,1)S(1)} %all_to_all.45.got_ref, bf16[4,2,32,256]{3,2,1,0:T(8,128)(2,1)S(1)} %all_to_all.40.own_ref, bf16[1024,1024]{1,0:T(8,128)(2,1)S(1)} %copy-done, f32[8,256]{1,0:T(8,128)S(1)} %copy-done.5, f32[4,256]{1,0:T(4,128)S(1)} %get-tuple-element.32.own_x_ref), custom_call_target="tpu_custom_call" | custom-call | bytes 4194304 | tf_op jit(solution)/shard_map/pallas_call | solution.py:46
Async XLA Ops:
  12.1 0.7 copy-start.4
  12.8 0.7 copy-start.6
  14.3 66.8 %copy-start = (bf16[1024,1024]{1,0:T(8,128)(2,1)S(1)}, bf16[1024,1024]{1,0:T(8,128)(2,1)}, u32[]{:S(2)}) copy-start(bf16[1024,1024]{1,0:T(8,128)(2,1)} %bare_ref.3) | copy-start | bytes 6291460
  14.3 66.8 %copy-start.5 = (f32[8,256]{1,0:T(8,128)S(1)}, f32[8,256]{1,0:T(8,128)}, u32[]{:S(2)}) copy-start(f32[8,256]{1,0:T(8,128)} %get-tuple-element.21.held_ref) | copy-start | bytes 24580
  14.3 66.8 %copy-start.7 = (s32[16]{0:T(128)S(1)}, s32[16]{0:T(128)}, u32[]{:S(2)}) copy-start(s32[16]{0:T(128)} %get-tuple-element.19.info_ref) | copy-start | bytes 196
  51.9 11.5 %collective-permute-start = (bf16[16,80,256]{2,1,0:T(8,128)(2,1)S(1)}, bf16[16,80,256]{2,1,0:T(8,128)(2,1)S(1)}, u32[]{:S(2)}, u32[]{:S(2)}) collective-permute-start(bf16[16,80,256]{2,1,0:T(8,128)(2,1)S(1)} %bitcast.2), channel_id=1, source_target_pairs={{0,4},{4,0},{1,5},{5,1},{2,6},{6,2},{3,7},{7,3},{8,12},{12,8},{9,1... | collective-permute-start | bytes 1966088 | tf_op jit(solution)/shard_map/ppermute | solution.py:24
  77.7 9.9 %all-to-all-start.3 = ((bf16[4,112,256]{2,1,0:T(8,128)(2,1)}), bf16[4,112,256]{2,1,0:T(8,128)(2,1)S(1)}, u32[]{:S(2)}, u32[]{:S(2)}) async-start(bf16[4,112,256]{2,1,0:T(8,128)(2,1)} %get-tuple-element.26), calls=%async_computation.3 | async-start | bytes 458752 | tf_op jit(solution)/shard_map/all_to_all | solution.py:20
  87.5 1.2 copy-start.1
  91.7 81.8 %copy-start.8 = (f32[3]{0:T(128)S(1)}, f32[3]{0:T(128)}, u32[]{:S(2)}) copy-start(f32[3]{0:T(128)} %cheb_ref.1) | copy-start | bytes 40
  91.7 29.2 %collective-permute-start.1 = (bf16[2,864,128]{2,1,0:T(8,128)(2,1)S(1)}, bf16[2,864,128]{2,1,0:T(8,128)(2,1)S(1)}, u32[]{:S(2)}, u32[]{:S(2)}) collective-permute-start(bf16[2,864,128]{2,1,0:T(8,128)(2,1)S(1)} %get-tuple-element.30.op_ref), channel_id=1, source_target_pairs={{0,1},{1,2},{2,3},{3,0},{4,5},{5,6},{6,7},{7,4},{8,9},{9,10},{10,1... | collective-permute-start | bytes 1327112 | tf_op jit(solution)/shard_map/ppermute | solution.py:29
  108.9 23.4 %all-to-all-start.5 = ((bf16[16,16,256]{2,1,0:T(8,128)(2,1)}), bf16[16,16,256]{2,1,0:T(8,128)(2,1)S(1)}, u32[]{:S(2)}, u32[]{:S(2)}) async-start(bf16[16,16,256]{2,1,0:T(8,128)(2,1)} %shard_map.97), calls=%async_computation.5 | async-start | bytes 262144 | tf_op jit(solution)/shard_map/all_to_all | solution.py:20
  117.7 13.3 %collective-permute-start.2 = (bf16[2,864,128]{2,1,0:T(8,128)(2,1)S(1)}, bf16[2,864,128]{2,1,0:T(8,128)(2,1)S(1)}, u32[]{:S(2)}, u32[]{:S(2)}) collective-permute-start(bf16[2,864,128]{2,1,0:T(8,128)(2,1)S(1)} %get-tuple-element.30.op_ref), channel_id=1, source_target_pairs={{0,3},{1,0},{2,1},{3,2},{4,7},{5,4},{6,5},{7,6},{8,11},{9,8},{10,9... | collective-permute-start | bytes 1327112 | tf_op jit(solution)/shard_map/ppermute | solution.py:29
  120.9 14.2 %collective-permute-start.3 = (bf16[2,864,128]{2,1,0:T(8,128)(2,1)S(1)}, bf16[2,864,128]{2,1,0:T(8,128)(2,1)}, u32[]{:S(2)}, u32[]{:S(2)}) collective-permute-start(bf16[2,864,128]{2,1,0:T(8,128)(2,1)S(1)} %collective-permute-done.1.left_ref), channel_id=1, source_target_pairs={{0,1},{1,2},{2,3},{3,0},{4,5},{5,6},{6,7},{7,4},{8,9},{9,10},{10,1... | collective-permute-start | bytes 1327112 | tf_op jit(solution)/shard_map/ppermute | solution.py:29
  131.1 0.8 copy-start.2
  135.2 1.0 copy-start.3

commit v6 on v5

--- a/solution.py
+++ b/solution.py
@@ -27,6 +27,10 @@
 def shift(shard, by):
     count = lax.axis_size("y")
     return lax.ppermute(shard, "y", [(k, (k + by) % count) for k in range(count)])
+
+
+def stay(array):
+    return pltpu.with_memory_space_constraint(array, pltpu.HBM)
 
 
 def dot(a, b):
@@ -100,7 +104,7 @@
 
 def info_kernel(
     pair_hbm, slot_hbm, order_hbm, orb_hbm, trial_hbm, trans_hbm,
-    info_ref, ids_ref, own_ref, held_ref, pair_ref, slot_ref, order_ref, trial_ref, trans_ref, sem,
+    ids_ref, own_ref, held_ref, pair_ref, slot_ref, order_ref, trial_ref, trans_ref, sem,
 ):
     moves = [
         (pair_hbm, pair_ref), (slot_hbm, slot_ref), (order_hbm, order_ref),
@@ -116,22 +120,17 @@
     short = lanes(1, 128)
     order = order_ref[...]
     ids = jnp.where(short == 6, position * 2, jnp.where(short == 7, position * 2 + 1, 0))
+    kind = lax.rem(lane, 16) // 2
+    spread_ids = position * 2 + kind - 6
     for i in range(3):
         first = pair_ref[i]
         second = first - position * 2 - slot_ref[i]
         second = jnp.where(second < 0, second + 256, second)
         for h, k in enumerate((first, second)):
             row = jnp.sum(jnp.where(order == k, lane, 0))
-            info_ref[2 * i + h] = row
             ids = jnp.where(short == 2 * i + h, row, ids)
-        info_ref[11 + i] = slot_ref[i]
-    info_ref[6] = position * 2
-    info_ref[7] = position * 2 + 1
-    info_ref[8] = lax.axis_index("z")
-    info_ref[9] = lax.axis_index(PLANE)
-    info_ref[10] = lax.axis_index("y")
-    info_ref[14] = 0
-    info_ref[15] = 0
+            spread_ids = jnp.where(kind == 2 * i + h, row, spread_ids)
+        ids = jnp.where(short == 8 + i, slot_ref[i], ids)
     for peer in range(8):
         ids_ref[peer] = ids
     for copy in copies[3:]:
@@ -140,10 +139,11 @@
     for s in range(2):
         held_ref[2 * s : 2 * s + 2, :] = trial_ref[:, s, :]
     held_ref[4:6, :] = trans_ref[...]
-
-
-def pack_kernel(info_ref, held_ref, own_ref, out_ref, tail_ref):
-    out_ref[0:64, :] = own_ref[info_ref[10]].reshape(64, 256)
+    held_ref[6:7, :] = spread_ids.astype(F32)
+
+
+def pack_kernel(held_ref, own_ref, out_ref, tail_ref):
+    out_ref[0:64, :] = own_ref[lax.axis_index("y")].reshape(64, 256)
     rows = [held_ref[2 * s : 2 * s + 2, :].astype(BF) for s in range(2)]
     parts = density_of(own_ref, rows)
     tail_ref[...] = jnp.zeros((16, 256), F32)
@@ -151,17 +151,18 @@
         tail_ref[2 * s : 2 * s + 2, :] = rows[s].astype(F32)
     for part in range(4):
         tail_ref[4 + 2 * part : 6 + 2 * part, :] = parts[part]
-    kind = lax.rem(lanes(1, 256), 16) // 2
-    ids = jnp.zeros((1, 256), jnp.int32)
-    for e in range(8):
-        ids = jnp.where(kind == e, info_ref[e], ids)
-    tail_ref[12:13, :] = ids.astype(F32)
+    tail_ref[12:13, :] = held_ref[6:7, :]
     out_ref[64:80, :] = tail_ref[...].astype(BF)
 
 
-def select_kernel(info_ref, plane_ref, gat_ref, twin_ref, out_ref, pick_ref):
+def select_kernel(plane_ref, gat_ref, twin_ref, out_ref, column_ref, pick_ref):
     lane = lanes(1, 512)
-    core = lax.rem(info_ref[9], 2)
+    core = lax.axis_index("c")
+    held = jnp.zeros((1, 256), F32)
+    for z in range(16):
+        row = gat_ref[z, 64:80, :].astype(F32)[12:13, :]
+        held = jnp.where(lanes(1, 256) // 16 == z, row, held)
+    column_ref[...] = jnp.broadcast_to(held, (8, 256))
     pick_ref[...] = jnp.zeros((128, 512), F32)
     for peer in range(4):
         for e in range(6):
@@ -192,9 +193,9 @@
     out_ref[:, 192:224, :] = picked.astype(BF).reshape(4, 32, 256)
 
 
-def accept_kernel(info_ref, got_ref, val_ref, cond_ref, dens_ref, tail_ref):
+def accept_kernel(plane_ref, got_ref, val_ref, cond_ref, dens_ref, tail_ref):
     for e in range(6):
-        column = lax.rem(info_ref[e] // 4, 4)
+        column = lax.rem(plane_ref[lax.axis_index(PLANE), 0, e] // 4, 4)
         val = got_ref[column, 32 * e : 32 * e + 16, :]
         for part in range(4):
             val_ref[part, 16 * e : 16 * e + 16, :] = val
@@ -211,25 +212,16 @@
 
 
 def base_kernel(
-    info_ref, plane_ref, dens_ref, gat_ref, own_ref, bare_ref, held_ref,
-    base_ref, route_ref, back_ref, base_s, route_s,
+    plane_ref, dens_ref, column_ref, own_ref, bare_hbm, held_ref,
+    base_ref, route_ref, back_ref, base_s, route_s, bare_ref, sem,
 ):
-    dens = [dens_ref[2 * part : 2 * part + 2, :] for part in range(4)]
-    terms = bare_of(own_ref, bare_ref, dens)
-    for s in range(2):
-        x = held_ref[2 * s : 2 * s + 2, :].astype(BF).astype(F32)
-        base_s[2 * s : 2 * s + 2, :] = held_ref[4 + s : 5 + s, :] * x + 2.0 * terms[s]
-    base_ref[...] = base_s[...]
-
+    copy = pltpu.make_async_copy(bare_hbm, bare_ref, sem)
+    copy.start()
     lane = lanes(1, 256)
-    held = jnp.zeros((1, 256), F32)
-    for z in range(16):
-        row = gat_ref[z, 64:80, :].astype(F32)[12:13, :]
-        held = jnp.where(lane // 16 == z, row, held)
-    held = held.astype(jnp.int32)
+    held = column_ref[0:1, :].astype(jnp.int32)
     parity = lax.rem(lane, 2)
-    z_me = info_ref[8]
-    q_me = info_ref[9]
+    z_me = lax.axis_index("z")
+    q_me = lax.axis_index(PLANE)
     for peer in range(8):
         for k in range(8):
             row = plane_ref[peer, 0, k] if k < 6 else z_me * 16 + peer * 2 + (k - 6)
@@ -249,6 +241,14 @@
     target = (row // 4) * 16 + q_me * 2 + lax.rem(row, 4) // 2
     hit = (sent == target) & (lax.rem(row, 2) == lax.rem(lanes(64, 128), 2))
     back_ref[...] = jnp.where(hit, -1.0, 0.0).astype(BF)
+
+    copy.wait()
+    dens = [dens_ref[2 * part : 2 * part + 2, :] for part in range(4)]
+    terms = bare_of(own_ref, bare_ref, dens)
+    for s in range(2):
+        x = held_ref[2 * s : 2 * s + 2, :].astype(BF).astype(F32)
+        base_s[2 * s : 2 * s + 2, :] = held_ref[4 + s : 5 + s, :] * x + 2.0 * terms[s]
+    base_ref[...] = base_s[...]
 
 
 def spread(x):
@@ -292,9 +292,11 @@
 
 
 def first_kernel(
-    info_ref, wide_ref, cond_ref, scr_ref, base_ref, op_ref, res_ref,
-    xs_ref, ys_ref, t_ref, u_ref, rs_ref, half_ref,
+    plane_ref, wide_ref, cond_ref, scr_hbm, base_ref, op_ref, res_ref,
+    xs_ref, ys_ref, t_ref, u_ref, rs_ref, half_ref, scr_ref, sem,
 ):
+    copy = pltpu.make_async_copy(scr_hbm, scr_ref, sem)
+    copy.start()
     for e in range(6):
         op_ref[0, 768 + 16 * e : 784 + 16 * e, :] = cond_ref[e, :, 0:128]
         op_ref[1, 768 + 16 * e : 784 + 16 * e, :] = cond_ref[e, :, 128:256]
@@ -303,8 +305,10 @@
         for e in range(6):
             xs_ref[e, 2 * part : 2 * part + 2, :] = tail[2 * e : 2 * e + 2, :]
 
+    copy.wait()
+
     def one(i, carry):
-        slot = info_ref[11 + i]
+        slot = plane_ref[lax.axis_index(PLANE), 0, 8 + i]
         total = jnp.zeros((256, 256), F32)
         for part in range(4):
             at = pl.multiple_of(i * 32, 16)
@@ -328,7 +332,7 @@
     for part in range(4):
         for e in range(6):
             rs_ref[part, 2 * e : 2 * e + 2, :] = ys_ref[e, 2 * part : 2 * part + 2, :]
-        mine = (info_ref[10] == part).astype(F32)
+        mine = (lax.axis_index("y") == part).astype(F32)
         rs_ref[part, 12:16, :] = base_ref[...] * mine
     for peer in range(8):
         for part in range(4):
@@ -417,23 +421,31 @@
     total = got_ref[0, :, 256:384].astype(F32)
     for peer in range(1, 8):
         total = total + got_ref[peer, :, 256:384].astype(F32)
-    buf_ref[...] = jnp.zeros((16, 16, 256), F32)
     for part in range(4):
         for h in range(2):
             at = 4 * part + 2 * h
-            buf_ref[0, 4 + 2 * part : 6 + 2 * part, 128 * h : 128 * h + 128] = total[at : at + 2, :]
+            span = slice(128 * h, 128 * h + 128)
+            buf_ref[0, 2 * part : 2 * part + 2, span] = total[at : at + 2, :]
     for z in range(16):
         if z:
-            buf_ref[z, 4:12, :] = buf_ref[0, 4:12, :]
-        buf_ref[z, 0:4, :] = full[4 * z : 4 * z + 4, :]
+            buf_ref[z, :, 0:256] = buf_ref[0, :, 0:256]
+        for h in range(2):
+            span = slice(128 * h, 128 * h + 128)
+            buf_ref[z, 4 * h : 4 * h + 4, 256:384] = full[4 * z : 4 * z + 4, span]
     out_ref[...] = buf_ref[...].astype(BF)
 
 
-def last_kernel(cheb_ref, got_ref, own_ref, bare_ref, held_ref, own_x_ref, out_ref):
+def last_kernel(
+    cheb_ref, got_ref, own_ref, bare_hbm, held_ref, own_x_ref, out_ref, bare_ref, sem
+):
+    copy = pltpu.make_async_copy(bare_hbm, bare_ref, sem)
+    copy.start()
     total = got_ref[0].astype(F32)
     for z in range(1, 16):
         total = total + got_ref[z].astype(F32)
-    dens = [total[4 + 2 * part : 6 + 2 * part, :] for part in range(4)]
+    dens = [total[2 * part : 2 * part + 2, 0:256] for part in range(4)]
+    rows = jnp.concatenate([total[0:4, 256:384], total[4:8, 256:384]], axis=1)
+    copy.wait()
     terms = bare_of(own_ref, bare_ref, dens)
     for s in range(2):
         x = own_x_ref[2 * s : 2 * s + 2, :]
@@ -441,18 +453,16 @@
         applied = (
             held_ref[4 + s : 5 + s, :] * x.astype(BF).astype(F32)
             + 2.0 * terms[s]
-            + total[2 * s : 2 * s + 2, :]
+            + rows[2 * s : 2 * s + 2, :]
         )
         second = 2.0 * applied - t
         out_ref[:, s, :] = cheb_ref[0] * t + cheb_ref[1] * x + cheb_ref[2] * second
 
 
 def body(orbitals, transition, trial, screened, bare, cheb, pair_k, pair_slot, k_order):
-    info, ids, copies, held = call(
+    ids, copies, held = call(
         info_kernel,
-        [
-            ((16,), jnp.int32), ((8, 1, 128), jnp.int32), ((4, 2, 32, 256), BF), ((8, 256), F32),
-        ],
+        [((8, 1, 128), jnp.int32), ((4, 2, 32, 256), BF), ((8, 256), F32)],
         (),
         [
             pltpu.SMEM((3,), jnp.int32),
@@ -463,32 +473,38 @@
             pltpu.SemaphoreType.DMA((9,)),
         ],
         range(6),
-        66600000,
-    )(pair_k, pair_slot, k_order.reshape(1, -1), orbitals, trial, transition)
+    )(*map(stay, (pair_k, pair_slot, k_order.reshape(1, -1), orbitals, trial, transition)))
+    far_bare = stay(bare)
     own = exchange(copies, "y")
     plane = exchange(ids, PLANE)
-    (packed,) = call(pack_kernel, [((80, 256), BF)], (0,), [pltpu.VMEM((16, 256), F32)])(
-        info, held, own
-    )
+    (packed,) = call(pack_kernel, [((80, 256), BF)], (), [pltpu.VMEM((16, 256), F32)])(held, own)
     gat = lax.all_gather(packed, "z")
-    twin = swap(gat)
-    (chosen,) = call(select_kernel, [((4, 224, 256), BF)], (0, 1), [pltpu.VMEM((128, 512), F32)])(
-        info, plane, gat, twin
-    )
+    chosen, column = call(
+        select_kernel,
+        [((4, 224, 256), BF), ((8, 256), F32)],
+        (0,),
+        [pltpu.VMEM((128, 512), F32)],
+    )(plane, gat, swap(gat))
     got = exchange(chosen, "x")
     val, cond, dens = call(
         accept_kernel,
         [((4, 112, 256), BF), ((6, 16, 256), BF), ((8, 256), F32)],
         (0,),
         [pltpu.VMEM((16, 256), F32)],
-    )(info, got)
+    )(plane, got)
     wide = exchange(val, "y")
     base, route, back = call(
         base_kernel,
         [((4, 256), F32), ((256, 128), BF), ((64, 128), BF)],
-        (0, 1),
-        [pltpu.VMEM((4, 256), F32), pltpu.VMEM((128, 256), F32)],
-    )(info, plane, dens, gat, own, bare, held)
+        (0,),
+        [
+            pltpu.VMEM((4, 256), F32),
+            pltpu.VMEM((128, 256), F32),
+            pltpu.VMEM(bare.shape, BF),
+            pltpu.SemaphoreType.DMA(()),
+        ],
+        (4,),
+    )(plane, dens, column, own, far_bare, held)
     work = [
         pltpu.VMEM((6, 8, 256), F32),
         pltpu.VMEM((6, 8, 256), F32),
@@ -500,8 +516,14 @@
         first_kernel,
         [((2, 864, 128), BF), ((32, 16, 256), BF)],
         (0,),
-        work + [pltpu.VMEM((6, 256, 128), F32)],
-    )(info, wide, cond, screened, base)
+        work
+        + [
+            pltpu.VMEM((6, 256, 128), F32),
+            pltpu.VMEM(screened.shape, BF),
+            pltpu.SemaphoreType.DMA(()),
+        ],
+        (3,),
+    )(plane, wide, cond, stay(screened), base)
     mixed = exchange(res, BLOCK)
     left = shift(op, 1)
     right = shift(op, -1)
@@ -522,12 +544,18 @@
             pltpu.VMEM((16, 128), F32),
         ],
     )(step, own, op, left, right, far)
-    (final,) = call(return_kernel, [((16, 16, 256), BF)], (), [pltpu.VMEM((16, 16, 256), F32)])(
+    (final,) = call(return_kernel, [((16, 8, 384), BF)], (), [pltpu.VMEM((16, 8, 384), F32)])(
         back, exchange(out2, PLANE)
     )
     last = exchange(final, "z")
-    (result,) = call(last_kernel, [(trial.shape, F32)], (0,))(
-        cheb, last, own, bare, held, own_x
+    (result,) = call(
+        last_kernel,
+        [(trial.shape, F32)],
+        (0,),
+        [pltpu.VMEM(bare.shape, BF), pltpu.SemaphoreType.DMA(())],
+        (3,),
+    )(
+        cheb, last, own, far_bare, held, own_x
     )
     return result
 

time: 177 us -> 172 us (0.972)
  local copies, waits for them, and re-layouts: 4.37 us -> 0.01 us
  Pallas kernels: 16.1 us -> 18.5 us
  blocking collectives: 117 us -> 115 us
    unnamed x18 -> x2, local copies, waits for them, and re-layouts: 4.37 us -> 0.01 us
    pallas_call x10, Pallas kernels: 16.1 us -> 18.5 us  [run(): pl.pallas_call(kernel, out_shape=[jax.ShapeDtypeStruct(s, d) for s, d in...]
  transfers between devices with their start and end apart: 6 -> 6, of which waited for: 4 -> 4; matrix products, arithmetic and copies ran while one was open for 0% -> 0% of each run, Pallas kernels for 1% -> 2%
where the time goes in v6:
time: 172 us; the launch traced here: 171 us
  blocking collectives  115 us (67%)
  starting transfers between devices  22.5 us (13%)
  Pallas kernels  18.5 us (11%)
  waiting for transfers between devices  14.7 us (9%)
    all_to_all x6, blocking collectives, exchange(): return lax.all_to_all(blocks, axis, 0, 0, tiled=True)  77.7 us
    all_gather x1, blocking collectives, body(): gat = lax.all_gather(packed, 'z')  37.5 us
    pallas_call x10, Pallas kernels, run(): pl.pallas_call(kernel, out_shape=[jax.ShapeDtypeStruct(s, d) for s, d in...  18.5 us
    all_to_all x2, starting transfers between devices, exchange(): return lax.all_to_all(blocks, axis, 0, 0, tiled=True)  12.2 us
    ppermute x3, waiting for transfers between devices, shift(): lax.ppermute(shard, 'y', [(k, (k + by) % count) for k in range(count)])  10.2 us
    ppermute x3, starting transfers between devices, shift(): lax.ppermute(shard, 'y', [(k, (k + by) % count) for k in range(count)])  8.31 us
    all_to_all x2, waiting for transfers between devices, exchange(): return lax.all_to_all(blocks, axis, 0, 0, tiled=True)  4.46 us
  transfers between devices with their start and end apart: 6, of which 4 were waited for; matrix products, arithmetic and copies ran while one was open for 0% of the time, Pallas kernels for 2%

profile of v6, /device:TPU:32, one launch (start us, length us, event | category | flops | bytes accessed | tf_op | source)
XLA Modules:
  0.0 170.9 jit_solution(1828436146295667984)
XLA Ops:
  0.0 1.0 shard_map.91
  1.0 10.2 %all_to_all.40.own_ref = bf16[4,2,32,256]{3,2,1,0:T(8,128)(2,1)S(1)} all-to-all(bf16[4,2,32,256]{3,2,1,0:T(8,128)(2,1)S(1)} %get-tuple-element.22), channel_id=1, replica_groups=mesh['z'=16,'x'=4,'c'=2,'y'=4] {'y'}, dimensions={0} | all-to-all | bytes 262144 | tf_op jit(solution)/shard_map/all_to_all | solution.py:20
  11.2 0.3 shard_map.92
  11.5 37.5 %all-gather = bf16[1280,256]{1,0:T(8,128)(2,1)S(1)} all-gather(bf16[80,256]{1,0:T(8,128)(2,1)S(1)} %shard_map.92), channel_id=2, replica_groups=mesh['z'=16,'x'=4,'c'=2,'y'=4] {'z'}, dimensions={0}, use_global_device_ids=true | all-gather | bytes 696320 | tf_op jit(solution)/shard_map/all_gather | solution.py:481
  49.0 1.9 %collective-permute-start = (bf16[16,80,256]{2,1,0:T(8,128)(2,1)S(1)}, bf16[16,80,256]{2,1,0:T(8,128)(2,1)S(1)}, u32[]{:S(2)}, u32[]{:S(2)}) collective-permute-start(bf16[16,80,256]{2,1,0:T(8,128)(2,1)S(1)} %bitcast.2), channel_id=1, source_target_pairs={{0,4},{4,0},{1,5},{5,1},{2,6},{6,2},{3,7},{7,3},{8,12},{12,8},{9,1... | collective-permute-start | bytes 1966088 | tf_op jit(solution)/shard_map/ppermute | solution.py:24
  50.9 9.5 %all_to_all.41.plane_ref = s32[8,1,128]{2,1,0:T(1,128)S(1)} all-to-all(s32[8,1,128]{2,1,0:T(1,128)S(1)} %get-tuple-element.20), channel_id=1, replica_groups=mesh['z'=16,'x'=4,'c'=2,'y'=4] {'x','c'}, dimensions={0} | all-to-all | bytes 8192 | tf_op jit(solution)/shard_map/all_to_all | solution.py:20
  60.4 0.0 collective-permute-done.twin_ref
  60.4 1.5 shard_map.93
  61.9 11.4 %all_to_all.42.got_ref = bf16[4,224,256]{2,1,0:T(8,128)(2,1)S(1)} all-to-all(bf16[4,224,256]{2,1,0:T(8,128)(2,1)S(1)} %get-tuple-element.23), channel_id=1, replica_groups=mesh['z'=16,'x'=4,'c'=2,'y'=4] {'x'}, dimensions={0} | all-to-all | bytes 917504 | tf_op jit(solution)/shard_map/all_to_all | solution.py:20
  73.3 1.4 shard_map.94
  74.7 3.4 %all-to-all-start.3 = ((bf16[4,112,256]{2,1,0:T(8,128)(2,1)}), bf16[4,112,256]{2,1,0:T(8,128)(2,1)S(1)}, u32[]{:S(2)}, u32[]{:S(2)}) async-start(bf16[4,112,256]{2,1,0:T(8,128)(2,1)} %get-tuple-element.28), calls=%async_computation.3 | async-start | bytes 458752 | tf_op jit(solution)/shard_map/all_to_all | solution.py:20
  78.1 3.3 %shard_map.95 = (f32[4,256]{1,0:T(4,128)S(1)}, bf16[256,128]{1,0:T(8,128)(2,1)S(1)}, bf16[64,128]{1,0:T(8,128)(2,1)S(1)}) custom-call(s32[8,1,128]{2,1,0:T(1,128)S(1)} %all_to_all.41.plane_ref, f32[8,256]{1,0:T(8,128)S(1)} %get-tuple-element.24.dens_ref, f32[8,256]{1,0:T(8,128)S(1)} %get-tuple-element.25.column_ref, ...), custom_call_target="tpu_custom_call" | custom-call | bytes 4194304 | tf_op jit(solution)/shard_map/pallas_call | solution.py:50
  81.4 3.2 %all-to-all-done.3.wide_ref = bf16[4,112,256]{2,1,0:T(8,128)(2,1)S(1)} async-done(((bf16[4,112,256]{2,1,0:T(8,128)(2,1)}), bf16[4,112,256]{2,1,0:T(8,128)(2,1)S(1)}, u32[]{:S(2)}, u32[]{:S(2)}) %all-to-all-start.3) | async-done | bytes 229408 | tf_op jit(solution)/shard_map/all_to_all | solution.py:20
  84.6 4.2 %shard_map.96 = (bf16[2,864,128]{2,1,0:T(8,128)(2,1)S(1)}, bf16[32,16,256]{2,1,0:T(8,128)(2,1)S(1)}) custom-call(s32[8,1,128]{2,1,0:T(1,128)S(1)} %all_to_all.41.plane_ref, bf16[4,112,256]{2,1,0:T(8,128)(2,1)S(1)} %all-to-all-done.3.wide_ref, bf16[6,16,256]{2,1,0:T(8,128)(2,1)S(1)} %get-tuple-element.29.cond_ref, bf16[2,1024,256]{2,1,0:T(8,128)(2,1)} %scr_hbm.1, ...), custom_call_target="tpu_custom_call" | custom-call | bytes 4194304 | tf_op jit(solution)/shard_map/pallas_call | solution.py:50
  88.8 0.0 copy-start
  88.8 2.5 %collective-permute-start.1 = (bf16[2,864,128]{2,1,0:T(8,128)(2,1)S(1)}, bf16[2,864,128]{2,1,0:T(8,128)(2,1)S(1)}, u32[]{:S(2)}, u32[]{:S(2)}) collective-permute-start(bf16[2,864,128]{2,1,0:T(8,128)(2,1)S(1)} %get-tuple-element.32.op_ref), channel_id=1, source_target_pairs={{0,1},{1,2},{2,3},{3,0},{4,5},{5,6},{6,7},{7,4},{8,9},{9,10},{10,1... | collective-permute-start | bytes 1327112 | tf_op jit(solution)/shard_map/ppermute | solution.py:29
  91.3 13.9 %all_to_all.43.got_ref = bf16[32,16,256]{2,1,0:T(8,128)(2,1)S(1)} all-to-all(bf16[32,16,256]{2,1,0:T(8,128)(2,1)S(1)} %get-tuple-element.31), channel_id=1, replica_groups=mesh['z'=16,'x'=4,'c'=2,'y'=4] {'x','c','y'}, dimensions={0} | all-to-all | bytes 524288 | tf_op jit(solution)/shard_map/all_to_all | solution.py:20
  105.2 0.8 shard_map.97
  106.0 8.9 %all-to-all-start.5 = ((bf16[16,16,256]{2,1,0:T(8,128)(2,1)}), bf16[16,16,256]{2,1,0:T(8,128)(2,1)S(1)}, u32[]{:S(2)}, u32[]{:S(2)}) async-start(bf16[16,16,256]{2,1,0:T(8,128)(2,1)} %shard_map.97), calls=%async_computation.5 | async-start | bytes 262144 | tf_op jit(solution)/shard_map/all_to_all | solution.py:20
  114.9 3.2 %collective-permute-start.2 = (bf16[2,864,128]{2,1,0:T(8,128)(2,1)S(1)}, bf16[2,864,128]{2,1,0:T(8,128)(2,1)S(1)}, u32[]{:S(2)}, u32[]{:S(2)}) collective-permute-start(bf16[2,864,128]{2,1,0:T(8,128)(2,1)S(1)} %get-tuple-element.32.op_ref), channel_id=1, source_target_pairs={{0,3},{1,0},{2,1},{3,2},{4,7},{5,4},{6,5},{7,6},{8,11},{9,8},{10,9... | collective-permute-start | bytes 1327112 | tf_op jit(solution)/shard_map/ppermute | solution.py:29
  118.0 0.0 collective-permute-done.1.left_ref
  118.1 2.7 %collective-permute-start.3 = (bf16[2,864,128]{2,1,0:T(8,128)(2,1)S(1)}, bf16[2,864,128]{2,1,0:T(8,128)(2,1)S(1)}, u32[]{:S(2)}, u32[]{:S(2)}) collective-permute-start(bf16[2,864,128]{2,1,0:T(8,128)(2,1)S(1)} %collective-permute-done.1.left_ref), channel_id=1, source_target_pairs={{0,1},{1,2},{2,3},{3,0},{4,5},{5,6},{6,7},{7,4},{8,9},{9,10},{10,1... | collective-permute-start | bytes 1327112 | tf_op jit(solution)/shard_map/ppermute | solution.py:29
  120.7 7.5 %collective-permute-done.2.right_ref = bf16[2,864,128]{2,1,0:T(8,128)(2,1)S(1)} collective-permute-done((bf16[2,864,128]{2,1,0:T(8,128)(2,1)S(1)}, bf16[2,864,128]{2,1,0:T(8,128)(2,1)S(1)}, u32[]{:S(2)}, u32[]{:S(2)}) %collective-permute-start.2) | collective-permute-done | bytes 442400 | tf_op jit(solution)/shard_map/ppermute | solution.py:29
  128.2 1.2 all-to-all-done.5.got_ref
  129.4 2.7 %collective-permute-done.3.far_ref = bf16[2,864,128]{2,1,0:T(8,128)(2,1)S(1)} collective-permute-done((bf16[2,864,128]{2,1,0:T(8,128)(2,1)S(1)}, bf16[2,864,128]{2,1,0:T(8,128)(2,1)S(1)}, u32[]{:S(2)}, u32[]{:S(2)}) %collective-permute-start.3) | collective-permute-done | bytes 442400 | tf_op jit(solution)/shard_map/ppermute | solution.py:29
  132.2 2.2 %shard_map.98 = (bf16[8,16,384]{2,1,0:T(8,128)(2,1)S(1)}, f32[4,256]{1,0:T(4,128)S(1)}) custom-call(bf16[16,16,256]{2,1,0:T(8,128)(2,1)S(1)} %all-to-all-done.5.got_ref, bf16[4,2,32,256]{3,2,1,0:T(8,128)(2,1)S(1)} %all_to_all.40.own_ref, bf16[2,864,128]{2,1,0:T(8,128)(2,1)S(1)} %get-tuple-element.32.op_ref, ...), custom_call_target="tpu_custom_call" | custom-call | bytes 4194304 | tf_op jit(solution)/shard_map/pallas_call | solution.py:50
  134.4 8.2 %all_to_all.44.got_ref = bf16[8,16,384]{2,1,0:T(8,128)(2,1)S(1)} all-to-all(bf16[8,16,384]{2,1,0:T(8,128)(2,1)S(1)} %get-tuple-element.33), channel_id=1, replica_groups=mesh['z'=16,'x'=4,'c'=2,'y'=4] {'x','c'}, dimensions={0} | all-to-all | bytes 196608 | tf_op jit(solution)/shard_map/all_to_all | solution.py:20
  142.6 0.2 shard_map.99
  142.7 24.5 %all_to_all.45.got_ref = bf16[16,8,384]{2,1,0:T(8,128)(2,1)S(1)} all-to-all(bf16[16,8,384]{2,1,0:T(8,128)(2,1)S(1)} %shard_map.99), channel_id=1, replica_groups=mesh['z'=16,'x'=4,'c'=2,'y'=4] {'z'}, dimensions={0} | all-to-all | bytes 196608 | tf_op jit(solution)/shard_map/all_to_all | solution.py:20
  167.2 0.0 copy-done
  167.2 3.7 %shard_map.100 = f32[2,2,256]{2,1,0:T(2,128)} custom-call(f32[3]{0:T(128)S(1)} %copy-done, bf16[16,8,384]{2,1,0:T(8,128)(2,1)S(1)} %all_to_all.45.got_ref, bf16[4,2,32,256]{3,2,1,0:T(8,128)(2,1)S(1)} %all_to_all.40.own_ref, bf16[1024,1024]{1,0:T(8,128)(2,1)} %bare_hbm.3, f32[8,256]{1,0:T(8,128)S(1)} %get-tuple-element.21.held_ref, ...), custom_call_target="tpu_custom_call" | custom-call | bytes 4194304 | tf_op jit(solution)/shard_map/pallas_call | solution.py:50
Async XLA Ops:
  49.0 11.4 %collective-permute-start = (bf16[16,80,256]{2,1,0:T(8,128)(2,1)S(1)}, bf16[16,80,256]{2,1,0:T(8,128)(2,1)S(1)}, u32[]{:S(2)}, u32[]{:S(2)}) collective-permute-start(bf16[16,80,256]{2,1,0:T(8,128)(2,1)S(1)} %bitcast.2), channel_id=1, source_target_pairs={{0,4},{4,0},{1,5},{5,1},{2,6},{6,2},{3,7},{7,3},{8,12},{12,8},{9,1... | collective-permute-start | bytes 1966088 | tf_op jit(solution)/shard_map/ppermute | solution.py:24
  74.7 9.9 %all-to-all-start.3 = ((bf16[4,112,256]{2,1,0:T(8,128)(2,1)}), bf16[4,112,256]{2,1,0:T(8,128)(2,1)S(1)}, u32[]{:S(2)}, u32[]{:S(2)}) async-start(bf16[4,112,256]{2,1,0:T(8,128)(2,1)} %get-tuple-element.28), calls=%async_computation.3 | async-start | bytes 458752 | tf_op jit(solution)/shard_map/all_to_all | solution.py:20
  88.8 78.4 %copy-start = (f32[3]{0:T(128)S(1)}, f32[3]{0:T(128)}, u32[]{:S(2)}) copy-start(f32[3]{0:T(128)} %cheb_ref.1) | copy-start | bytes 40
  88.8 29.2 %collective-permute-start.1 = (bf16[2,864,128]{2,1,0:T(8,128)(2,1)S(1)}, bf16[2,864,128]{2,1,0:T(8,128)(2,1)S(1)}, u32[]{:S(2)}, u32[]{:S(2)}) collective-permute-start(bf16[2,864,128]{2,1,0:T(8,128)(2,1)S(1)} %get-tuple-element.32.op_ref), channel_id=1, source_target_pairs={{0,1},{1,2},{2,3},{3,0},{4,5},{5,6},{6,7},{7,4},{8,9},{9,10},{10,1... | collective-permute-start | bytes 1327112 | tf_op jit(solution)/shard_map/ppermute | solution.py:29
  106.0 23.4 %all-to-all-start.5 = ((bf16[16,16,256]{2,1,0:T(8,128)(2,1)}), bf16[16,16,256]{2,1,0:T(8,128)(2,1)S(1)}, u32[]{:S(2)}, u32[]{:S(2)}) async-start(bf16[16,16,256]{2,1,0:T(8,128)(2,1)} %shard_map.97), calls=%async_computation.5 | async-start | bytes 262144 | tf_op jit(solution)/shard_map/all_to_all | solution.py:20
  114.9 13.3 %collective-permute-start.2 = (bf16[2,864,128]{2,1,0:T(8,128)(2,1)S(1)}, bf16[2,864,128]{2,1,0:T(8,128)(2,1)S(1)}, u32[]{:S(2)}, u32[]{:S(2)}) collective-permute-start(bf16[2,864,128]{2,1,0:T(8,128)(2,1)S(1)} %get-tuple-element.32.op_ref), channel_id=1, source_target_pairs={{0,3},{1,0},{2,1},{3,2},{4,7},{5,4},{6,5},{7,6},{8,11},{9,8},{10,9... | collective-permute-start | bytes 1327112 | tf_op jit(solution)/shard_map/ppermute | solution.py:29
  118.1 14.1 %collective-permute-start.3 = (bf16[2,864,128]{2,1,0:T(8,128)(2,1)S(1)}, bf16[2,864,128]{2,1,0:T(8,128)(2,1)S(1)}, u32[]{:S(2)}, u32[]{:S(2)}) collective-permute-start(bf16[2,864,128]{2,1,0:T(8,128)(2,1)S(1)} %collective-permute-done.1.left_ref), channel_id=1, source_target_pairs={{0,1},{1,2},{2,3},{3,0},{4,5},{5,6},{6,7},{7,4},{8,9},{9,10},{10,1... | collective-permute-start | bytes 1327112 | tf_op jit(solution)/shard_map/ppermute | solution.py:29

commit v7 on v6

--- a/solution.py
+++ b/solution.py
@@ -193,6 +193,12 @@
     out_ref[:, 192:224, :] = picked.astype(BF).reshape(4, 32, 256)
 
 
+def fetch_kernel(far_ref, near_ref, sem):
+    copy = pltpu.make_async_copy(far_ref, near_ref, sem)
+    copy.start()
+    copy.wait()
+
+
 def accept_kernel(plane_ref, got_ref, val_ref, cond_ref, dens_ref, tail_ref):
     for e in range(6):
         column = lax.rem(plane_ref[lax.axis_index(PLANE), 0, e] // 4, 4)
@@ -292,11 +298,9 @@
 
 
 def first_kernel(
-    plane_ref, wide_ref, cond_ref, scr_hbm, base_ref, op_ref, res_ref,
-    xs_ref, ys_ref, t_ref, u_ref, rs_ref, half_ref, scr_ref, sem,
+    plane_ref, wide_ref, cond_ref, scr_ref, base_ref, op_ref, res_ref,
+    xs_ref, ys_ref, t_ref, u_ref, rs_ref, half_ref,
 ):
-    copy = pltpu.make_async_copy(scr_hbm, scr_ref, sem)
-    copy.start()
     for e in range(6):
         op_ref[0, 768 + 16 * e : 784 + 16 * e, :] = cond_ref[e, :, 0:128]
         op_ref[1, 768 + 16 * e : 784 + 16 * e, :] = cond_ref[e, :, 128:256]
@@ -304,8 +308,6 @@
         tail = wide_ref[part, 96:112, :].astype(F32)
         for e in range(6):
             xs_ref[e, 2 * part : 2 * part + 2, :] = tail[2 * e : 2 * e + 2, :]
-
-    copy.wait()
 
     def one(i, carry):
         slot = plane_ref[lax.axis_index(PLANE), 0, 8 + i]
@@ -435,17 +437,12 @@
     out_ref[...] = buf_ref[...].astype(BF)
 
 
-def last_kernel(
-    cheb_ref, got_ref, own_ref, bare_hbm, held_ref, own_x_ref, out_ref, bare_ref, sem
-):
-    copy = pltpu.make_async_copy(bare_hbm, bare_ref, sem)
-    copy.start()
+def last_kernel(cheb_ref, got_ref, own_ref, bare_ref, held_ref, own_x_ref, out_ref):
     total = got_ref[0].astype(F32)
     for z in range(1, 16):
         total = total + got_ref[z].astype(F32)
     dens = [total[2 * part : 2 * part + 2, 0:256] for part in range(4)]
     rows = jnp.concatenate([total[0:4, 256:384], total[4:8, 256:384]], axis=1)
-    copy.wait()
     terms = bare_of(own_ref, bare_ref, dens)
     for s in range(2):
         x = own_x_ref[2 * s : 2 * s + 2, :]
@@ -486,6 +483,9 @@
         [pltpu.VMEM((128, 512), F32)],
     )(plane, gat, swap(gat))
     got = exchange(chosen, "x")
+    (scr,) = call(
+        fetch_kernel, [(screened.shape, BF)], (), [pltpu.SemaphoreType.DMA(())], (0,)
+    )(stay(screened))
     val, cond, dens = call(
         accept_kernel,
         [((4, 112, 256), BF), ((6, 16, 256), BF), ((8, 256), F32)],
@@ -516,14 +516,8 @@
         first_kernel,
         [((2, 864, 128), BF), ((32, 16, 256), BF)],
         (0,),
-        work
-        + [
-            pltpu.VMEM((6, 256, 128), F32),
-            pltpu.VMEM(screened.shape, BF),
-            pltpu.SemaphoreType.DMA(()),
-        ],
-        (3,),
-    )(plane, wide, cond, stay(screened), base)
+        work + [pltpu.VMEM((6, 256, 128), F32)],
+    )(plane, wide, cond, scr, base)
     mixed = exchange(res, BLOCK)
     left = shift(op, 1)
     right = shift(op, -1)
@@ -548,14 +542,11 @@
         back, exchange(out2, PLANE)
     )
     last = exchange(final, "z")
-    (result,) = call(
-        last_kernel,
-        [(trial.shape, F32)],
-        (0,),
-        [pltpu.VMEM(bare.shape, BF), pltpu.SemaphoreType.DMA(())],
-        (3,),
-    )(
-        cheb, last, own, far_bare, held, own_x
+    (near_bare,) = call(
+        fetch_kernel, [(bare.shape, BF)], (), [pltpu.SemaphoreType.DMA(())], (0,)
+    )(far_bare)
+    (result,) = call(last_kernel, [(trial.shape, F32)], (0,))(
+        cheb, last, own, near_bare, held, own_x
     )
     return result
 

time: 172 us -> 170 us (0.988)
  blocking collectives: 115 us -> 90.7 us
  starting transfers between devices: 22.5 us -> 34.5 us
  waiting for transfers between devices: 14.7 us -> 24.5 us
    all_to_all x6 -> x5, blocking collectives: 77.7 us -> 53.2 us  [exchange(): return lax.all_to_all(blocks, axis, 0, 0, tiled=True)]
    all_to_all x2 -> x3, starting transfers between devices: 12.2 us -> 24.3 us  [exchange(): return lax.all_to_all(blocks, axis, 0, 0, tiled=True)]
    all_to_all x2 -> x3, waiting for transfers between devices: 4.46 us -> 14.3 us  [exchange(): return lax.all_to_all(blocks, axis, 0, 0, tiled=True)]
    pallas_call x10 -> x12, Pallas kernels: 18.5 us -> 19.2 us  [run(): pl.pallas_call(kernel, out_shape=[jax.ShapeDtypeStruct(s, d) for s, d in...]
  transfers between devices with their start and end apart: 6 -> 7, of which waited for: 4 -> 5; matrix products, arithmetic and copies ran while one was open for 0% -> 0% of each run, Pallas kernels for 2% -> 4%
where the time goes in v7:
time: 170 us; the launch traced here: 169 us
  blocking collectives  90.7 us (53%)
  starting transfers between devices  34.5 us (20%)
  waiting for transfers between devices  24.5 us (14%)
  Pallas kernels  19.2 us (11%)
    all_to_all x5, blocking collectives, exchange(): return lax.all_to_all(blocks, axis, 0, 0, tiled=True)  53.2 us
    all_gather x1, blocking collectives, body(): gat = lax.all_gather(packed, 'z')  37.5 us
    all_to_all x3, starting transfers between devices, exchange(): return lax.all_to_all(blocks, axis, 0, 0, tiled=True)  24.3 us
    pallas_call x12, Pallas kernels, run(): pl.pallas_call(kernel, out_shape=[jax.ShapeDtypeStruct(s, d) for s, d in...  19.2 us
    all_to_all x3, waiting for transfers between devices, exchange(): return lax.all_to_all(blocks, axis, 0, 0, tiled=True)  14.3 us
    ppermute x3, waiting for transfers between devices, shift(): lax.ppermute(shard, 'y', [(k, (k + by) % count) for k in range(count)])  10.2 us
    ppermute x3, starting transfers between devices, shift(): lax.ppermute(shard, 'y', [(k, (k + by) % count) for k in range(count)])  8.31 us
  transfers between devices with their start and end apart: 7, of which 5 were waited for; matrix products, arithmetic and copies ran while one was open for 0% of the time, Pallas kernels for 4%

profile of v7, /device:TPU:32, one launch (start us, length us, event | category | flops | bytes accessed | tf_op | source)
XLA Modules:
  0.0 169.0 jit_solution(10413439545626866102)
XLA Ops:
  0.0 1.0 shard_map.91
  1.0 10.2 %all_to_all.40.own_ref = bf16[4,2,32,256]{3,2,1,0:T(8,128)(2,1)S(1)} all-to-all(bf16[4,2,32,256]{3,2,1,0:T(8,128)(2,1)S(1)} %get-tuple-element.22), channel_id=1, replica_groups=mesh['z'=16,'x'=4,'c'=2,'y'=4] {'y'}, dimensions={0} | all-to-all | bytes 262144 | tf_op jit(solution)/shard_map/all_to_all | solution.py:20
  11.2 0.3 shard_map.92
  11.5 37.5 %all-gather = bf16[1280,256]{1,0:T(8,128)(2,1)S(1)} all-gather(bf16[80,256]{1,0:T(8,128)(2,1)S(1)} %shard_map.92), channel_id=2, replica_groups=mesh['z'=16,'x'=4,'c'=2,'y'=4] {'z'}, dimensions={0}, use_global_device_ids=true | all-gather | bytes 696320 | tf_op jit(solution)/shard_map/all_gather | solution.py:478
  49.0 1.9 %collective-permute-start = (bf16[16,80,256]{2,1,0:T(8,128)(2,1)S(1)}, bf16[16,80,256]{2,1,0:T(8,128)(2,1)S(1)}, u32[]{:S(2)}, u32[]{:S(2)}) collective-permute-start(bf16[16,80,256]{2,1,0:T(8,128)(2,1)S(1)} %bitcast.2), channel_id=1, source_target_pairs={{0,4},{4,0},{1,5},{5,1},{2,6},{6,2},{3,7},{7,3},{8,12},{12,8},{9,1... | collective-permute-start | bytes 1966088 | tf_op jit(solution)/shard_map/ppermute | solution.py:24
  50.9 9.5 %all_to_all.41.plane_ref = s32[8,1,128]{2,1,0:T(1,128)S(1)} all-to-all(s32[8,1,128]{2,1,0:T(1,128)S(1)} %get-tuple-element.20), channel_id=1, replica_groups=mesh['z'=16,'x'=4,'c'=2,'y'=4] {'x','c'}, dimensions={0} | all-to-all | bytes 8192 | tf_op jit(solution)/shard_map/all_to_all | solution.py:20
  60.4 0.0 collective-permute-done.twin_ref
  60.4 1.5 shard_map.93
  61.9 11.4 %all_to_all.42.got_ref = bf16[4,224,256]{2,1,0:T(8,128)(2,1)S(1)} all-to-all(bf16[4,224,256]{2,1,0:T(8,128)(2,1)S(1)} %get-tuple-element.23), channel_id=1, replica_groups=mesh['z'=16,'x'=4,'c'=2,'y'=4] {'x'}, dimensions={0} | all-to-all | bytes 917504 | tf_op jit(solution)/shard_map/all_to_all | solution.py:20
  73.3 1.4 shard_map.94
  74.7 3.4 %all-to-all-start.3 = ((bf16[4,112,256]{2,1,0:T(8,128)(2,1)}), bf16[4,112,256]{2,1,0:T(8,128)(2,1)S(1)}, u32[]{:S(2)}, u32[]{:S(2)}) async-start(bf16[4,112,256]{2,1,0:T(8,128)(2,1)} %get-tuple-element.28), calls=%async_computation.3 | async-start | bytes 458752 | tf_op jit(solution)/shard_map/all_to_all | solution.py:20
  78.1 1.2 shard_map.96.scr_ref
  79.3 3.3 %shard_map.95 = (f32[4,256]{1,0:T(4,128)S(1)}, bf16[256,128]{1,0:T(8,128)(2,1)S(1)}, bf16[64,128]{1,0:T(8,128)(2,1)S(1)}) custom-call(s32[8,1,128]{2,1,0:T(1,128)S(1)} %all_to_all.41.plane_ref, f32[8,256]{1,0:T(8,128)S(1)} %get-tuple-element.24.dens_ref, f32[8,256]{1,0:T(8,128)S(1)} %get-tuple-element.25.column_ref, ...), custom_call_target="tpu_custom_call" | custom-call | bytes 4194304 | tf_op jit(solution)/shard_map/pallas_call | solution.py:50
  82.6 2.0 %all-to-all-done.3.wide_ref = bf16[4,112,256]{2,1,0:T(8,128)(2,1)S(1)} async-done(((bf16[4,112,256]{2,1,0:T(8,128)(2,1)}), bf16[4,112,256]{2,1,0:T(8,128)(2,1)S(1)}, u32[]{:S(2)}, u32[]{:S(2)}) %all-to-all-start.3) | async-done | bytes 229408 | tf_op jit(solution)/shard_map/all_to_all | solution.py:20
  84.6 3.0 %shard_map.97 = (bf16[2,864,128]{2,1,0:T(8,128)(2,1)S(1)}, bf16[32,16,256]{2,1,0:T(8,128)(2,1)S(1)}) custom-call(s32[8,1,128]{2,1,0:T(1,128)S(1)} %all_to_all.41.plane_ref, bf16[4,112,256]{2,1,0:T(8,128)(2,1)S(1)} %all-to-all-done.3.wide_ref, bf16[6,16,256]{2,1,0:T(8,128)(2,1)S(1)} %get-tuple-element.29.cond_ref, ...), custom_call_target="tpu_custom_call" | custom-call | bytes 4194304 | tf_op jit(solution)/shard_map/pallas_call | solution.py:50
  87.6 2.5 %collective-permute-start.1 = (bf16[2,864,128]{2,1,0:T(8,128)(2,1)S(1)}, bf16[2,864,128]{2,1,0:T(8,128)(2,1)S(1)}, u32[]{:S(2)}, u32[]{:S(2)}) collective-permute-start(bf16[2,864,128]{2,1,0:T(8,128)(2,1)S(1)} %get-tuple-element.32.op_ref), channel_id=1, source_target_pairs={{0,1},{1,2},{2,3},{3,0},{4,5},{5,6},{6,7},{7,4},{8,9},{9,10},{10,1... | collective-permute-start | bytes 1327112 | tf_op jit(solution)/shard_map/ppermute | solution.py:29
  90.1 13.9 %all_to_all.43.got_ref = bf16[32,16,256]{2,1,0:T(8,128)(2,1)S(1)} all-to-all(bf16[32,16,256]{2,1,0:T(8,128)(2,1)S(1)} %get-tuple-element.31), channel_id=1, replica_groups=mesh['z'=16,'x'=4,'c'=2,'y'=4] {'x','c','y'}, dimensions={0} | all-to-all | bytes 524288 | tf_op jit(solution)/shard_map/all_to_all | solution.py:20
  104.0 0.8 shard_map.98
  104.8 8.9 %all-to-all-start.5 = ((bf16[16,16,256]{2,1,0:T(8,128)(2,1)}), bf16[16,16,256]{2,1,0:T(8,128)(2,1)S(1)}, u32[]{:S(2)}, u32[]{:S(2)}) async-start(bf16[16,16,256]{2,1,0:T(8,128)(2,1)} %shard_map.98), calls=%async_computation.5 | async-start | bytes 262144 | tf_op jit(solution)/shard_map/all_to_all | solution.py:20
  113.7 3.2 %collective-permute-start.2 = (bf16[2,864,128]{2,1,0:T(8,128)(2,1)S(1)}, bf16[2,864,128]{2,1,0:T(8,128)(2,1)S(1)}, u32[]{:S(2)}, u32[]{:S(2)}) collective-permute-start(bf16[2,864,128]{2,1,0:T(8,128)(2,1)S(1)} %get-tuple-element.32.op_ref), channel_id=1, source_target_pairs={{0,3},{1,0},{2,1},{3,2},{4,7},{5,4},{6,5},{7,6},{8,11},{9,8},{10,9... | collective-permute-start | bytes 1327112 | tf_op jit(solution)/shard_map/ppermute | solution.py:29
  116.8 0.0 collective-permute-done.1.left_ref
  116.9 2.7 %collective-permute-start.3 = (bf16[2,864,128]{2,1,0:T(8,128)(2,1)S(1)}, bf16[2,864,128]{2,1,0:T(8,128)(2,1)S(1)}, u32[]{:S(2)}, u32[]{:S(2)}) collective-permute-start(bf16[2,864,128]{2,1,0:T(8,128)(2,1)S(1)} %collective-permute-done.1.left_ref), channel_id=1, source_target_pairs={{0,1},{1,2},{2,3},{3,0},{4,5},{5,6},{6,7},{7,4},{8,9},{9,10},{10,1... | collective-permute-start | bytes 1327112 | tf_op jit(solution)/shard_map/ppermute | solution.py:29
  119.5 7.5 %collective-permute-done.2.right_ref = bf16[2,864,128]{2,1,0:T(8,128)(2,1)S(1)} collective-permute-done((bf16[2,864,128]{2,1,0:T(8,128)(2,1)S(1)}, bf16[2,864,128]{2,1,0:T(8,128)(2,1)S(1)}, u32[]{:S(2)}, u32[]{:S(2)}) %collective-permute-start.2) | collective-permute-done | bytes 442400 | tf_op jit(solution)/shard_map/ppermute | solution.py:29
  127.0 1.3 all-to-all-done.5.got_ref
  128.3 2.7 %collective-permute-done.3.far_ref = bf16[2,864,128]{2,1,0:T(8,128)(2,1)S(1)} collective-permute-done((bf16[2,864,128]{2,1,0:T(8,128)(2,1)S(1)}, bf16[2,864,128]{2,1,0:T(8,128)(2,1)S(1)}, u32[]{:S(2)}, u32[]{:S(2)}) %collective-permute-start.3) | collective-permute-done | bytes 442400 | tf_op jit(solution)/shard_map/ppermute | solution.py:29
  131.0 2.2 %shard_map.99 = (bf16[8,16,384]{2,1,0:T(8,128)(2,1)S(1)}, f32[4,256]{1,0:T(4,128)S(1)}) custom-call(bf16[16,16,256]{2,1,0:T(8,128)(2,1)S(1)} %all-to-all-done.5.got_ref, bf16[4,2,32,256]{3,2,1,0:T(8,128)(2,1)S(1)} %all_to_all.40.own_ref, bf16[2,864,128]{2,1,0:T(8,128)(2,1)S(1)} %get-tuple-element.32.op_ref, ...), custom_call_target="tpu_custom_call" | custom-call | bytes 4194304 | tf_op jit(solution)/shard_map/pallas_call | solution.py:50
  133.2 8.2 %all_to_all.44.got_ref = bf16[8,16,384]{2,1,0:T(8,128)(2,1)S(1)} all-to-all(bf16[8,16,384]{2,1,0:T(8,128)(2,1)S(1)} %get-tuple-element.33), channel_id=1, replica_groups=mesh['z'=16,'x'=4,'c'=2,'y'=4] {'x','c'}, dimensions={0} | all-to-all | bytes 196608 | tf_op jit(solution)/shard_map/all_to_all | solution.py:20
  141.4 0.8 shard_map.100
  142.2 12.0 %all-to-all-start.7 = ((bf16[16,8,384]{2,1,0:T(8,128)(2,1)}), bf16[16,8,384]{2,1,0:T(8,128)(2,1)S(1)}, u32[]{:S(2)}, u32[]{:S(2)}) async-start(bf16[16,8,384]{2,1,0:T(8,128)(2,1)} %shard_map.100), calls=%async_computation.7 | async-start | bytes 196608 | tf_op jit(solution)/shard_map/all_to_all | solution.py:20
  154.2 0.0 copy-start
  154.2 1.6 shard_map.101.bare_ref
  155.8 11.1 %all-to-all-done.7.got_ref = bf16[16,8,384]{2,1,0:T(8,128)(2,1)S(1)} async-done(((bf16[16,8,384]{2,1,0:T(8,128)(2,1)}), bf16[16,8,384]{2,1,0:T(8,128)(2,1)S(1)}, u32[]{:S(2)}, u32[]{:S(2)}) %all-to-all-start.7) | async-done | bytes 98336 | tf_op jit(solution)/shard_map/all_to_all | solution.py:20
  166.9 0.0 copy-done
  166.9 2.1 %shard_map.102 = f32[2,2,256]{2,1,0:T(2,128)} custom-call(f32[3]{0:T(128)S(1)} %copy-done, bf16[16,8,384]{2,1,0:T(8,128)(2,1)S(1)} %all-to-all-done.7.got_ref, bf16[4,2,32,256]{3,2,1,0:T(8,128)(2,1)S(1)} %all_to_all.40.own_ref, bf16[1024,1024]{1,0:T(8,128)(2,1)S(1)} %shard_map.101.bare_ref, f32[8,256]{1,0:T(8,128)S(1)} %get-tuple-element.21.held_ref, ...), custom_call_target="tpu_custom_call" | custom-call | bytes 4194304 | tf_op jit(solution)/shard_map/pallas_call | solution.py:50
Async XLA Ops:
  49.0 11.4 %collective-permute-start = (bf16[16,80,256]{2,1,0:T(8,128)(2,1)S(1)}, bf16[16,80,256]{2,1,0:T(8,128)(2,1)S(1)}, u32[]{:S(2)}, u32[]{:S(2)}) collective-permute-start(bf16[16,80,256]{2,1,0:T(8,128)(2,1)S(1)} %bitcast.2), channel_id=1, source_target_pairs={{0,4},{4,0},{1,5},{5,1},{2,6},{6,2},{3,7},{7,3},{8,12},{12,8},{9,1... | collective-permute-start | bytes 1966088 | tf_op jit(solution)/shard_map/ppermute | solution.py:24
  74.7 9.9 %all-to-all-start.3 = ((bf16[4,112,256]{2,1,0:T(8,128)(2,1)}), bf16[4,112,256]{2,1,0:T(8,128)(2,1)S(1)}, u32[]{:S(2)}, u32[]{:S(2)}) async-start(bf16[4,112,256]{2,1,0:T(8,128)(2,1)} %get-tuple-element.28), calls=%async_computation.3 | async-start | bytes 458752 | tf_op jit(solution)/shard_map/all_to_all | solution.py:20
  87.6 29.2 %collective-permute-start.1 = (bf16[2,864,128]{2,1,0:T(8,128)(2,1)S(1)}, bf16[2,864,128]{2,1,0:T(8,128)(2,1)S(1)}, u32[]{:S(2)}, u32[]{:S(2)}) collective-permute-start(bf16[2,864,128]{2,1,0:T(8,128)(2,1)S(1)} %get-tuple-element.32.op_ref), channel_id=1, source_target_pairs={{0,1},{1,2},{2,3},{3,0},{4,5},{5,6},{6,7},{7,4},{8,9},{9,10},{10,1... | collective-permute-start | bytes 1327112 | tf_op jit(solution)/shard_map/ppermute | solution.py:29
  104.8 23.4 %all-to-all-start.5 = ((bf16[16,16,256]{2,1,0:T(8,128)(2,1)}), bf16[16,16,256]{2,1,0:T(8,128)(2,1)S(1)}, u32[]{:S(2)}, u32[]{:S(2)}) async-start(bf16[16,16,256]{2,1,0:T(8,128)(2,1)} %shard_map.98), calls=%async_computation.5 | async-start | bytes 262144 | tf_op jit(solution)/shard_map/all_to_all | solution.py:20
  113.7 13.3 %collective-permute-start.2 = (bf16[2,864,128]{2,1,0:T(8,128)(2,1)S(1)}, bf16[2,864,128]{2,1,0:T(8,128)(2,1)S(1)}, u32[]{:S(2)}, u32[]{:S(2)}) collective-permute-start(bf16[2,864,128]{2,1,0:T(8,128)(2,1)S(1)} %get-tuple-element.32.op_ref), channel_id=1, source_target_pairs={{0,3},{1,0},{2,1},{3,2},{4,7},{5,4},{6,5},{7,6},{8,11},{9,8},{10,9... | collective-permute-start | bytes 1327112 | tf_op jit(solution)/shard_map/ppermute | solution.py:29
  116.9 14.1 %collective-permute-start.3 = (bf16[2,864,128]{2,1,0:T(8,128)(2,1)S(1)}, bf16[2,864,128]{2,1,0:T(8,128)(2,1)S(1)}, u32[]{:S(2)}, u32[]{:S(2)}) collective-permute-start(bf16[2,864,128]{2,1,0:T(8,128)(2,1)S(1)} %collective-permute-done.1.left_ref), channel_id=1, source_target_pairs={{0,1},{1,2},{2,3},{3,0},{4,5},{5,6},{6,7},{7,4},{8,9},{9,10},{10,1... | collective-permute-start | bytes 1327112 | tf_op jit(solution)/shard_map/ppermute | solution.py:29
  142.2 24.7 %all-to-all-start.7 = ((bf16[16,8,384]{2,1,0:T(8,128)(2,1)}), bf16[16,8,384]{2,1,0:T(8,128)(2,1)S(1)}, u32[]{:S(2)}, u32[]{:S(2)}) async-start(bf16[16,8,384]{2,1,0:T(8,128)(2,1)} %shard_map.100), calls=%async_computation.7 | async-start | bytes 196608 | tf_op jit(solution)/shard_map/all_to_all | solution.py:20
  154.2 12.7 %copy-start = (f32[3]{0:T(128)S(1)}, f32[3]{0:T(128)}, u32[]{:S(2)}) copy-start(f32[3]{0:T(128)} %cheb_ref.1) | copy-start | bytes 40

commit v8 on v7

--- a/solution.py
+++ b/solution.py
@@ -102,14 +102,24 @@
     return terms
 
 
+def copies_kernel(orb_hbm, own_ref, sem):
+    copies = [
+        pltpu.make_async_copy(orb_hbm, own_ref.at[part], sem.at[part]) for part in range(4)
+    ]
+    for copy in copies:
+        copy.start()
+    for copy in copies:
+        copy.wait()
+
+
 def info_kernel(
-    pair_hbm, slot_hbm, order_hbm, orb_hbm, trial_hbm, trans_hbm,
-    ids_ref, own_ref, held_ref, pair_ref, slot_ref, order_ref, trial_ref, trans_ref, sem,
+    pair_hbm, slot_hbm, order_hbm, trial_hbm, trans_hbm,
+    ids_ref, held_ref, pair_ref, slot_ref, order_ref, trial_ref, trans_ref, sem,
 ):
     moves = [
         (pair_hbm, pair_ref), (slot_hbm, slot_ref), (order_hbm, order_ref),
         (trial_hbm, trial_ref), (trans_hbm, trans_ref),
-    ] + [(orb_hbm, own_ref.at[part]) for part in range(4)]
+    ]
     copies = [pltpu.make_async_copy(a, b, sem.at[k]) for k, (a, b) in enumerate(moves)]
     for copy in copies:
         copy.start()
@@ -457,9 +467,14 @@
 
 
 def body(orbitals, transition, trial, screened, bare, cheb, pair_k, pair_slot, k_order):
-    ids, copies, held = call(
+    (copies,) = call(
+        copies_kernel, [((4, 2, 32, 256), BF)], (), [pltpu.SemaphoreType.DMA((4,))], (0,)
+    )(stay(orbitals))
+    far_bare = stay(bare)
+    own = exchange(copies, "y")
+    ids, held = call(
         info_kernel,
-        [((8, 1, 128), jnp.int32), ((4, 2, 32, 256), BF), ((8, 256), F32)],
+        [((8, 1, 128), jnp.int32), ((8, 256), F32)],
         (),
         [
             pltpu.SMEM((3,), jnp.int32),
@@ -467,21 +482,20 @@
             pltpu.VMEM((1, 256), jnp.int32),
             pltpu.VMEM((2, 2, 256), F32),
             pltpu.VMEM((2, 256), F32),
-            pltpu.SemaphoreType.DMA((9,)),
+            pltpu.SemaphoreType.DMA((5,)),
         ],
-        range(6),
-    )(*map(stay, (pair_k, pair_slot, k_order.reshape(1, -1), orbitals, trial, transition)))
-    far_bare = stay(bare)
-    own = exchange(copies, "y")
+        range(5),
+    )(*map(stay, (pair_k, pair_slot, k_order.reshape(1, -1), trial, transition)))
     plane = exchange(ids, PLANE)
     (packed,) = call(pack_kernel, [((80, 256), BF)], (), [pltpu.VMEM((16, 256), F32)])(held, own)
     gat = lax.all_gather(packed, "z")
+    twin = swap(gat)
     chosen, column = call(
         select_kernel,
         [((4, 224, 256), BF), ((8, 256), F32)],
         (0,),
         [pltpu.VMEM((128, 512), F32)],
-    )(plane, gat, swap(gat))
+    )(plane, gat, twin)
     got = exchange(chosen, "x")
     (scr,) = call(
         fetch_kernel, [(screened.shape, BF)], (), [pltpu.SemaphoreType.DMA(())], (0,)

time: 170 us -> 171 us (level)
  blocking collectives: 90.7 us -> 80.4 us
  waiting for transfers between devices: 24.5 us -> 29.6 us
  starting transfers between devices: 34.5 us -> 39 us
    all_to_all x5 -> x4, blocking collectives: 53.2 us -> 43 us  [exchange(): return lax.all_to_all(blocks, axis, 0, 0, tiled=True)]
    all_to_all x3 -> x4, waiting for transfers between devices: 14.3 us -> 19.4 us  [exchange(): return lax.all_to_all(blocks, axis, 0, 0, tiled=True)]
    all_to_all x3 -> x4, starting transfers between devices: 24.3 us -> 28.7 us  [exchange(): return lax.all_to_all(blocks, axis, 0, 0, tiled=True)]
    pallas_call x12 -> x13, Pallas kernels: 19.2 us -> 20.7 us  [run(): pl.pallas_call(kernel, out_shape=[jax.ShapeDtypeStruct(s, d) for s, d in...]
  transfers between devices with their start and end apart: 7 -> 8, of which waited for: 5 -> 6; matrix products, arithmetic and copies ran while one was open for 0% -> 0% of each run, Pallas kernels for 4% -> 5%
where the time goes in v8:
time: 171 us; the launch traced here: 170 us
  blocking collectives  80.4 us (47%)
  starting transfers between devices  39 us (23%)
  waiting for transfers between devices  29.6 us (17%)
  Pallas kernels  20.7 us (12%)
    all_to_all x4, blocking collectives, exchange(): return lax.all_to_all(blocks, axis, 0, 0, tiled=True)  43 us
    all_gather x1, blocking collectives, body(): gat = lax.all_gather(packed, 'z')  37.5 us
    all_to_all x4, starting transfers between devices, exchange(): return lax.all_to_all(blocks, axis, 0, 0, tiled=True)  28.7 us
    pallas_call x13, Pallas kernels, run(): pl.pallas_call(kernel, out_shape=[jax.ShapeDtypeStruct(s, d) for s, d in...  20.7 us
    all_to_all x4, waiting for transfers between devices, exchange(): return lax.all_to_all(blocks, axis, 0, 0, tiled=True)  19.4 us
    ppermute x3, waiting for transfers between devices, shift(): lax.ppermute(shard, 'y', [(k, (k + by) % count) for k in range(count)])  10.2 us
    ppermute x3, starting transfers between devices, shift(): lax.ppermute(shard, 'y', [(k, (k + by) % count) for k in range(count)])  8.31 us
  transfers between devices with their start and end apart: 8, of which 6 were waited for; matrix products, arithmetic and copies ran while one was open for 0% of the time, Pallas kernels for 5%

profile of v8, /device:TPU:32, one launch (start us, length us, event | category | flops | bytes accessed | tf_op | source)
XLA Modules:
  0.0 169.8 jit_solution(12521487494986121683)
XLA Ops:
  0.0 1.6 shard_map.92
  1.6 4.5 %all-to-all-start.1 = ((bf16[4,2,32,256]{3,2,1,0:T(8,128)(2,1)}), bf16[4,2,32,256]{3,2,1,0:T(8,128)(2,1)S(1)}, u32[]{:S(2)}, u32[]{:S(2)}) async-start(bf16[4,2,32,256]{3,2,1,0:T(8,128)(2,1)} %shard_map.92), calls=%async_computation.1 | async-start | bytes 262144 | tf_op jit(solution)/shard_map/all_to_all | solution.py:20
  6.1 0.9 shard_map.91
  7.0 5.1 %all-to-all-done.1.own_ref = bf16[4,2,32,256]{3,2,1,0:T(8,128)(2,1)S(1)} async-done(((bf16[4,2,32,256]{3,2,1,0:T(8,128)(2,1)}), bf16[4,2,32,256]{3,2,1,0:T(8,128)(2,1)S(1)}, u32[]{:S(2)}, u32[]{:S(2)}) %all-to-all-start.1) | async-done | bytes 131104 | tf_op jit(solution)/shard_map/all_to_all | solution.py:20
  12.1 0.3 shard_map.93
  12.3 37.5 %all-gather = bf16[1280,256]{1,0:T(8,128)(2,1)S(1)} all-gather(bf16[80,256]{1,0:T(8,128)(2,1)S(1)} %shard_map.93), channel_id=2, replica_groups=mesh['z'=16,'x'=4,'c'=2,'y'=4] {'z'}, dimensions={0}, use_global_device_ids=true | all-gather | bytes 696320 | tf_op jit(solution)/shard_map/all_gather | solution.py:491
  49.8 1.9 %collective-permute-start = (bf16[16,80,256]{2,1,0:T(8,128)(2,1)S(1)}, bf16[16,80,256]{2,1,0:T(8,128)(2,1)S(1)}, u32[]{:S(2)}, u32[]{:S(2)}) collective-permute-start(bf16[16,80,256]{2,1,0:T(8,128)(2,1)S(1)} %bitcast.2), channel_id=1, source_target_pairs={{0,4},{4,0},{1,5},{5,1},{2,6},{6,2},{3,7},{7,3},{8,12},{12,8},{9,1... | collective-permute-start | bytes 1966088 | tf_op jit(solution)/shard_map/ppermute | solution.py:24
  51.7 9.5 %all_to_all.40.plane_ref = s32[8,1,128]{2,1,0:T(1,128)S(1)} all-to-all(s32[8,1,128]{2,1,0:T(1,128)S(1)} %get-tuple-element.19), channel_id=1, replica_groups=mesh['z'=16,'x'=4,'c'=2,'y'=4] {'x','c'}, dimensions={0} | all-to-all | bytes 8192 | tf_op jit(solution)/shard_map/all_to_all | solution.py:20
  61.2 0.0 collective-permute-done.twin_ref
  61.2 1.5 shard_map.94
  62.8 11.4 %all_to_all.41.got_ref = bf16[4,224,256]{2,1,0:T(8,128)(2,1)S(1)} all-to-all(bf16[4,224,256]{2,1,0:T(8,128)(2,1)S(1)} %get-tuple-element.21), channel_id=1, replica_groups=mesh['z'=16,'x'=4,'c'=2,'y'=4] {'x'}, dimensions={0} | all-to-all | bytes 917504 | tf_op jit(solution)/shard_map/all_to_all | solution.py:20
  74.2 1.4 shard_map.95
  75.5 3.4 %all-to-all-start.3 = ((bf16[4,112,256]{2,1,0:T(8,128)(2,1)}), bf16[4,112,256]{2,1,0:T(8,128)(2,1)S(1)}, u32[]{:S(2)}, u32[]{:S(2)}) async-start(bf16[4,112,256]{2,1,0:T(8,128)(2,1)} %get-tuple-element.26), calls=%async_computation.3 | async-start | bytes 458752 | tf_op jit(solution)/shard_map/all_to_all | solution.py:20
  78.9 1.2 shard_map.97.scr_ref
  80.2 3.3 %shard_map.96 = (f32[4,256]{1,0:T(4,128)S(1)}, bf16[256,128]{1,0:T(8,128)(2,1)S(1)}, bf16[64,128]{1,0:T(8,128)(2,1)S(1)}) custom-call(s32[8,1,128]{2,1,0:T(1,128)S(1)} %all_to_all.40.plane_ref, f32[8,256]{1,0:T(8,128)S(1)} %get-tuple-element.22.dens_ref, f32[8,256]{1,0:T(8,128)S(1)} %get-tuple-element.23.column_ref, ...), custom_call_target="tpu_custom_call" | custom-call | bytes 4194304 | tf_op jit(solution)/shard_map/pallas_call | solution.py:50
  83.4 2.0 %all-to-all-done.3.wide_ref = bf16[4,112,256]{2,1,0:T(8,128)(2,1)S(1)} async-done(((bf16[4,112,256]{2,1,0:T(8,128)(2,1)}), bf16[4,112,256]{2,1,0:T(8,128)(2,1)S(1)}, u32[]{:S(2)}, u32[]{:S(2)}) %all-to-all-start.3) | async-done | bytes 229408 | tf_op jit(solution)/shard_map/all_to_all | solution.py:20
  85.4 3.0 %shard_map.98 = (bf16[2,864,128]{2,1,0:T(8,128)(2,1)S(1)}, bf16[32,16,256]{2,1,0:T(8,128)(2,1)S(1)}) custom-call(s32[8,1,128]{2,1,0:T(1,128)S(1)} %all_to_all.40.plane_ref, bf16[4,112,256]{2,1,0:T(8,128)(2,1)S(1)} %all-to-all-done.3.wide_ref, bf16[6,16,256]{2,1,0:T(8,128)(2,1)S(1)} %get-tuple-element.27.cond_ref, ...), custom_call_target="tpu_custom_call" | custom-call | bytes 4194304 | tf_op jit(solution)/shard_map/pallas_call | solution.py:50
  88.4 2.5 %collective-permute-start.1 = (bf16[2,864,128]{2,1,0:T(8,128)(2,1)S(1)}, bf16[2,864,128]{2,1,0:T(8,128)(2,1)S(1)}, u32[]{:S(2)}, u32[]{:S(2)}) collective-permute-start(bf16[2,864,128]{2,1,0:T(8,128)(2,1)S(1)} %get-tuple-element.30.op_ref), channel_id=1, source_target_pairs={{0,1},{1,2},{2,3},{3,0},{4,5},{5,6},{6,7},{7,4},{8,9},{9,10},{10,1... | collective-permute-start | bytes 1327112 | tf_op jit(solution)/shard_map/ppermute | solution.py:29
  90.9 13.9 %all_to_all.42.got_ref = bf16[32,16,256]{2,1,0:T(8,128)(2,1)S(1)} all-to-all(bf16[32,16,256]{2,1,0:T(8,128)(2,1)S(1)} %get-tuple-element.29), channel_id=1, replica_groups=mesh['z'=16,'x'=4,'c'=2,'y'=4] {'x','c','y'}, dimensions={0} | all-to-all | bytes 524288 | tf_op jit(solution)/shard_map/all_to_all | solution.py:20
  104.8 0.9 shard_map.99
  105.6 8.9 %all-to-all-start.5 = ((bf16[16,16,256]{2,1,0:T(8,128)(2,1)}), bf16[16,16,256]{2,1,0:T(8,128)(2,1)S(1)}, u32[]{:S(2)}, u32[]{:S(2)}) async-start(bf16[16,16,256]{2,1,0:T(8,128)(2,1)} %shard_map.99), calls=%async_computation.5 | async-start | bytes 262144 | tf_op jit(solution)/shard_map/all_to_all | solution.py:20
  114.5 3.2 %collective-permute-start.2 = (bf16[2,864,128]{2,1,0:T(8,128)(2,1)S(1)}, bf16[2,864,128]{2,1,0:T(8,128)(2,1)S(1)}, u32[]{:S(2)}, u32[]{:S(2)}) collective-permute-start(bf16[2,864,128]{2,1,0:T(8,128)(2,1)S(1)} %get-tuple-element.30.op_ref), channel_id=1, source_target_pairs={{0,3},{1,0},{2,1},{3,2},{4,7},{5,4},{6,5},{7,6},{8,11},{9,8},{10,9... | collective-permute-start | bytes 1327112 | tf_op jit(solution)/shard_map/ppermute | solution.py:29
  117.7 0.0 collective-permute-done.1.left_ref
  117.7 2.7 %collective-permute-start.3 = (bf16[2,864,128]{2,1,0:T(8,128)(2,1)S(1)}, bf16[2,864,128]{2,1,0:T(8,128)(2,1)S(1)}, u32[]{:S(2)}, u32[]{:S(2)}) collective-permute-start(bf16[2,864,128]{2,1,0:T(8,128)(2,1)S(1)} %collective-permute-done.1.left_ref), channel_id=1, source_target_pairs={{0,1},{1,2},{2,3},{3,0},{4,5},{5,6},{6,7},{7,4},{8,9},{9,10},{10,1... | collective-permute-start | bytes 1327112 | tf_op jit(solution)/shard_map/ppermute | solution.py:29
  120.4 7.5 %collective-permute-done.2.right_ref = bf16[2,864,128]{2,1,0:T(8,128)(2,1)S(1)} collective-permute-done((bf16[2,864,128]{2,1,0:T(8,128)(2,1)S(1)}, bf16[2,864,128]{2,1,0:T(8,128)(2,1)S(1)}, u32[]{:S(2)}, u32[]{:S(2)}) %collective-permute-start.2) | collective-permute-done | bytes 442400 | tf_op jit(solution)/shard_map/ppermute | solution.py:29
  127.8 1.2 all-to-all-done.5.got_ref
  129.1 2.7 %collective-permute-done.3.far_ref = bf16[2,864,128]{2,1,0:T(8,128)(2,1)S(1)} collective-permute-done((bf16[2,864,128]{2,1,0:T(8,128)(2,1)S(1)}, bf16[2,864,128]{2,1,0:T(8,128)(2,1)S(1)}, u32[]{:S(2)}, u32[]{:S(2)}) %collective-permute-start.3) | collective-permute-done | bytes 442400 | tf_op jit(solution)/shard_map/ppermute | solution.py:29
  131.8 2.2 %shard_map.100 = (bf16[8,16,384]{2,1,0:T(8,128)(2,1)S(1)}, f32[4,256]{1,0:T(4,128)S(1)}) custom-call(bf16[16,16,256]{2,1,0:T(8,128)(2,1)S(1)} %all-to-all-done.5.got_ref, bf16[4,2,32,256]{3,2,1,0:T(8,128)(2,1)S(1)} %all-to-all-done.1.own_ref, bf16[2,864,128]{2,1,0:T(8,128)(2,1)S(1)} %get-tuple-element.30.op_ref, ...), custom_call_target="tpu_custom_call" | custom-call | bytes 4194304 | tf_op jit(solution)/shard_map/pallas_call | solution.py:50
  134.0 8.2 %all_to_all.43.got_ref = bf16[8,16,384]{2,1,0:T(8,128)(2,1)S(1)} all-to-all(bf16[8,16,384]{2,1,0:T(8,128)(2,1)S(1)} %get-tuple-element.31), channel_id=1, replica_groups=mesh['z'=16,'x'=4,'c'=2,'y'=4] {'x','c'}, dimensions={0} | all-to-all | bytes 196608 | tf_op jit(solution)/shard_map/all_to_all | solution.py:20
  142.2 0.8 shard_map.101
  143.0 12.0 %all-to-all-start.7 = ((bf16[16,8,384]{2,1,0:T(8,128)(2,1)}), bf16[16,8,384]{2,1,0:T(8,128)(2,1)S(1)}, u32[]{:S(2)}, u32[]{:S(2)}) async-start(bf16[16,8,384]{2,1,0:T(8,128)(2,1)} %shard_map.101), calls=%async_computation.7 | async-start | bytes 196608 | tf_op jit(solution)/shard_map/all_to_all | solution.py:20
  155.0 0.0 copy-start
  155.0 1.6 shard_map.102.bare_ref
  156.6 11.1 %all-to-all-done.7.got_ref = bf16[16,8,384]{2,1,0:T(8,128)(2,1)S(1)} async-done(((bf16[16,8,384]{2,1,0:T(8,128)(2,1)}), bf16[16,8,384]{2,1,0:T(8,128)(2,1)S(1)}, u32[]{:S(2)}, u32[]{:S(2)}) %all-to-all-start.7) | async-done | bytes 98336 | tf_op jit(solution)/shard_map/all_to_all | solution.py:20
  167.7 0.0 copy-done
  167.7 2.1 %shard_map.103 = f32[2,2,256]{2,1,0:T(2,128)} custom-call(f32[3]{0:T(128)S(1)} %copy-done, bf16[16,8,384]{2,1,0:T(8,128)(2,1)S(1)} %all-to-all-done.7.got_ref, bf16[4,2,32,256]{3,2,1,0:T(8,128)(2,1)S(1)} %all-to-all-done.1.own_ref, bf16[1024,1024]{1,0:T(8,128)(2,1)S(1)} %shard_map.102.bare_ref, f32[8,256]{1,0:T(8,128)S(1)} %get-tuple-element.20.held_ref, ...), custom_call_target="tpu_custom_call" | custom-call | bytes 4194304 | tf_op jit(solution)/shard_map/pallas_call | solution.py:50
Async XLA Ops:
  1.6 10.5 %all-to-all-start.1 = ((bf16[4,2,32,256]{3,2,1,0:T(8,128)(2,1)}), bf16[4,2,32,256]{3,2,1,0:T(8,128)(2,1)S(1)}, u32[]{:S(2)}, u32[]{:S(2)}) async-start(bf16[4,2,32,256]{3,2,1,0:T(8,128)(2,1)} %shard_map.92), calls=%async_computation.1 | async-start | bytes 262144 | tf_op jit(solution)/shard_map/all_to_all | solution.py:20
  49.8 11.4 %collective-permute-start = (bf16[16,80,256]{2,1,0:T(8,128)(2,1)S(1)}, bf16[16,80,256]{2,1,0:T(8,128)(2,1)S(1)}, u32[]{:S(2)}, u32[]{:S(2)}) collective-permute-start(bf16[16,80,256]{2,1,0:T(8,128)(2,1)S(1)} %bitcast.2), channel_id=1, source_target_pairs={{0,4},{4,0},{1,5},{5,1},{2,6},{6,2},{3,7},{7,3},{8,12},{12,8},{9,1... | collective-permute-start | bytes 1966088 | tf_op jit(solution)/shard_map/ppermute | solution.py:24
  75.5 9.9 %all-to-all-start.3 = ((bf16[4,112,256]{2,1,0:T(8,128)(2,1)}), bf16[4,112,256]{2,1,0:T(8,128)(2,1)S(1)}, u32[]{:S(2)}, u32[]{:S(2)}) async-start(bf16[4,112,256]{2,1,0:T(8,128)(2,1)} %get-tuple-element.26), calls=%async_computation.3 | async-start | bytes 458752 | tf_op jit(solution)/shard_map/all_to_all | solution.py:20
  88.4 29.3 %collective-permute-start.1 = (bf16[2,864,128]{2,1,0:T(8,128)(2,1)S(1)}, bf16[2,864,128]{2,1,0:T(8,128)(2,1)S(1)}, u32[]{:S(2)}, u32[]{:S(2)}) collective-permute-start(bf16[2,864,128]{2,1,0:T(8,128)(2,1)S(1)} %get-tuple-element.30.op_ref), channel_id=1, source_target_pairs={{0,1},{1,2},{2,3},{3,0},{4,5},{5,6},{6,7},{7,4},{8,9},{9,10},{10,1... | collective-permute-start | bytes 1327112 | tf_op jit(solution)/shard_map/ppermute | solution.py:29
  105.6 23.4 %all-to-all-start.5 = ((bf16[16,16,256]{2,1,0:T(8,128)(2,1)}), bf16[16,16,256]{2,1,0:T(8,128)(2,1)S(1)}, u32[]{:S(2)}, u32[]{:S(2)}) async-start(bf16[16,16,256]{2,1,0:T(8,128)(2,1)} %shard_map.99), calls=%async_computation.5 | async-start | bytes 262144 | tf_op jit(solution)/shard_map/all_to_all | solution.py:20
  114.5 13.3 %collective-permute-start.2 = (bf16[2,864,128]{2,1,0:T(8,128)(2,1)S(1)}, bf16[2,864,128]{2,1,0:T(8,128)(2,1)S(1)}, u32[]{:S(2)}, u32[]{:S(2)}) collective-permute-start(bf16[2,864,128]{2,1,0:T(8,128)(2,1)S(1)} %get-tuple-element.30.op_ref), channel_id=1, source_target_pairs={{0,3},{1,0},{2,1},{3,2},{4,7},{5,4},{6,5},{7,6},{8,11},{9,8},{10,9... | collective-permute-start | bytes 1327112 | tf_op jit(solution)/shard_map/ppermute | solution.py:29
  117.7 14.1 %collective-permute-start.3 = (bf16[2,864,128]{2,1,0:T(8,128)(2,1)S(1)}, bf16[2,864,128]{2,1,0:T(8,128)(2,1)S(1)}, u32[]{:S(2)}, u32[]{:S(2)}) collective-permute-start(bf16[2,864,128]{2,1,0:T(8,128)(2,1)S(1)} %collective-permute-done.1.left_ref), channel_id=1, source_target_pairs={{0,1},{1,2},{2,3},{3,0},{4,5},{5,6},{6,7},{7,4},{8,9},{9,10},{10,1... | collective-permute-start | bytes 1327112 | tf_op jit(solution)/shard_map/ppermute | solution.py:29
  143.0 24.7 %all-to-all-start.7 = ((bf16[16,8,384]{2,1,0:T(8,128)(2,1)}), bf16[16,8,384]{2,1,0:T(8,128)(2,1)S(1)}, u32[]{:S(2)}, u32[]{:S(2)}) async-start(bf16[16,8,384]{2,1,0:T(8,128)(2,1)} %shard_map.101), calls=%async_computation.7 | async-start | bytes 196608 | tf_op jit(solution)/shard_map/all_to_all | solution.py:20
  155.0 12.7 %copy-start = (f32[3]{0:T(128)S(1)}, f32[3]{0:T(128)}, u32[]{:S(2)}) copy-start(f32[3]{0:T(128)} %cheb_ref.1) | copy-start | bytes 40

commit v9 on v8

--- a/solution.py
+++ b/solution.py
@@ -31,6 +31,10 @@
 
 def stay(array):
     return pltpu.with_memory_space_constraint(array, pltpu.HBM)
+
+
+def aligned(value, by):
+    return value if isinstance(value, int) else pl.multiple_of(value, by)
 
 
 def dot(a, b):
@@ -68,9 +72,9 @@
 
 
 def products_of(own_ref, s, part):
-    val = own_ref[part, s, 0:16, :].astype(F32)
-    cond = own_ref[part, s, 16:32, :].astype(F32)
-    pieces = [(val[v : v + 1, :] * cond).astype(BF) for v in range(16)]
+    val = own_ref[part, s, 0:16, :]
+    cond = own_ref[part, s, 16:32, :]
+    pieces = [val[v : v + 1, :] * cond for v in range(16)]
     return jnp.concatenate(pieces, axis=0)
 
 
@@ -184,7 +188,7 @@
             for n in range(2):
                 at = peer * 32 + 2 * e + n
                 pick_ref[at : at + 1, :] = (lane == first + n).astype(F32)
-            at = pl.multiple_of(s * 32, 32)
+            at = aligned(s * 32, 32)
 
             @pl.when(ours)
             def _():
@@ -323,15 +327,13 @@
         slot = plane_ref[lax.axis_index(PLANE), 0, 8 + i]
         total = jnp.zeros((256, 256), F32)
         for part in range(4):
-            at = pl.multiple_of(i * 32, 16)
-            a = wide_ref[part, pl.ds(at, 16), :].astype(F32)
-            b = wide_ref[part, pl.ds(at + 16, 16), :].astype(F32)
-            left = jnp.concatenate(
-                [(a[v : v + 1, :] * b).astype(BF) for v in range(16)], axis=0
-            )
+            at = aligned(i * 32, 16)
+            a = wide_ref[part, pl.ds(at, 16), :]
+            b = wide_ref[part, pl.ds(at + 16, 16), :]
+            left = jnp.concatenate([a[v : v + 1, :] * b for v in range(16)], axis=0)
             total = total + dot(left, scr_ref[slot, part * 256 : (part + 1) * 256, :])
         total = total.astype(BF)
-        at = pl.multiple_of(i * 256, 256)
+        at = aligned(i * 256, 256)
         op_ref[0, pl.ds(at, 256), :] = total[:, 0:128]
         op_ref[1, pl.ds(at, 256), :] = total[:, 128:256]
         total = total.astype(F32)
@@ -340,7 +342,8 @@
         apply_pair(i, half_ref, cond_ref, xs_ref, ys_ref, t_ref, u_ref)
         return carry
 
-    lax.fori_loop(0, 3, one, 0)
+    for i in range(3):
+        one(i, 0)
     for part in range(4):
         for e in range(6):
             rs_ref[part, 2 * e : 2 * e + 2, :] = ys_ref[e, 2 * part : 2 * part + 2, :]
@@ -388,20 +391,20 @@
     chunks = [(ref, h) for ref in (op_ref, left_ref, right_ref, far_ref) for h in range(2)]
 
     def one(p, carry):
-        at = pl.multiple_of(p * 64, 64)
+        at = aligned(p * 64, 64)
         conds = []
         for end in range(2):
-            row = pl.multiple_of(768 + p * 32 + end * 16, 16)
+            row = aligned(768 + p * 32 + end * 16, 16)
             conds.append(
                 jnp.concatenate([ref[h, pl.ds(row, 16), :] for ref, h in chunks], axis=1)
             )
-            t_ref[end] = dot(x_ref[pl.ds(pl.multiple_of(at + 32 * end, 32), 32), :], conds[end])
+            t_ref[end] = dot(x_ref[pl.ds(aligned(at + 32 * end, 32), 32), :], conds[end])
         for k, (ref, h) in enumerate(chunks):
             span = slice(128 * k, 128 * k + 128)
             t_c = [t_ref[1, 8 * g : 8 * g + 8, span] for g in range(4)]
             sums = [None] * 4
             for v in range(16):
-                tile = ref[h, pl.ds(pl.multiple_of(p * 256 + 16 * v, 16), 16), :].astype(F32)
+                tile = ref[h, pl.ds(aligned(p * 256 + 16 * v, 16), 16), :].astype(F32)
                 lo, hi = tile[0:8, :], tile[8:16, :]
                 for n in range(2):
                     ua_ref[128 * n + 8 * v : 128 * n + 8 * v + 8, span] = (
@@ -416,10 +419,11 @@
                 uc_ref[8 * g : 8 * g + 8, span] = sums[g]
         first = dot_t(ua_ref[...].astype(BF), conds[0])
         y_ref[pl.ds(at, 32), :] = jnp.sum(first.reshape(32, 8, 16), axis=1)
-        y_ref[pl.ds(pl.multiple_of(at + 32, 32), 32), :] = dot_t(uc_ref[...].astype(BF), conds[1])
+        y_ref[pl.ds(aligned(at + 32, 32), 32), :] = dot_t(uc_ref[...].astype(BF), conds[1])
         return carry
 
-    lax.fori_loop(0, 3, one, 0)
+    for p in range(3):
+        one(p, 0)
     full = dot(y_ref[...].astype(BF), picker(16, 256)).reshape(12, 16, 256)
     rs_ref[0:12, :] = jnp.sum(jnp.where(here[None], full, 0.0), axis=1)
     rs_ref[12:16, :] = jnp.zeros((4, 256), F32)

time: 171 us -> 170 us (level)
  no operation moved by 1% of the time
where the time goes in v9:
time: 170 us; the launch traced here: 169 us
  blocking collectives  80.4 us (47%)
  starting transfers between devices  39 us (23%)
  waiting for transfers between devices  29.6 us (17%)
  Pallas kernels  20 us (12%)
    all_to_all x4, blocking collectives, exchange(): return lax.all_to_all(blocks, axis, 0, 0, tiled=True)  43 us
    all_gather x1, blocking collectives, body(): gat = lax.all_gather(packed, 'z')  37.5 us
    all_to_all x4, starting transfers between devices, exchange(): return lax.all_to_all(blocks, axis, 0, 0, tiled=True)  28.7 us
    pallas_call x13, Pallas kernels, run(): pl.pallas_call(kernel, out_shape=[jax.ShapeDtypeStruct(s, d) for s, d in...  20 us
    all_to_all x4, waiting for transfers between devices, exchange(): return lax.all_to_all(blocks, axis, 0, 0, tiled=True)  19.4 us
    ppermute x3, waiting for transfers between devices, shift(): lax.ppermute(shard, 'y', [(k, (k + by) % count) for k in range(count)])  10.2 us
    ppermute x3, starting transfers between devices, shift(): lax.ppermute(shard, 'y', [(k, (k + by) % count) for k in range(count)])  8.31 us
  transfers between devices with their start and end apart: 8, of which 6 were waited for; matrix products, arithmetic and copies ran while one was open for 0% of the time, Pallas kernels for 5%

profile of v9, /device:TPU:32, one launch (start us, length us, event | category | flops | bytes accessed | tf_op | source)
XLA Modules:
  0.0 169.1 jit_solution(14575804106107010213)
XLA Ops:
  0.0 1.6 shard_map.92
  1.6 4.5 %all-to-all-start.1 = ((bf16[4,2,32,256]{3,2,1,0:T(8,128)(2,1)}), bf16[4,2,32,256]{3,2,1,0:T(8,128)(2,1)S(1)}, u32[]{:S(2)}, u32[]{:S(2)}) async-start(bf16[4,2,32,256]{3,2,1,0:T(8,128)(2,1)} %shard_map.92), calls=%async_computation.1 | async-start | bytes 262144 | tf_op jit(solution)/shard_map/all_to_all | solution.py:20
  6.1 0.9 shard_map.91
  7.0 5.1 %all-to-all-done.1.own_ref = bf16[4,2,32,256]{3,2,1,0:T(8,128)(2,1)S(1)} async-done(((bf16[4,2,32,256]{3,2,1,0:T(8,128)(2,1)}), bf16[4,2,32,256]{3,2,1,0:T(8,128)(2,1)S(1)}, u32[]{:S(2)}, u32[]{:S(2)}) %all-to-all-start.1) | async-done | bytes 131104 | tf_op jit(solution)/shard_map/all_to_all | solution.py:20
  12.1 0.3 shard_map.93
  12.3 37.5 %all-gather = bf16[1280,256]{1,0:T(8,128)(2,1)S(1)} all-gather(bf16[80,256]{1,0:T(8,128)(2,1)S(1)} %shard_map.93), channel_id=2, replica_groups=mesh['z'=16,'x'=4,'c'=2,'y'=4] {'z'}, dimensions={0}, use_global_device_ids=true | all-gather | bytes 696320 | tf_op jit(solution)/shard_map/all_gather | solution.py:495
  49.8 1.9 %collective-permute-start = (bf16[16,80,256]{2,1,0:T(8,128)(2,1)S(1)}, bf16[16,80,256]{2,1,0:T(8,128)(2,1)S(1)}, u32[]{:S(2)}, u32[]{:S(2)}) collective-permute-start(bf16[16,80,256]{2,1,0:T(8,128)(2,1)S(1)} %bitcast.2), channel_id=1, source_target_pairs={{0,4},{4,0},{1,5},{5,1},{2,6},{6,2},{3,7},{7,3},{8,12},{12,8},{9,1... | collective-permute-start | bytes 1966088 | tf_op jit(solution)/shard_map/ppermute | solution.py:24
  51.7 9.5 %all_to_all.40.plane_ref = s32[8,1,128]{2,1,0:T(1,128)S(1)} all-to-all(s32[8,1,128]{2,1,0:T(1,128)S(1)} %get-tuple-element.19), channel_id=1, replica_groups=mesh['z'=16,'x'=4,'c'=2,'y'=4] {'x','c'}, dimensions={0} | all-to-all | bytes 8192 | tf_op jit(solution)/shard_map/all_to_all | solution.py:20
  61.2 0.0 collective-permute-done.twin_ref
  61.2 1.5 shard_map.94
  62.8 11.4 %all_to_all.41.got_ref = bf16[4,224,256]{2,1,0:T(8,128)(2,1)S(1)} all-to-all(bf16[4,224,256]{2,1,0:T(8,128)(2,1)S(1)} %get-tuple-element.21), channel_id=1, replica_groups=mesh['z'=16,'x'=4,'c'=2,'y'=4] {'x'}, dimensions={0} | all-to-all | bytes 917504 | tf_op jit(solution)/shard_map/all_to_all | solution.py:20
  74.2 1.4 shard_map.95
  75.5 3.4 %all-to-all-start.3 = ((bf16[4,112,256]{2,1,0:T(8,128)(2,1)}), bf16[4,112,256]{2,1,0:T(8,128)(2,1)S(1)}, u32[]{:S(2)}, u32[]{:S(2)}) async-start(bf16[4,112,256]{2,1,0:T(8,128)(2,1)} %get-tuple-element.26), calls=%async_computation.3 | async-start | bytes 458752 | tf_op jit(solution)/shard_map/all_to_all | solution.py:20
  78.9 1.2 shard_map.97.scr_ref
  80.2 3.3 %shard_map.96 = (f32[4,256]{1,0:T(4,128)S(1)}, bf16[256,128]{1,0:T(8,128)(2,1)S(1)}, bf16[64,128]{1,0:T(8,128)(2,1)S(1)}) custom-call(s32[8,1,128]{2,1,0:T(1,128)S(1)} %all_to_all.40.plane_ref, f32[8,256]{1,0:T(8,128)S(1)} %get-tuple-element.22.dens_ref, f32[8,256]{1,0:T(8,128)S(1)} %get-tuple-element.23.column_ref, ...), custom_call_target="tpu_custom_call" | custom-call | bytes 4194304 | tf_op jit(solution)/shard_map/pallas_call | solution.py:54
  83.4 2.0 %all-to-all-done.3.wide_ref = bf16[4,112,256]{2,1,0:T(8,128)(2,1)S(1)} async-done(((bf16[4,112,256]{2,1,0:T(8,128)(2,1)}), bf16[4,112,256]{2,1,0:T(8,128)(2,1)S(1)}, u32[]{:S(2)}, u32[]{:S(2)}) %all-to-all-start.3) | async-done | bytes 229408 | tf_op jit(solution)/shard_map/all_to_all | solution.py:20
  85.4 2.7 %shard_map.98 = (bf16[2,864,128]{2,1,0:T(8,128)(2,1)S(1)}, bf16[32,16,256]{2,1,0:T(8,128)(2,1)S(1)}) custom-call(s32[8,1,128]{2,1,0:T(1,128)S(1)} %all_to_all.40.plane_ref, bf16[4,112,256]{2,1,0:T(8,128)(2,1)S(1)} %all-to-all-done.3.wide_ref, bf16[6,16,256]{2,1,0:T(8,128)(2,1)S(1)} %get-tuple-element.27.cond_ref, ...), custom_call_target="tpu_custom_call" | custom-call | bytes 4194304 | tf_op jit(solution)/shard_map/pallas_call | solution.py:54
  88.1 2.5 %collective-permute-start.1 = (bf16[2,864,128]{2,1,0:T(8,128)(2,1)S(1)}, bf16[2,864,128]{2,1,0:T(8,128)(2,1)S(1)}, u32[]{:S(2)}, u32[]{:S(2)}) collective-permute-start(bf16[2,864,128]{2,1,0:T(8,128)(2,1)S(1)} %get-tuple-element.30.op_ref), channel_id=1, source_target_pairs={{0,1},{1,2},{2,3},{3,0},{4,5},{5,6},{6,7},{7,4},{8,9},{9,10},{10,1... | collective-permute-start | bytes 1327112 | tf_op jit(solution)/shard_map/ppermute | solution.py:29
  90.6 13.9 %all_to_all.42.got_ref = bf16[32,16,256]{2,1,0:T(8,128)(2,1)S(1)} all-to-all(bf16[32,16,256]{2,1,0:T(8,128)(2,1)S(1)} %get-tuple-element.29), channel_id=1, replica_groups=mesh['z'=16,'x'=4,'c'=2,'y'=4] {'x','c','y'}, dimensions={0} | all-to-all | bytes 524288 | tf_op jit(solution)/shard_map/all_to_all | solution.py:20
  104.4 0.9 shard_map.99
  105.3 8.9 %all-to-all-start.5 = ((bf16[16,16,256]{2,1,0:T(8,128)(2,1)}), bf16[16,16,256]{2,1,0:T(8,128)(2,1)S(1)}, u32[]{:S(2)}, u32[]{:S(2)}) async-start(bf16[16,16,256]{2,1,0:T(8,128)(2,1)} %shard_map.99), calls=%async_computation.5 | async-start | bytes 262144 | tf_op jit(solution)/shard_map/all_to_all | solution.py:20
  114.2 3.2 %collective-permute-start.2 = (bf16[2,864,128]{2,1,0:T(8,128)(2,1)S(1)}, bf16[2,864,128]{2,1,0:T(8,128)(2,1)S(1)}, u32[]{:S(2)}, u32[]{:S(2)}) collective-permute-start(bf16[2,864,128]{2,1,0:T(8,128)(2,1)S(1)} %get-tuple-element.30.op_ref), channel_id=1, source_target_pairs={{0,3},{1,0},{2,1},{3,2},{4,7},{5,4},{6,5},{7,6},{8,11},{9,8},{10,9... | collective-permute-start | bytes 1327112 | tf_op jit(solution)/shard_map/ppermute | solution.py:29
  117.3 0.0 collective-permute-done.1.left_ref
  117.3 2.7 %collective-permute-start.3 = (bf16[2,864,128]{2,1,0:T(8,128)(2,1)S(1)}, bf16[2,864,128]{2,1,0:T(8,128)(2,1)S(1)}, u32[]{:S(2)}, u32[]{:S(2)}) collective-permute-start(bf16[2,864,128]{2,1,0:T(8,128)(2,1)S(1)} %collective-permute-done.1.left_ref), channel_id=1, source_target_pairs={{0,1},{1,2},{2,3},{3,0},{4,5},{5,6},{6,7},{7,4},{8,9},{9,10},{10,1... | collective-permute-start | bytes 1327112 | tf_op jit(solution)/shard_map/ppermute | solution.py:29
  120.0 7.5 %collective-permute-done.2.right_ref = bf16[2,864,128]{2,1,0:T(8,128)(2,1)S(1)} collective-permute-done((bf16[2,864,128]{2,1,0:T(8,128)(2,1)S(1)}, bf16[2,864,128]{2,1,0:T(8,128)(2,1)S(1)}, u32[]{:S(2)}, u32[]{:S(2)}) %collective-permute-start.2) | collective-permute-done | bytes 442400 | tf_op jit(solution)/shard_map/ppermute | solution.py:29
  127.5 1.2 all-to-all-done.5.got_ref
  128.7 2.7 %collective-permute-done.3.far_ref = bf16[2,864,128]{2,1,0:T(8,128)(2,1)S(1)} collective-permute-done((bf16[2,864,128]{2,1,0:T(8,128)(2,1)S(1)}, bf16[2,864,128]{2,1,0:T(8,128)(2,1)S(1)}, u32[]{:S(2)}, u32[]{:S(2)}) %collective-permute-start.3) | collective-permute-done | bytes 442400 | tf_op jit(solution)/shard_map/ppermute | solution.py:29
  131.5 1.8 %shard_map.100 = (bf16[8,16,384]{2,1,0:T(8,128)(2,1)S(1)}, f32[4,256]{1,0:T(4,128)S(1)}) custom-call(bf16[16,16,256]{2,1,0:T(8,128)(2,1)S(1)} %all-to-all-done.5.got_ref, bf16[4,2,32,256]{3,2,1,0:T(8,128)(2,1)S(1)} %all-to-all-done.1.own_ref, bf16[2,864,128]{2,1,0:T(8,128)(2,1)S(1)} %get-tuple-element.30.op_ref, ...), custom_call_target="tpu_custom_call" | custom-call | bytes 4194304 | tf_op jit(solution)/shard_map/pallas_call | solution.py:54
  133.3 8.2 %all_to_all.43.got_ref = bf16[8,16,384]{2,1,0:T(8,128)(2,1)S(1)} all-to-all(bf16[8,16,384]{2,1,0:T(8,128)(2,1)S(1)} %get-tuple-element.31), channel_id=1, replica_groups=mesh['z'=16,'x'=4,'c'=2,'y'=4] {'x','c'}, dimensions={0} | all-to-all | bytes 196608 | tf_op jit(solution)/shard_map/all_to_all | solution.py:20
  141.5 0.8 shard_map.101
  142.3 12.0 %all-to-all-start.7 = ((bf16[16,8,384]{2,1,0:T(8,128)(2,1)}), bf16[16,8,384]{2,1,0:T(8,128)(2,1)S(1)}, u32[]{:S(2)}, u32[]{:S(2)}) async-start(bf16[16,8,384]{2,1,0:T(8,128)(2,1)} %shard_map.101), calls=%async_computation.7 | async-start | bytes 196608 | tf_op jit(solution)/shard_map/all_to_all | solution.py:20
  154.3 0.0 copy-start
  154.3 1.6 shard_map.102.bare_ref
  155.9 11.1 %all-to-all-done.7.got_ref = bf16[16,8,384]{2,1,0:T(8,128)(2,1)S(1)} async-done(((bf16[16,8,384]{2,1,0:T(8,128)(2,1)}), bf16[16,8,384]{2,1,0:T(8,128)(2,1)S(1)}, u32[]{:S(2)}, u32[]{:S(2)}) %all-to-all-start.7) | async-done | bytes 98336 | tf_op jit(solution)/shard_map/all_to_all | solution.py:20
  167.0 0.0 copy-done
  167.0 2.1 %shard_map.103 = f32[2,2,256]{2,1,0:T(2,128)} custom-call(f32[3]{0:T(128)S(1)} %copy-done, bf16[16,8,384]{2,1,0:T(8,128)(2,1)S(1)} %all-to-all-done.7.got_ref, bf16[4,2,32,256]{3,2,1,0:T(8,128)(2,1)S(1)} %all-to-all-done.1.own_ref, bf16[1024,1024]{1,0:T(8,128)(2,1)S(1)} %shard_map.102.bare_ref, f32[8,256]{1,0:T(8,128)S(1)} %get-tuple-element.20.held_ref, ...), custom_call_target="tpu_custom_call" | custom-call | bytes 4194304 | tf_op jit(solution)/shard_map/pallas_call | solution.py:54
Async XLA Ops:
  1.6 10.5 %all-to-all-start.1 = ((bf16[4,2,32,256]{3,2,1,0:T(8,128)(2,1)}), bf16[4,2,32,256]{3,2,1,0:T(8,128)(2,1)S(1)}, u32[]{:S(2)}, u32[]{:S(2)}) async-start(bf16[4,2,32,256]{3,2,1,0:T(8,128)(2,1)} %shard_map.92), calls=%async_computation.1 | async-start | bytes 262144 | tf_op jit(solution)/shard_map/all_to_all | solution.py:20
  49.8 11.4 %collective-permute-start = (bf16[16,80,256]{2,1,0:T(8,128)(2,1)S(1)}, bf16[16,80,256]{2,1,0:T(8,128)(2,1)S(1)}, u32[]{:S(2)}, u32[]{:S(2)}) collective-permute-start(bf16[16,80,256]{2,1,0:T(8,128)(2,1)S(1)} %bitcast.2), channel_id=1, source_target_pairs={{0,4},{4,0},{1,5},{5,1},{2,6},{6,2},{3,7},{7,3},{8,12},{12,8},{9,1... | collective-permute-start | bytes 1966088 | tf_op jit(solution)/shard_map/ppermute | solution.py:24
  75.5 9.9 %all-to-all-start.3 = ((bf16[4,112,256]{2,1,0:T(8,128)(2,1)}), bf16[4,112,256]{2,1,0:T(8,128)(2,1)S(1)}, u32[]{:S(2)}, u32[]{:S(2)}) async-start(bf16[4,112,256]{2,1,0:T(8,128)(2,1)} %get-tuple-element.26), calls=%async_computation.3 | async-start | bytes 458752 | tf_op jit(solution)/shard_map/all_to_all | solution.py:20
  88.1 29.3 %collective-permute-start.1 = (bf16[2,864,128]{2,1,0:T(8,128)(2,1)S(1)}, bf16[2,864,128]{2,1,0:T(8,128)(2,1)S(1)}, u32[]{:S(2)}, u32[]{:S(2)}) collective-permute-start(bf16[2,864,128]{2,1,0:T(8,128)(2,1)S(1)} %get-tuple-element.30.op_ref), channel_id=1, source_target_pairs={{0,1},{1,2},{2,3},{3,0},{4,5},{5,6},{6,7},{7,4},{8,9},{9,10},{10,1... | collective-permute-start | bytes 1327112 | tf_op jit(solution)/shard_map/ppermute | solution.py:29
  105.3 23.4 %all-to-all-start.5 = ((bf16[16,16,256]{2,1,0:T(8,128)(2,1)}), bf16[16,16,256]{2,1,0:T(8,128)(2,1)S(1)}, u32[]{:S(2)}, u32[]{:S(2)}) async-start(bf16[16,16,256]{2,1,0:T(8,128)(2,1)} %shard_map.99), calls=%async_computation.5 | async-start | bytes 262144 | tf_op jit(solution)/shard_map/all_to_all | solution.py:20
  114.2 13.3 %collective-permute-start.2 = (bf16[2,864,128]{2,1,0:T(8,128)(2,1)S(1)}, bf16[2,864,128]{2,1,0:T(8,128)(2,1)S(1)}, u32[]{:S(2)}, u32[]{:S(2)}) collective-permute-start(bf16[2,864,128]{2,1,0:T(8,128)(2,1)S(1)} %get-tuple-element.30.op_ref), channel_id=1, source_target_pairs={{0,3},{1,0},{2,1},{3,2},{4,7},{5,4},{6,5},{7,6},{8,11},{9,8},{10,9... | collective-permute-start | bytes 1327112 | tf_op jit(solution)/shard_map/ppermute | solution.py:29
  117.3 14.1 %collective-permute-start.3 = (bf16[2,864,128]{2,1,0:T(8,128)(2,1)S(1)}, bf16[2,864,128]{2,1,0:T(8,128)(2,1)S(1)}, u32[]{:S(2)}, u32[]{:S(2)}) collective-permute-start(bf16[2,864,128]{2,1,0:T(8,128)(2,1)S(1)} %collective-permute-done.1.left_ref), channel_id=1, source_target_pairs={{0,1},{1,2},{2,3},{3,0},{4,5},{5,6},{6,7},{7,4},{8,9},{9,10},{10,1... | collective-permute-start | bytes 1327112 | tf_op jit(solution)/shard_map/ppermute | solution.py:29
  142.3 24.7 %all-to-all-start.7 = ((bf16[16,8,384]{2,1,0:T(8,128)(2,1)}), bf16[16,8,384]{2,1,0:T(8,128)(2,1)S(1)}, u32[]{:S(2)}, u32[]{:S(2)}) async-start(bf16[16,8,384]{2,1,0:T(8,128)(2,1)} %shard_map.101), calls=%async_computation.7 | async-start | bytes 196608 | tf_op jit(solution)/shard_map/all_to_all | solution.py:20
  154.3 12.7 %copy-start = (f32[3]{0:T(128)S(1)}, f32[3]{0:T(128)}, u32[]{:S(2)}) copy-start(f32[3]{0:T(128)} %cheb_ref.1) | copy-start | bytes 40

commit v10 on v9

--- a/solution.py
+++ b/solution.py
@@ -104,16 +104,6 @@
             total = total + dot_t(pots[part], products_of(own_ref, s, part))
         terms.append(total)
     return terms
-
-
-def copies_kernel(orb_hbm, own_ref, sem):
-    copies = [
-        pltpu.make_async_copy(orb_hbm, own_ref.at[part], sem.at[part]) for part in range(4)
-    ]
-    for copy in copies:
-        copy.start()
-    for copy in copies:
-        copy.wait()
 
 
 def info_kernel(
@@ -371,7 +361,7 @@
 
 
 def second_kernel(
-    got_ref, own_ref, op_ref, left_ref, right_ref, far_ref, out_ref, own_x_ref,
+    got_ref, own_ref, op_ref, left_ref, right_ref, far_ref, rest_ref, out_ref, own_x_ref,
     x_ref, y_ref, t_ref, ua_ref, uc_ref, rs_ref, ds_ref,
 ):
     total = got_ref[0].astype(F32)
@@ -388,7 +378,8 @@
     rows = [jnp.where(here, total[k : k + 1, :], 0.0).astype(BF) for k in range(12)]
     x_ref[...] = dot(jnp.concatenate(rows, axis=0), picker(256, 16)).astype(BF)
 
-    chunks = [(ref, h) for ref in (op_ref, left_ref, right_ref, far_ref) for h in range(2)]
+    chunks = [(ref, h) for ref in (op_ref, left_ref, right_ref) for h in range(2)]
+    chunks += [(far_ref, 0), (rest_ref, 0)]
 
     def one(p, carry):
         at = aligned(p * 64, 64)
@@ -471,11 +462,7 @@
 
 
 def body(orbitals, transition, trial, screened, bare, cheb, pair_k, pair_slot, k_order):
-    (copies,) = call(
-        copies_kernel, [((4, 2, 32, 256), BF)], (), [pltpu.SemaphoreType.DMA((4,))], (0,)
-    )(stay(orbitals))
     far_bare = stay(bare)
-    own = exchange(copies, "y")
     ids, held = call(
         info_kernel,
         [((8, 1, 128), jnp.int32), ((8, 256), F32)],
@@ -491,6 +478,7 @@
         range(5),
     )(*map(stay, (pair_k, pair_slot, k_order.reshape(1, -1), trial, transition)))
     plane = exchange(ids, PLANE)
+    own = lax.all_gather(orbitals, "y")
     (packed,) = call(pack_kernel, [((80, 256), BF)], (), [pltpu.VMEM((16, 256), F32)])(held, own)
     gat = lax.all_gather(packed, "z")
     twin = swap(gat)
@@ -541,7 +529,8 @@
     right = shift(op, -1)
     (middle,) = call(middle_kernel, [((16, 16, 256), BF)], ())(route, mixed)
     step = exchange(middle, "z")
-    far = shift(left, 1)
+    far = shift(left[0], 1)
+    rest = shift(right[1], -1)
     out2, own_x = call(
         second_kernel,
         [((8, 16, 384), BF), ((4, 256), F32)],
@@ -555,7 +544,7 @@
             pltpu.VMEM((16, 256), F32),
             pltpu.VMEM((16, 128), F32),
         ],
-    )(step, own, op, left, right, far)
+    )(step, own, op, left, right, far[None], rest[None])
     (final,) = call(return_kernel, [((16, 8, 384), BF)], (), [pltpu.VMEM((16, 8, 384), F32)])(
         back, exchange(out2, PLANE)
     )

time: 170 us -> 167 us (0.982)
  waiting for transfers between devices: 29.6 us -> 27.3 us
  starting transfers between devices: 39 us -> 41.3 us
    all_to_all x4 -> x3, blocking collectives: 43 us -> 29.1 us  [exchange(): return lax.all_to_all(blocks, axis, 0, 0, tiled=True)]
    all_gather x0 -> x1, blocking collectives: none -> 12.7 us  [body(): own = lax.all_gather(orbitals, 'y')]
    ppermute x3 -> x4, starting transfers between devices: 8.31 us -> 12.6 us  [shift(): lax.ppermute(shard, 'y', [(k, (k + by) % count) for k in range(count)])]
    ppermute x3 -> x4, waiting for transfers between devices: 10.2 us -> 7.04 us  [shift(): lax.ppermute(shard, 'y', [(k, (k + by) % count) for k in range(count)])]
    all_to_all x4, starting transfers between devices: 28.7 us -> 26.8 us  [exchange(): return lax.all_to_all(blocks, axis, 0, 0, tiled=True)]
    pallas_call x13 -> x12, Pallas kernels: 20 us -> 19 us  [run(): pl.pallas_call(kernel, out_shape=[jax.ShapeDtypeStruct(s, d) for s, d in...]
  transfers between devices with their start and end apart: 8 -> 9, of which waited for: 6 -> 6; matrix products, arithmetic and copies ran while one was open for 0% -> 0% of each run, Pallas kernels for 5% -> 4%
where the time goes in v10:
time: 167 us
  blocking collectives  78.8 us (47%)
  starting transfers between devices  41.3 us (25%)
  waiting for transfers between devices  27.3 us (16%)
  Pallas kernels  19 us (11%)
    all_gather x1, blocking collectives, body(): gat = lax.all_gather(packed, 'z')  37 us
    all_to_all x3, blocking collectives, exchange(): return lax.all_to_all(blocks, axis, 0, 0, tiled=True)  29.1 us
    all_to_all x4, starting transfers between devices, exchange(): return lax.all_to_all(blocks, axis, 0, 0, tiled=True)  26.8 us
    all_to_all x4, waiting for transfers between devices, exchange(): return lax.all_to_all(blocks, axis, 0, 0, tiled=True)  20.2 us
    pallas_call x12, Pallas kernels, run(): pl.pallas_call(kernel, out_shape=[jax.ShapeDtypeStruct(s, d) for s, d in...  19 us
    all_gather x1, blocking collectives, body(): own = lax.all_gather(orbitals, 'y')  12.7 us
    ppermute x4, starting transfers between devices, shift(): lax.ppermute(shard, 'y', [(k, (k + by) % count) for k in range(count)])  12.6 us
    ppermute x4, waiting for transfers between devices, shift(): lax.ppermute(shard, 'y', [(k, (k + by) % count) for k in range(count)])  7.04 us
  transfers between devices with their start and end apart: 9, of which 6 were waited for; matrix products, arithmetic and copies ran while one was open for 0% of the time, Pallas kernels for 4%

profile of v10, /device:TPU:32, one launch (start us, length us, event | category | flops | bytes accessed | tf_op | source)
XLA Modules:
  0.0 166.5 jit_solution(4832347218355375663)
XLA Ops:
  0.0 12.7 %all-gather = bf16[8,32,256]{2,1,0:T(8,128)(2,1)S(1)} all-gather(bf16[2,32,256]{2,1,0:T(8,128)(2,1)} %param.9), channel_id=2, replica_groups=mesh['z'=16,'x'=4,'c'=2,'y'=4] {'y'}, dimensions={0}, use_global_device_ids=true | all-gather | bytes 163840 | tf_op jit(solution)/shard_map/all_gather | solution.py:481
  12.7 0.9 shard_map.91
  13.6 0.3 shard_map.92
  13.9 37.0 %all-gather.1 = bf16[1280,256]{1,0:T(8,128)(2,1)S(1)} all-gather(bf16[80,256]{1,0:T(8,128)(2,1)S(1)} %shard_map.92), channel_id=3, replica_groups=mesh['z'=16,'x'=4,'c'=2,'y'=4] {'z'}, dimensions={0}, use_global_device_ids=true | all-gather | bytes 696320 | tf_op jit(solution)/shard_map/all_gather | solution.py:483
  50.9 1.9 %collective-permute-start = (bf16[16,80,256]{2,1,0:T(8,128)(2,1)S(1)}, bf16[16,80,256]{2,1,0:T(8,128)(2,1)S(1)}, u32[]{:S(2)}, u32[]{:S(2)}) collective-permute-start(bf16[16,80,256]{2,1,0:T(8,128)(2,1)S(1)} %bitcast.13), channel_id=1, source_target_pairs={{0,4},{4,0},{1,5},{5,1},{2,6},{6,2},{3,7},{7,3},{8,12},{12,8},{9,1... | collective-permute-start | bytes 1966088 | tf_op jit(solution)/shard_map/ppermute | solution.py:24
  52.8 9.5 %all_to_all.35.plane_ref = s32[8,1,128]{2,1,0:T(1,128)S(1)} all-to-all(s32[8,1,128]{2,1,0:T(1,128)S(1)} %get-tuple-element.19), channel_id=1, replica_groups=mesh['z'=16,'x'=4,'c'=2,'y'=4] {'x','c'}, dimensions={0} | all-to-all | bytes 8192 | tf_op jit(solution)/shard_map/all_to_all | solution.py:20
  62.3 0.0 collective-permute-done.twin_ref
  62.3 1.5 shard_map.93
  63.8 11.4 %all_to_all.36.got_ref = bf16[4,224,256]{2,1,0:T(8,128)(2,1)S(1)} all-to-all(bf16[4,224,256]{2,1,0:T(8,128)(2,1)S(1)} %get-tuple-element.21), channel_id=1, replica_groups=mesh['z'=16,'x'=4,'c'=2,'y'=4] {'x'}, dimensions={0} | all-to-all | bytes 917504 | tf_op jit(solution)/shard_map/all_to_all | solution.py:20
  75.2 1.3 shard_map.94
  76.6 3.7 %all-to-all-start.2 = ((bf16[4,112,256]{2,1,0:T(8,128)(2,1)}), bf16[4,112,256]{2,1,0:T(8,128)(2,1)S(1)}, u32[]{:S(2)}, u32[]{:S(2)}) async-start(bf16[4,112,256]{2,1,0:T(8,128)(2,1)} %get-tuple-element.26), calls=%async_computation.2 | async-start | bytes 458752 | tf_op jit(solution)/shard_map/all_to_all | solution.py:20
  80.2 1.2 shard_map.96.scr_ref
  81.5 3.3 %shard_map.95 = (f32[4,256]{1,0:T(4,128)S(1)}, bf16[256,128]{1,0:T(8,128)(2,1)S(1)}, bf16[64,128]{1,0:T(8,128)(2,1)S(1)}) custom-call(s32[8,1,128]{2,1,0:T(1,128)S(1)} %all_to_all.35.plane_ref, f32[8,256]{1,0:T(8,128)S(1)} %get-tuple-element.22.dens_ref, f32[8,256]{1,0:T(8,128)S(1)} %get-tuple-element.23.column_ref, bf16[4,2,32,256]{3,2,1,0:T(8,128)(2,1)S(1)} %bitcast.10, ...), custom_call_target="tpu_custom_call" | custom-call | bytes 4194304 | tf_op jit(solution)/shard_map/pallas_call | solution.py:54
  84.7 2.0 %all-to-all-done.2.wide_ref = bf16[4,112,256]{2,1,0:T(8,128)(2,1)S(1)} async-done(((bf16[4,112,256]{2,1,0:T(8,128)(2,1)}), bf16[4,112,256]{2,1,0:T(8,128)(2,1)S(1)}, u32[]{:S(2)}, u32[]{:S(2)}) %all-to-all-start.2) | async-done | bytes 229408 | tf_op jit(solution)/shard_map/all_to_all | solution.py:20
  86.7 3.4 %shard_map.97 = (bf16[2,864,128]{2,1,0:T(8,128)(2,1)S(1)}, bf16[32,16,256]{2,1,0:T(8,128)(2,1)}) custom-call(s32[8,1,128]{2,1,0:T(1,128)S(1)} %all_to_all.35.plane_ref, bf16[4,112,256]{2,1,0:T(8,128)(2,1)S(1)} %all-to-all-done.2.wide_ref, bf16[6,16,256]{2,1,0:T(8,128)(2,1)S(1)} %get-tuple-element.27.cond_ref, bf16[2,1024,256]{2,1,0:T(8,128)(2,1)S(1)} %shard_map.96.scr_ref, ...), custom_call_target="tpu_custom_call" | custom-call | bytes 4194304 | tf_op jit(solution)/shard_map/pallas_call | solution.py:54
  90.1 3.1 %collective-permute-start.2 = (bf16[2,864,128]{2,1,0:T(8,128)(2,1)S(1)}, bf16[2,864,128]{2,1,0:T(8,128)(2,1)S(1)}, u32[]{:S(2)}, u32[]{:S(2)}) collective-permute-start(bf16[2,864,128]{2,1,0:T(8,128)(2,1)S(1)} %get-tuple-element.30.op_ref), channel_id=1, source_target_pairs={{0,3},{1,0},{2,1},{3,2},{4,7},{5,4},{6,5},{7,6},{8,11},{9,8},{10,9... | collective-permute-start | bytes 1327112 | tf_op jit(solution)/shard_map/ppermute | solution.py:29
  93.3 3.9 %all-to-all-start.3 = ((bf16[32,16,256]{2,1,0:T(8,128)(2,1)}), bf16[32,16,256]{2,1,0:T(8,128)(2,1)S(1)}, u32[]{:S(2)}, u32[]{:S(2)}) async-start(bf16[32,16,256]{2,1,0:T(8,128)(2,1)} %get-tuple-element.29), calls=%async_computation.3 | async-start | bytes 524288 | tf_op jit(solution)/shard_map/all_to_all | solution.py:20
  97.1 3.6 %collective-permute-start.1 = (bf16[2,864,128]{2,1,0:T(8,128)(2,1)S(1)}, bf16[2,864,128]{2,1,0:T(8,128)(2,1)S(1)}, u32[]{:S(2)}, u32[]{:S(2)}) collective-permute-start(bf16[2,864,128]{2,1,0:T(8,128)(2,1)S(1)} %get-tuple-element.30.op_ref), channel_id=1, source_target_pairs={{0,1},{1,2},{2,3},{3,0},{4,5},{5,6},{6,7},{7,4},{8,9},{9,10},{10,1... | collective-permute-start | bytes 1327112 | tf_op jit(solution)/shard_map/ppermute | solution.py:29
  100.7 5.5 %all-to-all-done.3.got_ref = bf16[32,16,256]{2,1,0:T(8,128)(2,1)S(1)} async-done(((bf16[32,16,256]{2,1,0:T(8,128)(2,1)}), bf16[32,16,256]{2,1,0:T(8,128)(2,1)S(1)}, u32[]{:S(2)}, u32[]{:S(2)}) %all-to-all-start.3) | async-done | bytes 262176 | tf_op jit(solution)/shard_map/all_to_all | solution.py:20
  106.3 0.8 shard_map.98
  107.1 8.9 %all-to-all-start.4 = ((bf16[16,16,256]{2,1,0:T(8,128)(2,1)}), bf16[16,16,256]{2,1,0:T(8,128)(2,1)S(1)}, u32[]{:S(2)}, u32[]{:S(2)}) async-start(bf16[16,16,256]{2,1,0:T(8,128)(2,1)} %shard_map.98), calls=%async_computation.4 | async-start | bytes 262144 | tf_op jit(solution)/shard_map/all_to_all | solution.py:20
  116.0 0.0 collective-permute-done.2.right_ref
  116.0 3.4 %collective-permute-start.4 = (bf16[864,128]{1,0:T(8,128)(2,1)S(1)}, bf16[864,128]{1,0:T(8,128)(2,1)S(1)}, u32[]{:S(2)}, u32[]{:S(2)}) collective-permute-start(bf16[864,128]{1,0:T(8,128)(2,1)S(1)} %slice_bitcast_fusion), channel_id=1, source_target_pairs={{0,3},{1,0},{2,1},{3,2},{4,7},{5,4},{6,5},{7,6},{8,11},{9,8},{10,9... | collective-permute-start | bytes 663560 | tf_op jit(solution)/shard_map/ppermute | solution.py:29
  119.4 0.0 collective-permute-done.1.left_ref
  119.4 2.5 %collective-permute-start.3 = (bf16[864,128]{1,0:T(8,128)(2,1)S(1)}, bf16[864,128]{1,0:T(8,128)(2,1)S(1)}, u32[]{:S(2)}, u32[]{:S(2)}) collective-permute-start(bf16[864,128]{1,0:T(8,128)(2,1)S(1)} %slice_bitcast_fusion.1), channel_id=1, source_target_pairs={{0,1},{1,2},{2,3},{3,0},{4,5},{5,6},{6,7},{7,4},{8,9},{9,10},{10,1... | collective-permute-start | bytes 663560 | tf_op jit(solution)/shard_map/ppermute | solution.py:29
  121.9 2.7 %collective-permute-done.4 = bf16[864,128]{1,0:T(8,128)(2,1)S(1)} collective-permute-done((bf16[864,128]{1,0:T(8,128)(2,1)S(1)}, bf16[864,128]{1,0:T(8,128)(2,1)S(1)}, u32[]{:S(2)}, u32[]{:S(2)}) %collective-permute-start.4) | collective-permute-done | bytes 221216 | tf_op jit(solution)/shard_map/ppermute | solution.py:29
  124.6 4.3 %collective-permute-done.3 = bf16[864,128]{1,0:T(8,128)(2,1)S(1)} collective-permute-done((bf16[864,128]{1,0:T(8,128)(2,1)S(1)}, bf16[864,128]{1,0:T(8,128)(2,1)S(1)}, u32[]{:S(2)}, u32[]{:S(2)}) %collective-permute-start.3) | collective-permute-done | bytes 221216 | tf_op jit(solution)/shard_map/ppermute | solution.py:29
  128.9 1.6 all-to-all-done.4.got_ref
  130.6 1.8 %shard_map.99 = (bf16[8,16,384]{2,1,0:T(8,128)(2,1)S(1)}, f32[4,256]{1,0:T(4,128)S(1)}) custom-call(bf16[16,16,256]{2,1,0:T(8,128)(2,1)S(1)} %all-to-all-done.4.got_ref, bf16[4,2,32,256]{3,2,1,0:T(8,128)(2,1)S(1)} %bitcast.11, bf16[2,864,128]{2,1,0:T(8,128)(2,1)S(1)} %get-tuple-element.30.op_ref, bf16[2,864,128]{2,1,0:T(8,128)(2,1)S(1)} %collective-permute-done.1.left_ref, ...), custom_call_target="tpu_custom_call" | custom-call | bytes 4194304 | tf_op jit(solution)/shard_map/pallas_call | solution.py:54
  132.4 8.2 %all_to_all.37.got_ref = bf16[8,16,384]{2,1,0:T(8,128)(2,1)S(1)} all-to-all(bf16[8,16,384]{2,1,0:T(8,128)(2,1)S(1)} %get-tuple-element.31), channel_id=1, replica_groups=mesh['z'=16,'x'=4,'c'=2,'y'=4] {'x','c'}, dimensions={0} | all-to-all | bytes 196608 | tf_op jit(solution)/shard_map/all_to_all | solution.py:20
  140.6 0.8 shard_map.100
  141.4 10.4 %all-to-all-start.6 = ((bf16[16,8,384]{2,1,0:T(8,128)(2,1)}), bf16[16,8,384]{2,1,0:T(8,128)(2,1)S(1)}, u32[]{:S(2)}, u32[]{:S(2)}) async-start(bf16[16,8,384]{2,1,0:T(8,128)(2,1)} %shard_map.100), calls=%async_computation.6 | async-start | bytes 196608 | tf_op jit(solution)/shard_map/all_to_all | solution.py:20
  151.8 0.0 copy-start
  151.8 1.6 shard_map.101.bare_ref
  153.4 11.1 %all-to-all-done.6.got_ref = bf16[16,8,384]{2,1,0:T(8,128)(2,1)S(1)} async-done(((bf16[16,8,384]{2,1,0:T(8,128)(2,1)}), bf16[16,8,384]{2,1,0:T(8,128)(2,1)S(1)}, u32[]{:S(2)}, u32[]{:S(2)}) %all-to-all-start.6) | async-done | bytes 98336 | tf_op jit(solution)/shard_map/all_to_all | solution.py:20
  164.5 0.0 copy-done
  164.5 2.1 %shard_map.102 = f32[2,2,256]{2,1,0:T(2,128)} custom-call(f32[3]{0:T(128)S(1)} %copy-done, bf16[16,8,384]{2,1,0:T(8,128)(2,1)S(1)} %all-to-all-done.6.got_ref, bf16[4,2,32,256]{3,2,1,0:T(8,128)(2,1)S(1)} %bitcast.12, bf16[1024,1024]{1,0:T(8,128)(2,1)S(1)} %shard_map.101.bare_ref, f32[8,256]{1,0:T(8,128)S(1)} %get-tuple-element.20.held_ref, ...), custom_call_target="tpu_custom_call" | custom-call | bytes 4194304 | tf_op jit(solution)/shard_map/pallas_call | solution.py:54
  (2 shorter events, 0.0 us)
Async XLA Ops:
  50.9 11.4 %collective-permute-start = (bf16[16,80,256]{2,1,0:T(8,128)(2,1)S(1)}, bf16[16,80,256]{2,1,0:T(8,128)(2,1)S(1)}, u32[]{:S(2)}, u32[]{:S(2)}) collective-permute-start(bf16[16,80,256]{2,1,0:T(8,128)(2,1)S(1)} %bitcast.13), channel_id=1, source_target_pairs={{0,4},{4,0},{1,5},{5,1},{2,6},{6,2},{3,7},{7,3},{8,12},{12,8},{9,1... | collective-permute-start | bytes 1966088 | tf_op jit(solution)/shard_map/ppermute | solution.py:24
  76.6 10.2 %all-to-all-start.2 = ((bf16[4,112,256]{2,1,0:T(8,128)(2,1)}), bf16[4,112,256]{2,1,0:T(8,128)(2,1)S(1)}, u32[]{:S(2)}, u32[]{:S(2)}) async-start(bf16[4,112,256]{2,1,0:T(8,128)(2,1)} %get-tuple-element.26), calls=%async_computation.2 | async-start | bytes 458752 | tf_op jit(solution)/shard_map/all_to_all | solution.py:20
  90.1 25.9 %collective-permute-start.2 = (bf16[2,864,128]{2,1,0:T(8,128)(2,1)S(1)}, bf16[2,864,128]{2,1,0:T(8,128)(2,1)S(1)}, u32[]{:S(2)}, u32[]{:S(2)}) collective-permute-start(bf16[2,864,128]{2,1,0:T(8,128)(2,1)S(1)} %get-tuple-element.30.op_ref), channel_id=1, source_target_pairs={{0,3},{1,0},{2,1},{3,2},{4,7},{5,4},{6,5},{7,6},{8,11},{9,8},{10,9... | collective-permute-start | bytes 1327112 | tf_op jit(solution)/shard_map/ppermute | solution.py:29
  93.3 13.0 %all-to-all-start.3 = ((bf16[32,16,256]{2,1,0:T(8,128)(2,1)}), bf16[32,16,256]{2,1,0:T(8,128)(2,1)S(1)}, u32[]{:S(2)}, u32[]{:S(2)}) async-start(bf16[32,16,256]{2,1,0:T(8,128)(2,1)} %get-tuple-element.29), calls=%async_computation.3 | async-start | bytes 524288 | tf_op jit(solution)/shard_map/all_to_all | solution.py:20
  97.1 22.2 %collective-permute-start.1 = (bf16[2,864,128]{2,1,0:T(8,128)(2,1)S(1)}, bf16[2,864,128]{2,1,0:T(8,128)(2,1)S(1)}, u32[]{:S(2)}, u32[]{:S(2)}) collective-permute-start(bf16[2,864,128]{2,1,0:T(8,128)(2,1)S(1)} %get-tuple-element.30.op_ref), channel_id=1, source_target_pairs={{0,1},{1,2},{2,3},{3,0},{4,5},{5,6},{6,7},{7,4},{8,9},{9,10},{10,1... | collective-permute-start | bytes 1327112 | tf_op jit(solution)/shard_map/ppermute | solution.py:29
  107.1 23.4 %all-to-all-start.4 = ((bf16[16,16,256]{2,1,0:T(8,128)(2,1)}), bf16[16,16,256]{2,1,0:T(8,128)(2,1)S(1)}, u32[]{:S(2)}, u32[]{:S(2)}) async-start(bf16[16,16,256]{2,1,0:T(8,128)(2,1)} %shard_map.98), calls=%async_computation.4 | async-start | bytes 262144 | tf_op jit(solution)/shard_map/all_to_all | solution.py:20
  116.0 8.6 %collective-permute-start.4 = (bf16[864,128]{1,0:T(8,128)(2,1)S(1)}, bf16[864,128]{1,0:T(8,128)(2,1)S(1)}, u32[]{:S(2)}, u32[]{:S(2)}) collective-permute-start(bf16[864,128]{1,0:T(8,128)(2,1)S(1)} %slice_bitcast_fusion), channel_id=1, source_target_pairs={{0,3},{1,0},{2,1},{3,2},{4,7},{5,4},{6,5},{7,6},{8,11},{9,8},{10,9... | collective-permute-start | bytes 663560 | tf_op jit(solution)/shard_map/ppermute | solution.py:29
  119.4 9.5 %collective-permute-start.3 = (bf16[864,128]{1,0:T(8,128)(2,1)S(1)}, bf16[864,128]{1,0:T(8,128)(2,1)S(1)}, u32[]{:S(2)}, u32[]{:S(2)}) collective-permute-start(bf16[864,128]{1,0:T(8,128)(2,1)S(1)} %slice_bitcast_fusion.1), channel_id=1, source_target_pairs={{0,1},{1,2},{2,3},{3,0},{4,5},{5,6},{6,7},{7,4},{8,9},{9,10},{10,1... | collective-permute-start | bytes 663560 | tf_op jit(solution)/shard_map/ppermute | solution.py:29
  141.4 23.1 %all-to-all-start.6 = ((bf16[16,8,384]{2,1,0:T(8,128)(2,1)}), bf16[16,8,384]{2,1,0:T(8,128)(2,1)S(1)}, u32[]{:S(2)}, u32[]{:S(2)}) async-start(bf16[16,8,384]{2,1,0:T(8,128)(2,1)} %shard_map.100), calls=%async_computation.6 | async-start | bytes 196608 | tf_op jit(solution)/shard_map/all_to_all | solution.py:20
  151.8 12.7 %copy-start = (f32[3]{0:T(128)S(1)}, f32[3]{0:T(128)}, u32[]{:S(2)}) copy-start(f32[3]{0:T(128)} %cheb_ref.1) | copy-start | bytes 40

commit v11 on v9

--- a/solution.py
+++ b/solution.py
@@ -371,7 +371,7 @@
 
 
 def second_kernel(
-    got_ref, own_ref, op_ref, left_ref, right_ref, far_ref, out_ref, own_x_ref,
+    got_ref, own_ref, op_ref, left_ref, right_ref, far_ref, rest_ref, out_ref, own_x_ref,
     x_ref, y_ref, t_ref, ua_ref, uc_ref, rs_ref, ds_ref,
 ):
     total = got_ref[0].astype(F32)
@@ -388,7 +388,8 @@
     rows = [jnp.where(here, total[k : k + 1, :], 0.0).astype(BF) for k in range(12)]
     x_ref[...] = dot(jnp.concatenate(rows, axis=0), picker(256, 16)).astype(BF)
 
-    chunks = [(ref, h) for ref in (op_ref, left_ref, right_ref, far_ref) for h in range(2)]
+    chunks = [(ref, h) for ref in (op_ref, left_ref, right_ref) for h in range(2)]
+    chunks += [(far_ref, 0), (rest_ref, 0)]
 
     def one(p, carry):
         at = aligned(p * 64, 64)
@@ -541,7 +542,8 @@
     right = shift(op, -1)
     (middle,) = call(middle_kernel, [((16, 16, 256), BF)], ())(route, mixed)
     step = exchange(middle, "z")
-    far = shift(left, 1)
+    far = shift(left[0], 1)
+    rest = shift(right[1], -1)
     out2, own_x = call(
         second_kernel,
         [((8, 16, 384), BF), ((4, 256), F32)],
@@ -555,9 +557,10 @@
             pltpu.VMEM((16, 256), F32),
             pltpu.VMEM((16, 128), F32),
         ],
-    )(step, own, op, left, right, far)
+    )(step, own, op, left, right, far[None], rest[None])
+    returned = exchange(out2, PLANE)
     (final,) = call(return_kernel, [((16, 8, 384), BF)], (), [pltpu.VMEM((16, 8, 384), F32)])(
-        back, exchange(out2, PLANE)
+        back, returned
     )
     last = exchange(final, "z")
     (near_bare,) = call(

time: 170 us -> 166 us (0.976)
  blocking collectives: 80.4 us -> 66.6 us
  starting transfers between devices: 39 us -> 45.8 us
  waiting for transfers between devices: 29.6 us -> 32.3 us
    all_to_all x4 -> x3, blocking collectives: 43 us -> 29.1 us  [exchange(): return lax.all_to_all(blocks, axis, 0, 0, tiled=True)]
    all_to_all x4 -> x5, waiting for transfers between devices: 19.4 us -> 25 us  [exchange(): return lax.all_to_all(blocks, axis, 0, 0, tiled=True)]
    ppermute x3 -> x4, starting transfers between devices: 8.31 us -> 12.6 us  [shift(): lax.ppermute(shard, 'y', [(k, (k + by) % count) for k in range(count)])]
    ppermute x3 -> x4, waiting for transfers between devices: 10.2 us -> 7.32 us  [shift(): lax.ppermute(shard, 'y', [(k, (k + by) % count) for k in range(count)])]
    all_to_all x4 -> x5, starting transfers between devices: 28.7 us -> 31.3 us  [exchange(): return lax.all_to_all(blocks, axis, 0, 0, tiled=True)]
  transfers between devices with their start and end apart: 8 -> 10, of which waited for: 6 -> 7; matrix products, arithmetic and copies ran while one was open for 0% -> 0% of each run, Pallas kernels for 5% -> 5%
where the time goes in v11:
time: 166 us; the launch traced here: 165 us
  blocking collectives  66.6 us (40%)
  starting transfers between devices  45.8 us (28%)
  waiting for transfers between devices  32.3 us (19%)
  Pallas kernels  20.6 us (12%)
    all_gather x1, blocking collectives, body(): gat = lax.all_gather(packed, 'z')  37.5 us
    all_to_all x5, starting transfers between devices, exchange(): return lax.all_to_all(blocks, axis, 0, 0, tiled=True)  31.3 us
    all_to_all x3, blocking collectives, exchange(): return lax.all_to_all(blocks, axis, 0, 0, tiled=True)  29.1 us
    all_to_all x5, waiting for transfers between devices, exchange(): return lax.all_to_all(blocks, axis, 0, 0, tiled=True)  25 us
    pallas_call x13, Pallas kernels, run(): pl.pallas_call(kernel, out_shape=[jax.ShapeDtypeStruct(s, d) for s, d in...  20.6 us
    ppermute x4, starting transfers between devices, shift(): lax.ppermute(shard, 'y', [(k, (k + by) % count) for k in range(count)])  12.6 us
    ppermute x4, waiting for transfers between devices, shift(): lax.ppermute(shard, 'y', [(k, (k + by) % count) for k in range(count)])  7.32 us
  transfers between devices with their start and end apart: 10, of which 7 were waited for; matrix products, arithmetic and copies ran while one was open for 0% of the time, Pallas kernels for 5%

profile of v11, /device:TPU:32, one launch (start us, length us, event | category | flops | bytes accessed | tf_op | source)
XLA Modules:
  0.0 165.5 jit_solution(4878762864461544700)
XLA Ops:
  0.0 1.6 shard_map.92
  1.6 4.5 %all-to-all-start.1 = ((bf16[4,2,32,256]{3,2,1,0:T(8,128)(2,1)}), bf16[4,2,32,256]{3,2,1,0:T(8,128)(2,1)S(1)}, u32[]{:S(2)}, u32[]{:S(2)}) async-start(bf16[4,2,32,256]{3,2,1,0:T(8,128)(2,1)} %shard_map.92), calls=%async_computation.1 | async-start | bytes 262144 | tf_op jit(solution)/shard_map/all_to_all | solution.py:20
  6.1 0.9 shard_map.91
  7.0 5.1 %all-to-all-done.1.own_ref = bf16[4,2,32,256]{3,2,1,0:T(8,128)(2,1)S(1)} async-done(((bf16[4,2,32,256]{3,2,1,0:T(8,128)(2,1)}), bf16[4,2,32,256]{3,2,1,0:T(8,128)(2,1)S(1)}, u32[]{:S(2)}, u32[]{:S(2)}) %all-to-all-start.1) | async-done | bytes 131104 | tf_op jit(solution)/shard_map/all_to_all | solution.py:20
  12.0 0.3 shard_map.93
  12.3 37.5 %all-gather = bf16[1280,256]{1,0:T(8,128)(2,1)S(1)} all-gather(bf16[80,256]{1,0:T(8,128)(2,1)S(1)} %shard_map.93), channel_id=2, replica_groups=mesh['z'=16,'x'=4,'c'=2,'y'=4] {'z'}, dimensions={0}, use_global_device_ids=true | all-gather | bytes 696320 | tf_op jit(solution)/shard_map/all_gather | solution.py:496
  49.8 1.9 %collective-permute-start = (bf16[16,80,256]{2,1,0:T(8,128)(2,1)S(1)}, bf16[16,80,256]{2,1,0:T(8,128)(2,1)S(1)}, u32[]{:S(2)}, u32[]{:S(2)}) collective-permute-start(bf16[16,80,256]{2,1,0:T(8,128)(2,1)S(1)} %bitcast.8), channel_id=1, source_target_pairs={{0,4},{4,0},{1,5},{5,1},{2,6},{6,2},{3,7},{7,3},{8,12},{12,8},{9,1... | collective-permute-start | bytes 1966088 | tf_op jit(solution)/shard_map/ppermute | solution.py:24
  51.7 9.5 %all_to_all.40.plane_ref = s32[8,1,128]{2,1,0:T(1,128)S(1)} all-to-all(s32[8,1,128]{2,1,0:T(1,128)S(1)} %get-tuple-element.19), channel_id=1, replica_groups=mesh['z'=16,'x'=4,'c'=2,'y'=4] {'x','c'}, dimensions={0} | all-to-all | bytes 8192 | tf_op jit(solution)/shard_map/all_to_all | solution.py:20
  61.2 0.0 collective-permute-done.twin_ref
  61.2 1.5 shard_map.94
  62.7 11.4 %all_to_all.41.got_ref = bf16[4,224,256]{2,1,0:T(8,128)(2,1)S(1)} all-to-all(bf16[4,224,256]{2,1,0:T(8,128)(2,1)S(1)} %get-tuple-element.21), channel_id=1, replica_groups=mesh['z'=16,'x'=4,'c'=2,'y'=4] {'x'}, dimensions={0} | all-to-all | bytes 917504 | tf_op jit(solution)/shard_map/all_to_all | solution.py:20
  74.1 1.3 shard_map.95
  75.5 3.4 %all-to-all-start.3 = ((bf16[4,112,256]{2,1,0:T(8,128)(2,1)}), bf16[4,112,256]{2,1,0:T(8,128)(2,1)S(1)}, u32[]{:S(2)}, u32[]{:S(2)}) async-start(bf16[4,112,256]{2,1,0:T(8,128)(2,1)} %get-tuple-element.26), calls=%async_computation.3 | async-start | bytes 458752 | tf_op jit(solution)/shard_map/all_to_all | solution.py:20
  78.9 1.2 shard_map.97.scr_ref
  80.1 3.3 %shard_map.96 = (f32[4,256]{1,0:T(4,128)S(1)}, bf16[256,128]{1,0:T(8,128)(2,1)S(1)}, bf16[64,128]{1,0:T(8,128)(2,1)S(1)}) custom-call(s32[8,1,128]{2,1,0:T(1,128)S(1)} %all_to_all.40.plane_ref, f32[8,256]{1,0:T(8,128)S(1)} %get-tuple-element.22.dens_ref, f32[8,256]{1,0:T(8,128)S(1)} %get-tuple-element.23.column_ref, ...), custom_call_target="tpu_custom_call" | custom-call | bytes 4194304 | tf_op jit(solution)/shard_map/pallas_call | solution.py:54
  83.4 2.0 %all-to-all-done.3.wide_ref = bf16[4,112,256]{2,1,0:T(8,128)(2,1)S(1)} async-done(((bf16[4,112,256]{2,1,0:T(8,128)(2,1)}), bf16[4,112,256]{2,1,0:T(8,128)(2,1)S(1)}, u32[]{:S(2)}, u32[]{:S(2)}) %all-to-all-start.3) | async-done | bytes 229408 | tf_op jit(solution)/shard_map/all_to_all | solution.py:20
  85.3 3.4 %shard_map.98 = (bf16[2,864,128]{2,1,0:T(8,128)(2,1)S(1)}, bf16[32,16,256]{2,1,0:T(8,128)(2,1)}) custom-call(s32[8,1,128]{2,1,0:T(1,128)S(1)} %all_to_all.40.plane_ref, bf16[4,112,256]{2,1,0:T(8,128)(2,1)S(1)} %all-to-all-done.3.wide_ref, bf16[6,16,256]{2,1,0:T(8,128)(2,1)S(1)} %get-tuple-element.27.cond_ref, bf16[2,1024,256]{2,1,0:T(8,128)(2,1)S(1)} %shard_map.97.scr_ref, ...), custom_call_target="tpu_custom_call" | custom-call | bytes 4194304 | tf_op jit(solution)/shard_map/pallas_call | solution.py:54
  88.7 3.1 %collective-permute-start.2 = (bf16[2,864,128]{2,1,0:T(8,128)(2,1)S(1)}, bf16[2,864,128]{2,1,0:T(8,128)(2,1)S(1)}, u32[]{:S(2)}, u32[]{:S(2)}) collective-permute-start(bf16[2,864,128]{2,1,0:T(8,128)(2,1)S(1)} %get-tuple-element.30.op_ref), channel_id=1, source_target_pairs={{0,3},{1,0},{2,1},{3,2},{4,7},{5,4},{6,5},{7,6},{8,11},{9,8},{10,9... | collective-permute-start | bytes 1327112 | tf_op jit(solution)/shard_map/ppermute | solution.py:29
  91.9 3.9 %all-to-all-start.4 = ((bf16[32,16,256]{2,1,0:T(8,128)(2,1)}), bf16[32,16,256]{2,1,0:T(8,128)(2,1)S(1)}, u32[]{:S(2)}, u32[]{:S(2)}) async-start(bf16[32,16,256]{2,1,0:T(8,128)(2,1)} %get-tuple-element.29), calls=%async_computation.4 | async-start | bytes 524288 | tf_op jit(solution)/shard_map/all_to_all | solution.py:20
  95.8 3.6 %collective-permute-start.1 = (bf16[2,864,128]{2,1,0:T(8,128)(2,1)S(1)}, bf16[2,864,128]{2,1,0:T(8,128)(2,1)S(1)}, u32[]{:S(2)}, u32[]{:S(2)}) collective-permute-start(bf16[2,864,128]{2,1,0:T(8,128)(2,1)S(1)} %get-tuple-element.30.op_ref), channel_id=1, source_target_pairs={{0,1},{1,2},{2,3},{3,0},{4,5},{5,6},{6,7},{7,4},{8,9},{9,10},{10,1... | collective-permute-start | bytes 1327112 | tf_op jit(solution)/shard_map/ppermute | solution.py:29
  99.4 5.5 %all-to-all-done.4.got_ref = bf16[32,16,256]{2,1,0:T(8,128)(2,1)S(1)} async-done(((bf16[32,16,256]{2,1,0:T(8,128)(2,1)}), bf16[32,16,256]{2,1,0:T(8,128)(2,1)S(1)}, u32[]{:S(2)}, u32[]{:S(2)}) %all-to-all-start.4) | async-done | bytes 262176 | tf_op jit(solution)/shard_map/all_to_all | solution.py:20
  104.9 0.8 shard_map.99
  105.7 8.9 %all-to-all-start.5 = ((bf16[16,16,256]{2,1,0:T(8,128)(2,1)}), bf16[16,16,256]{2,1,0:T(8,128)(2,1)S(1)}, u32[]{:S(2)}, u32[]{:S(2)}) async-start(bf16[16,16,256]{2,1,0:T(8,128)(2,1)} %shard_map.99), calls=%async_computation.5 | async-start | bytes 262144 | tf_op jit(solution)/shard_map/all_to_all | solution.py:20
  114.6 0.0 collective-permute-done.2.right_ref
  114.6 3.6 %collective-permute-start.4 = (bf16[864,128]{1,0:T(8,128)(2,1)S(1)}, bf16[864,128]{1,0:T(8,128)(2,1)S(1)}, u32[]{:S(2)}, u32[]{:S(2)}) collective-permute-start(bf16[864,128]{1,0:T(8,128)(2,1)S(1)} %slice_bitcast_fusion), channel_id=1, source_target_pairs={{0,3},{1,0},{2,1},{3,2},{4,7},{5,4},{6,5},{7,6},{8,11},{9,8},{10,9... | collective-permute-start | bytes 663560 | tf_op jit(solution)/shard_map/ppermute | solution.py:29
  118.3 0.0 collective-permute-done.1.left_ref
  118.3 2.2 %collective-permute-start.3 = (bf16[864,128]{1,0:T(8,128)(2,1)S(1)}, bf16[864,128]{1,0:T(8,128)(2,1)S(1)}, u32[]{:S(2)}, u32[]{:S(2)}) collective-permute-start(bf16[864,128]{1,0:T(8,128)(2,1)S(1)} %slice_bitcast_fusion.1), channel_id=1, source_target_pairs={{0,1},{1,2},{2,3},{3,0},{4,5},{5,6},{6,7},{7,4},{8,9},{9,10},{10,1... | collective-permute-start | bytes 663560 | tf_op jit(solution)/shard_map/ppermute | solution.py:29
  120.5 2.7 %collective-permute-done.4 = bf16[864,128]{1,0:T(8,128)(2,1)S(1)} collective-permute-done((bf16[864,128]{1,0:T(8,128)(2,1)S(1)}, bf16[864,128]{1,0:T(8,128)(2,1)S(1)}, u32[]{:S(2)}, u32[]{:S(2)}) %collective-permute-start.4) | collective-permute-done | bytes 221216 | tf_op jit(solution)/shard_map/ppermute | solution.py:29
  123.2 4.6 %collective-permute-done.3 = bf16[864,128]{1,0:T(8,128)(2,1)S(1)} collective-permute-done((bf16[864,128]{1,0:T(8,128)(2,1)S(1)}, bf16[864,128]{1,0:T(8,128)(2,1)S(1)}, u32[]{:S(2)}, u32[]{:S(2)}) %collective-permute-start.3) | collective-permute-done | bytes 221216 | tf_op jit(solution)/shard_map/ppermute | solution.py:29
  127.8 1.3 all-to-all-done.5.got_ref
  129.2 1.8 %shard_map.100 = (bf16[8,16,384]{2,1,0:T(8,128)(2,1)S(1)}, f32[4,256]{1,0:T(4,128)S(1)}) custom-call(bf16[16,16,256]{2,1,0:T(8,128)(2,1)S(1)} %all-to-all-done.5.got_ref, bf16[4,2,32,256]{3,2,1,0:T(8,128)(2,1)S(1)} %all-to-all-done.1.own_ref, bf16[2,864,128]{2,1,0:T(8,128)(2,1)S(1)} %get-tuple-element.30.op_ref, ...), custom_call_target="tpu_custom_call" | custom-call | bytes 4194304 | tf_op jit(solution)/shard_map/pallas_call | solution.py:54
  131.0 8.2 %all_to_all.42.got_ref = bf16[8,16,384]{2,1,0:T(8,128)(2,1)S(1)} all-to-all(bf16[8,16,384]{2,1,0:T(8,128)(2,1)S(1)} %get-tuple-element.31), channel_id=1, replica_groups=mesh['z'=16,'x'=4,'c'=2,'y'=4] {'x','c'}, dimensions={0} | all-to-all | bytes 196608 | tf_op jit(solution)/shard_map/all_to_all | solution.py:20
  139.2 0.8 shard_map.101
  140.0 10.7 %all-to-all-start.7 = ((bf16[16,8,384]{2,1,0:T(8,128)(2,1)}), bf16[16,8,384]{2,1,0:T(8,128)(2,1)S(1)}, u32[]{:S(2)}, u32[]{:S(2)}) async-start(bf16[16,8,384]{2,1,0:T(8,128)(2,1)} %shard_map.101), calls=%async_computation.7 | async-start | bytes 196608 | tf_op jit(solution)/shard_map/all_to_all | solution.py:20
  150.7 0.0 copy-start
  150.7 1.6 shard_map.102.bare_ref
  152.3 11.1 %all-to-all-done.7.got_ref = bf16[16,8,384]{2,1,0:T(8,128)(2,1)S(1)} async-done(((bf16[16,8,384]{2,1,0:T(8,128)(2,1)}), bf16[16,8,384]{2,1,0:T(8,128)(2,1)S(1)}, u32[]{:S(2)}, u32[]{:S(2)}) %all-to-all-start.7) | async-done | bytes 98336 | tf_op jit(solution)/shard_map/all_to_all | solution.py:20
  163.4 0.0 copy-done
  163.4 2.1 %shard_map.103 = f32[2,2,256]{2,1,0:T(2,128)} custom-call(f32[3]{0:T(128)S(1)} %copy-done, bf16[16,8,384]{2,1,0:T(8,128)(2,1)S(1)} %all-to-all-done.7.got_ref, bf16[4,2,32,256]{3,2,1,0:T(8,128)(2,1)S(1)} %all-to-all-done.1.own_ref, bf16[1024,1024]{1,0:T(8,128)(2,1)S(1)} %shard_map.102.bare_ref, f32[8,256]{1,0:T(8,128)S(1)} %get-tuple-element.20.held_ref, ...), custom_call_target="tpu_custom_call" | custom-call | bytes 4194304 | tf_op jit(solution)/shard_map/pallas_call | solution.py:54
  (2 shorter events, 0.0 us)
Async XLA Ops:
  1.6 10.5 %all-to-all-start.1 = ((bf16[4,2,32,256]{3,2,1,0:T(8,128)(2,1)}), bf16[4,2,32,256]{3,2,1,0:T(8,128)(2,1)S(1)}, u32[]{:S(2)}, u32[]{:S(2)}) async-start(bf16[4,2,32,256]{3,2,1,0:T(8,128)(2,1)} %shard_map.92), calls=%async_computation.1 | async-start | bytes 262144 | tf_op jit(solution)/shard_map/all_to_all | solution.py:20
  49.8 11.4 %collective-permute-start = (bf16[16,80,256]{2,1,0:T(8,128)(2,1)S(1)}, bf16[16,80,256]{2,1,0:T(8,128)(2,1)S(1)}, u32[]{:S(2)}, u32[]{:S(2)}) collective-permute-start(bf16[16,80,256]{2,1,0:T(8,128)(2,1)S(1)} %bitcast.8), channel_id=1, source_target_pairs={{0,4},{4,0},{1,5},{5,1},{2,6},{6,2},{3,7},{7,3},{8,12},{12,8},{9,1... | collective-permute-start | bytes 1966088 | tf_op jit(solution)/shard_map/ppermute | solution.py:24
  75.5 9.9 %all-to-all-start.3 = ((bf16[4,112,256]{2,1,0:T(8,128)(2,1)}), bf16[4,112,256]{2,1,0:T(8,128)(2,1)S(1)}, u32[]{:S(2)}, u32[]{:S(2)}) async-start(bf16[4,112,256]{2,1,0:T(8,128)(2,1)} %get-tuple-element.26), calls=%async_computation.3 | async-start | bytes 458752 | tf_op jit(solution)/shard_map/all_to_all | solution.py:20
  88.7 25.9 %collective-permute-start.2 = (bf16[2,864,128]{2,1,0:T(8,128)(2,1)S(1)}, bf16[2,864,128]{2,1,0:T(8,128)(2,1)S(1)}, u32[]{:S(2)}, u32[]{:S(2)}) collective-permute-start(bf16[2,864,128]{2,1,0:T(8,128)(2,1)S(1)} %get-tuple-element.30.op_ref), channel_id=1, source_target_pairs={{0,3},{1,0},{2,1},{3,2},{4,7},{5,4},{6,5},{7,6},{8,11},{9,8},{10,9... | collective-permute-start | bytes 1327112 | tf_op jit(solution)/shard_map/ppermute | solution.py:29
  91.9 13.0 %all-to-all-start.4 = ((bf16[32,16,256]{2,1,0:T(8,128)(2,1)}), bf16[32,16,256]{2,1,0:T(8,128)(2,1)S(1)}, u32[]{:S(2)}, u32[]{:S(2)}) async-start(bf16[32,16,256]{2,1,0:T(8,128)(2,1)} %get-tuple-element.29), calls=%async_computation.4 | async-start | bytes 524288 | tf_op jit(solution)/shard_map/all_to_all | solution.py:20
  95.8 22.5 %collective-permute-start.1 = (bf16[2,864,128]{2,1,0:T(8,128)(2,1)S(1)}, bf16[2,864,128]{2,1,0:T(8,128)(2,1)S(1)}, u32[]{:S(2)}, u32[]{:S(2)}) collective-permute-start(bf16[2,864,128]{2,1,0:T(8,128)(2,1)S(1)} %get-tuple-element.30.op_ref), channel_id=1, source_target_pairs={{0,1},{1,2},{2,3},{3,0},{4,5},{5,6},{6,7},{7,4},{8,9},{9,10},{10,1... | collective-permute-start | bytes 1327112 | tf_op jit(solution)/shard_map/ppermute | solution.py:29
  105.7 23.4 %all-to-all-start.5 = ((bf16[16,16,256]{2,1,0:T(8,128)(2,1)}), bf16[16,16,256]{2,1,0:T(8,128)(2,1)S(1)}, u32[]{:S(2)}, u32[]{:S(2)}) async-start(bf16[16,16,256]{2,1,0:T(8,128)(2,1)} %shard_map.99), calls=%async_computation.5 | async-start | bytes 262144 | tf_op jit(solution)/shard_map/all_to_all | solution.py:20
  114.6 8.6 %collective-permute-start.4 = (bf16[864,128]{1,0:T(8,128)(2,1)S(1)}, bf16[864,128]{1,0:T(8,128)(2,1)S(1)}, u32[]{:S(2)}, u32[]{:S(2)}) collective-permute-start(bf16[864,128]{1,0:T(8,128)(2,1)S(1)} %slice_bitcast_fusion), channel_id=1, source_target_pairs={{0,3},{1,0},{2,1},{3,2},{4,7},{5,4},{6,5},{7,6},{8,11},{9,8},{10,9... | collective-permute-start | bytes 663560 | tf_op jit(solution)/shard_map/ppermute | solution.py:29
  118.3 9.5 %collective-permute-start.3 = (bf16[864,128]{1,0:T(8,128)(2,1)S(1)}, bf16[864,128]{1,0:T(8,128)(2,1)S(1)}, u32[]{:S(2)}, u32[]{:S(2)}) collective-permute-start(bf16[864,128]{1,0:T(8,128)(2,1)S(1)} %slice_bitcast_fusion.1), channel_id=1, source_target_pairs={{0,1},{1,2},{2,3},{3,0},{4,5},{5,6},{6,7},{7,4},{8,9},{9,10},{10,1... | collective-permute-start | bytes 663560 | tf_op jit(solution)/shard_map/ppermute | solution.py:29
  140.0 23.4 %all-to-all-start.7 = ((bf16[16,8,384]{2,1,0:T(8,128)(2,1)}), bf16[16,8,384]{2,1,0:T(8,128)(2,1)S(1)}, u32[]{:S(2)}, u32[]{:S(2)}) async-start(bf16[16,8,384]{2,1,0:T(8,128)(2,1)} %shard_map.101), calls=%async_computation.7 | async-start | bytes 196608 | tf_op jit(solution)/shard_map/all_to_all | solution.py:20
  150.7 12.7 %copy-start = (f32[3]{0:T(128)S(1)}, f32[3]{0:T(128)}, u32[]{:S(2)}) copy-start(f32[3]{0:T(128)} %cheb_ref.1) | copy-start | bytes 40

commit v12 on v11

--- a/solution.py
+++ b/solution.py
@@ -45,7 +45,7 @@
     return lax.dot_general(a, b, LAST, preferred_element_type=F32)
 
 
-def call(kernel, outs, smem, scratch=(), far=(), limit=LIMIT):
+def call(kernel, outs, smem, scratch=(), far=(), limit=LIMIT, out_space=pltpu.VMEM):
     def space(k):
         return pltpu.SMEM if k in smem else pltpu.HBM if k in far else pltpu.VMEM
 
@@ -56,7 +56,7 @@
             out_shape=[jax.ShapeDtypeStruct(s, d) for s, d in outs],
             in_specs=specs,
             out_specs=[
-                pl.BlockSpec(memory_space=pltpu.SMEM if len(s) == 1 else pltpu.VMEM)
+                pl.BlockSpec(memory_space=pltpu.SMEM if len(s) == 1 else out_space)
                 for s, _ in outs
             ],
             scratch_shapes=list(scratch),
@@ -473,7 +473,8 @@
 
 def body(orbitals, transition, trial, screened, bare, cheb, pair_k, pair_slot, k_order):
     (copies,) = call(
-        copies_kernel, [((4, 2, 32, 256), BF)], (), [pltpu.SemaphoreType.DMA((4,))], (0,)
+        copies_kernel, [((4, 2, 32, 256), BF)], (), [pltpu.SemaphoreType.DMA((4,))], (0,),
+        out_space=pltpu.HBM,
     )(stay(orbitals))
     far_bare = stay(bare)
     own = exchange(copies, "y")

time: 166 us -> 170 us (1.024)
  Pallas kernels: 20.6 us -> 24.1 us
    pallas_call x13, Pallas kernels: 20.6 us -> 24.1 us  [run(): pl.pallas_call(kernel, out_shape=[jax.ShapeDtypeStruct(s, d) for s, d in...]
where the time goes in v12:
time: 170 us; the launch traced here: 169 us
  blocking collectives  66.6 us (39%)
  starting transfers between devices  45.8 us (27%)
  waiting for transfers between devices  32.3 us (19%)
  Pallas kernels  24.1 us (14%)
    all_gather x1, blocking collectives, body(): gat = lax.all_gather(packed, 'z')  37.5 us
    all_to_all x5, starting transfers between devices, exchange(): return lax.all_to_all(blocks, axis, 0, 0, tiled=True)  31.3 us
    all_to_all x3, blocking collectives, exchange(): return lax.all_to_all(blocks, axis, 0, 0, tiled=True)  29.1 us
    all_to_all x5, waiting for transfers between devices, exchange(): return lax.all_to_all(blocks, axis, 0, 0, tiled=True)  25 us
    pallas_call x13, Pallas kernels, run(): pl.pallas_call(kernel, out_shape=[jax.ShapeDtypeStruct(s, d) for s, d in...  24.1 us
    ppermute x4, starting transfers between devices, shift(): lax.ppermute(shard, 'y', [(k, (k + by) % count) for k in range(count)])  12.6 us
    ppermute x4, waiting for transfers between devices, shift(): lax.ppermute(shard, 'y', [(k, (k + by) % count) for k in range(count)])  7.32 us
  transfers between devices with their start and end apart: 10, of which 7 were waited for; matrix products, arithmetic and copies ran while one was open for 0% of the time, Pallas kernels for 5%

profile of v12, /device:TPU:32, one launch (start us, length us, event | category | flops | bytes accessed | tf_op | source)
XLA Modules:
  0.0 169.0 jit_solution(1484547543238311718)
XLA Ops:
  0.0 5.1 %shard_map.92 = bf16[4,2,32,256]{3,2,1,0:T(8,128)(2,1)} custom-call(bf16[2,32,256]{2,1,0:T(8,128)(2,1)} %orb_hbm.1), custom_call_target="tpu_custom_call" | custom-call | bytes 4194304 | tf_op jit(solution)/shard_map/pallas_call | solution.py:54
  5.1 4.5 %all-to-all-start.1 = ((bf16[4,2,32,256]{3,2,1,0:T(8,128)(2,1)}), bf16[4,2,32,256]{3,2,1,0:T(8,128)(2,1)S(1)}, u32[]{:S(2)}, u32[]{:S(2)}) async-start(bf16[4,2,32,256]{3,2,1,0:T(8,128)(2,1)} %shard_map.92), calls=%async_computation.1 | async-start | bytes 262144 | tf_op jit(solution)/shard_map/all_to_all | solution.py:20
  9.6 0.9 shard_map.91
  10.5 5.1 %all-to-all-done.1.own_ref = bf16[4,2,32,256]{3,2,1,0:T(8,128)(2,1)S(1)} async-done(((bf16[4,2,32,256]{3,2,1,0:T(8,128)(2,1)}), bf16[4,2,32,256]{3,2,1,0:T(8,128)(2,1)S(1)}, u32[]{:S(2)}, u32[]{:S(2)}) %all-to-all-start.1) | async-done | bytes 131104 | tf_op jit(solution)/shard_map/all_to_all | solution.py:20
  15.6 0.3 shard_map.93
  15.8 37.5 %all-gather = bf16[1280,256]{1,0:T(8,128)(2,1)S(1)} all-gather(bf16[80,256]{1,0:T(8,128)(2,1)S(1)} %shard_map.93), channel_id=2, replica_groups=mesh['z'=16,'x'=4,'c'=2,'y'=4] {'z'}, dimensions={0}, use_global_device_ids=true | all-gather | bytes 696320 | tf_op jit(solution)/shard_map/all_gather | solution.py:497
  53.3 1.9 %collective-permute-start = (bf16[16,80,256]{2,1,0:T(8,128)(2,1)S(1)}, bf16[16,80,256]{2,1,0:T(8,128)(2,1)S(1)}, u32[]{:S(2)}, u32[]{:S(2)}) collective-permute-start(bf16[16,80,256]{2,1,0:T(8,128)(2,1)S(1)} %bitcast.8), channel_id=1, source_target_pairs={{0,4},{4,0},{1,5},{5,1},{2,6},{6,2},{3,7},{7,3},{8,12},{12,8},{9,1... | collective-permute-start | bytes 1966088 | tf_op jit(solution)/shard_map/ppermute | solution.py:24
  55.2 9.5 %all_to_all.40.plane_ref = s32[8,1,128]{2,1,0:T(1,128)S(1)} all-to-all(s32[8,1,128]{2,1,0:T(1,128)S(1)} %get-tuple-element.19), channel_id=1, replica_groups=mesh['z'=16,'x'=4,'c'=2,'y'=4] {'x','c'}, dimensions={0} | all-to-all | bytes 8192 | tf_op jit(solution)/shard_map/all_to_all | solution.py:20
  64.7 0.0 collective-permute-done.twin_ref
  64.7 1.5 shard_map.94
  66.3 11.4 %all_to_all.41.got_ref = bf16[4,224,256]{2,1,0:T(8,128)(2,1)S(1)} all-to-all(bf16[4,224,256]{2,1,0:T(8,128)(2,1)S(1)} %get-tuple-element.21), channel_id=1, replica_groups=mesh['z'=16,'x'=4,'c'=2,'y'=4] {'x'}, dimensions={0} | all-to-all | bytes 917504 | tf_op jit(solution)/shard_map/all_to_all | solution.py:20
  77.7 1.3 shard_map.95
  79.0 3.4 %all-to-all-start.3 = ((bf16[4,112,256]{2,1,0:T(8,128)(2,1)}), bf16[4,112,256]{2,1,0:T(8,128)(2,1)S(1)}, u32[]{:S(2)}, u32[]{:S(2)}) async-start(bf16[4,112,256]{2,1,0:T(8,128)(2,1)} %get-tuple-element.26), calls=%async_computation.3 | async-start | bytes 458752 | tf_op jit(solution)/shard_map/all_to_all | solution.py:20
  82.4 1.2 shard_map.97.scr_ref
  83.7 3.3 %shard_map.96 = (f32[4,256]{1,0:T(4,128)S(1)}, bf16[256,128]{1,0:T(8,128)(2,1)S(1)}, bf16[64,128]{1,0:T(8,128)(2,1)S(1)}) custom-call(s32[8,1,128]{2,1,0:T(1,128)S(1)} %all_to_all.40.plane_ref, f32[8,256]{1,0:T(8,128)S(1)} %get-tuple-element.22.dens_ref, f32[8,256]{1,0:T(8,128)S(1)} %get-tuple-element.23.column_ref, ...), custom_call_target="tpu_custom_call" | custom-call | bytes 4194304 | tf_op jit(solution)/shard_map/pallas_call | solution.py:54
  86.9 2.0 %all-to-all-done.3.wide_ref = bf16[4,112,256]{2,1,0:T(8,128)(2,1)S(1)} async-done(((bf16[4,112,256]{2,1,0:T(8,128)(2,1)}), bf16[4,112,256]{2,1,0:T(8,128)(2,1)S(1)}, u32[]{:S(2)}, u32[]{:S(2)}) %all-to-all-start.3) | async-done | bytes 229408 | tf_op jit(solution)/shard_map/all_to_all | solution.py:20
  88.9 3.4 %shard_map.98 = (bf16[2,864,128]{2,1,0:T(8,128)(2,1)S(1)}, bf16[32,16,256]{2,1,0:T(8,128)(2,1)}) custom-call(s32[8,1,128]{2,1,0:T(1,128)S(1)} %all_to_all.40.plane_ref, bf16[4,112,256]{2,1,0:T(8,128)(2,1)S(1)} %all-to-all-done.3.wide_ref, bf16[6,16,256]{2,1,0:T(8,128)(2,1)S(1)} %get-tuple-element.27.cond_ref, bf16[2,1024,256]{2,1,0:T(8,128)(2,1)S(1)} %shard_map.97.scr_ref, ...), custom_call_target="tpu_custom_call" | custom-call | bytes 4194304 | tf_op jit(solution)/shard_map/pallas_call | solution.py:54
  92.3 3.1 %collective-permute-start.2 = (bf16[2,864,128]{2,1,0:T(8,128)(2,1)S(1)}, bf16[2,864,128]{2,1,0:T(8,128)(2,1)S(1)}, u32[]{:S(2)}, u32[]{:S(2)}) collective-permute-start(bf16[2,864,128]{2,1,0:T(8,128)(2,1)S(1)} %get-tuple-element.30.op_ref), channel_id=1, source_target_pairs={{0,3},{1,0},{2,1},{3,2},{4,7},{5,4},{6,5},{7,6},{8,11},{9,8},{10,9... | collective-permute-start | bytes 1327112 | tf_op jit(solution)/shard_map/ppermute | solution.py:29
  95.4 3.9 %all-to-all-start.4 = ((bf16[32,16,256]{2,1,0:T(8,128)(2,1)}), bf16[32,16,256]{2,1,0:T(8,128)(2,1)S(1)}, u32[]{:S(2)}, u32[]{:S(2)}) async-start(bf16[32,16,256]{2,1,0:T(8,128)(2,1)} %get-tuple-element.29), calls=%async_computation.4 | async-start | bytes 524288 | tf_op jit(solution)/shard_map/all_to_all | solution.py:20
  99.3 3.6 %collective-permute-start.1 = (bf16[2,864,128]{2,1,0:T(8,128)(2,1)S(1)}, bf16[2,864,128]{2,1,0:T(8,128)(2,1)S(1)}, u32[]{:S(2)}, u32[]{:S(2)}) collective-permute-start(bf16[2,864,128]{2,1,0:T(8,128)(2,1)S(1)} %get-tuple-element.30.op_ref), channel_id=1, source_target_pairs={{0,1},{1,2},{2,3},{3,0},{4,5},{5,6},{6,7},{7,4},{8,9},{9,10},{10,1... | collective-permute-start | bytes 1327112 | tf_op jit(solution)/shard_map/ppermute | solution.py:29
  102.9 5.5 %all-to-all-done.4.got_ref = bf16[32,16,256]{2,1,0:T(8,128)(2,1)S(1)} async-done(((bf16[32,16,256]{2,1,0:T(8,128)(2,1)}), bf16[32,16,256]{2,1,0:T(8,128)(2,1)S(1)}, u32[]{:S(2)}, u32[]{:S(2)}) %all-to-all-start.4) | async-done | bytes 262176 | tf_op jit(solution)/shard_map/all_to_all | solution.py:20
  108.4 0.8 shard_map.99
  109.3 8.9 %all-to-all-start.5 = ((bf16[16,16,256]{2,1,0:T(8,128)(2,1)}), bf16[16,16,256]{2,1,0:T(8,128)(2,1)S(1)}, u32[]{:S(2)}, u32[]{:S(2)}) async-start(bf16[16,16,256]{2,1,0:T(8,128)(2,1)} %shard_map.99), calls=%async_computation.5 | async-start | bytes 262144 | tf_op jit(solution)/shard_map/all_to_all | solution.py:20
  118.1 0.0 collective-permute-done.2.right_ref
  118.2 3.6 %collective-permute-start.4 = (bf16[864,128]{1,0:T(8,128)(2,1)S(1)}, bf16[864,128]{1,0:T(8,128)(2,1)S(1)}, u32[]{:S(2)}, u32[]{:S(2)}) collective-permute-start(bf16[864,128]{1,0:T(8,128)(2,1)S(1)} %slice_bitcast_fusion), channel_id=1, source_target_pairs={{0,3},{1,0},{2,1},{3,2},{4,7},{5,4},{6,5},{7,6},{8,11},{9,8},{10,9... | collective-permute-start | bytes 663560 | tf_op jit(solution)/shard_map/ppermute | solution.py:29
  121.8 0.0 collective-permute-done.1.left_ref
  121.8 2.2 %collective-permute-start.3 = (bf16[864,128]{1,0:T(8,128)(2,1)S(1)}, bf16[864,128]{1,0:T(8,128)(2,1)S(1)}, u32[]{:S(2)}, u32[]{:S(2)}) collective-permute-start(bf16[864,128]{1,0:T(8,128)(2,1)S(1)} %slice_bitcast_fusion.1), channel_id=1, source_target_pairs={{0,1},{1,2},{2,3},{3,0},{4,5},{5,6},{6,7},{7,4},{8,9},{9,10},{10,1... | collective-permute-start | bytes 663560 | tf_op jit(solution)/shard_map/ppermute | solution.py:29
  124.1 2.7 %collective-permute-done.4 = bf16[864,128]{1,0:T(8,128)(2,1)S(1)} collective-permute-done((bf16[864,128]{1,0:T(8,128)(2,1)S(1)}, bf16[864,128]{1,0:T(8,128)(2,1)S(1)}, u32[]{:S(2)}, u32[]{:S(2)}) %collective-permute-start.4) | collective-permute-done | bytes 221216 | tf_op jit(solution)/shard_map/ppermute | solution.py:29
  126.8 4.6 %collective-permute-done.3 = bf16[864,128]{1,0:T(8,128)(2,1)S(1)} collective-permute-done((bf16[864,128]{1,0:T(8,128)(2,1)S(1)}, bf16[864,128]{1,0:T(8,128)(2,1)S(1)}, u32[]{:S(2)}, u32[]{:S(2)}) %collective-permute-start.3) | collective-permute-done | bytes 221216 | tf_op jit(solution)/shard_map/ppermute | solution.py:29
  131.4 1.3 all-to-all-done.5.got_ref
  132.7 1.8 %shard_map.100 = (bf16[8,16,384]{2,1,0:T(8,128)(2,1)S(1)}, f32[4,256]{1,0:T(4,128)S(1)}) custom-call(bf16[16,16,256]{2,1,0:T(8,128)(2,1)S(1)} %all-to-all-done.5.got_ref, bf16[4,2,32,256]{3,2,1,0:T(8,128)(2,1)S(1)} %all-to-all-done.1.own_ref, bf16[2,864,128]{2,1,0:T(8,128)(2,1)S(1)} %get-tuple-element.30.op_ref, ...), custom_call_target="tpu_custom_call" | custom-call | bytes 4194304 | tf_op jit(solution)/shard_map/pallas_call | solution.py:54
  134.5 8.2 %all_to_all.42.got_ref = bf16[8,16,384]{2,1,0:T(8,128)(2,1)S(1)} all-to-all(bf16[8,16,384]{2,1,0:T(8,128)(2,1)S(1)} %get-tuple-element.31), channel_id=1, replica_groups=mesh['z'=16,'x'=4,'c'=2,'y'=4] {'x','c'}, dimensions={0} | all-to-all | bytes 196608 | tf_op jit(solution)/shard_map/all_to_all | solution.py:20
  142.7 0.8 shard_map.101
  143.5 10.7 %all-to-all-start.7 = ((bf16[16,8,384]{2,1,0:T(8,128)(2,1)}), bf16[16,8,384]{2,1,0:T(8,128)(2,1)S(1)}, u32[]{:S(2)}, u32[]{:S(2)}) async-start(bf16[16,8,384]{2,1,0:T(8,128)(2,1)} %shard_map.101), calls=%async_computation.7 | async-start | bytes 196608 | tf_op jit(solution)/shard_map/all_to_all | solution.py:20
  154.2 0.0 copy-start
  154.2 1.6 shard_map.102.bare_ref
  155.8 11.1 %all-to-all-done.7.got_ref = bf16[16,8,384]{2,1,0:T(8,128)(2,1)S(1)} async-done(((bf16[16,8,384]{2,1,0:T(8,128)(2,1)}), bf16[16,8,384]{2,1,0:T(8,128)(2,1)S(1)}, u32[]{:S(2)}, u32[]{:S(2)}) %all-to-all-start.7) | async-done | bytes 98336 | tf_op jit(solution)/shard_map/all_to_all | solution.py:20
  166.9 0.0 copy-done
  166.9 2.1 %shard_map.103 = f32[2,2,256]{2,1,0:T(2,128)} custom-call(f32[3]{0:T(128)S(1)} %copy-done, bf16[16,8,384]{2,1,0:T(8,128)(2,1)S(1)} %all-to-all-done.7.got_ref, bf16[4,2,32,256]{3,2,1,0:T(8,128)(2,1)S(1)} %all-to-all-done.1.own_ref, bf16[1024,1024]{1,0:T(8,128)(2,1)S(1)} %shard_map.102.bare_ref, f32[8,256]{1,0:T(8,128)S(1)} %get-tuple-element.20.held_ref, ...), custom_call_target="tpu_custom_call" | custom-call | bytes 4194304 | tf_op jit(solution)/shard_map/pallas_call | solution.py:54
  (2 shorter events, 0.0 us)
Async XLA Ops:
  5.1 10.5 %all-to-all-start.1 = ((bf16[4,2,32,256]{3,2,1,0:T(8,128)(2,1)}), bf16[4,2,32,256]{3,2,1,0:T(8,128)(2,1)S(1)}, u32[]{:S(2)}, u32[]{:S(2)}) async-start(bf16[4,2,32,256]{3,2,1,0:T(8,128)(2,1)} %shard_map.92), calls=%async_computation.1 | async-start | bytes 262144 | tf_op jit(solution)/shard_map/all_to_all | solution.py:20
  53.3 11.4 %collective-permute-start = (bf16[16,80,256]{2,1,0:T(8,128)(2,1)S(1)}, bf16[16,80,256]{2,1,0:T(8,128)(2,1)S(1)}, u32[]{:S(2)}, u32[]{:S(2)}) collective-permute-start(bf16[16,80,256]{2,1,0:T(8,128)(2,1)S(1)} %bitcast.8), channel_id=1, source_target_pairs={{0,4},{4,0},{1,5},{5,1},{2,6},{6,2},{3,7},{7,3},{8,12},{12,8},{9,1... | collective-permute-start | bytes 1966088 | tf_op jit(solution)/shard_map/ppermute | solution.py:24
  79.0 9.9 %all-to-all-start.3 = ((bf16[4,112,256]{2,1,0:T(8,128)(2,1)}), bf16[4,112,256]{2,1,0:T(8,128)(2,1)S(1)}, u32[]{:S(2)}, u32[]{:S(2)}) async-start(bf16[4,112,256]{2,1,0:T(8,128)(2,1)} %get-tuple-element.26), calls=%async_computation.3 | async-start | bytes 458752 | tf_op jit(solution)/shard_map/all_to_all | solution.py:20
  92.3 25.9 %collective-permute-start.2 = (bf16[2,864,128]{2,1,0:T(8,128)(2,1)S(1)}, bf16[2,864,128]{2,1,0:T(8,128)(2,1)S(1)}, u32[]{:S(2)}, u32[]{:S(2)}) collective-permute-start(bf16[2,864,128]{2,1,0:T(8,128)(2,1)S(1)} %get-tuple-element.30.op_ref), channel_id=1, source_target_pairs={{0,3},{1,0},{2,1},{3,2},{4,7},{5,4},{6,5},{7,6},{8,11},{9,8},{10,9... | collective-permute-start | bytes 1327112 | tf_op jit(solution)/shard_map/ppermute | solution.py:29
  95.4 13.0 %all-to-all-start.4 = ((bf16[32,16,256]{2,1,0:T(8,128)(2,1)}), bf16[32,16,256]{2,1,0:T(8,128)(2,1)S(1)}, u32[]{:S(2)}, u32[]{:S(2)}) async-start(bf16[32,16,256]{2,1,0:T(8,128)(2,1)} %get-tuple-element.29), calls=%async_computation.4 | async-start | bytes 524288 | tf_op jit(solution)/shard_map/all_to_all | solution.py:20
  99.3 22.5 %collective-permute-start.1 = (bf16[2,864,128]{2,1,0:T(8,128)(2,1)S(1)}, bf16[2,864,128]{2,1,0:T(8,128)(2,1)S(1)}, u32[]{:S(2)}, u32[]{:S(2)}) collective-permute-start(bf16[2,864,128]{2,1,0:T(8,128)(2,1)S(1)} %get-tuple-element.30.op_ref), channel_id=1, source_target_pairs={{0,1},{1,2},{2,3},{3,0},{4,5},{5,6},{6,7},{7,4},{8,9},{9,10},{10,1... | collective-permute-start | bytes 1327112 | tf_op jit(solution)/shard_map/ppermute | solution.py:29
  109.3 23.4 %all-to-all-start.5 = ((bf16[16,16,256]{2,1,0:T(8,128)(2,1)}), bf16[16,16,256]{2,1,0:T(8,128)(2,1)S(1)}, u32[]{:S(2)}, u32[]{:S(2)}) async-start(bf16[16,16,256]{2,1,0:T(8,128)(2,1)} %shard_map.99), calls=%async_computation.5 | async-start | bytes 262144 | tf_op jit(solution)/shard_map/all_to_all | solution.py:20
  118.2 8.6 %collective-permute-start.4 = (bf16[864,128]{1,0:T(8,128)(2,1)S(1)}, bf16[864,128]{1,0:T(8,128)(2,1)S(1)}, u32[]{:S(2)}, u32[]{:S(2)}) collective-permute-start(bf16[864,128]{1,0:T(8,128)(2,1)S(1)} %slice_bitcast_fusion), channel_id=1, source_target_pairs={{0,3},{1,0},{2,1},{3,2},{4,7},{5,4},{6,5},{7,6},{8,11},{9,8},{10,9... | collective-permute-start | bytes 663560 | tf_op jit(solution)/shard_map/ppermute | solution.py:29
  121.8 9.5 %collective-permute-start.3 = (bf16[864,128]{1,0:T(8,128)(2,1)S(1)}, bf16[864,128]{1,0:T(8,128)(2,1)S(1)}, u32[]{:S(2)}, u32[]{:S(2)}) collective-permute-start(bf16[864,128]{1,0:T(8,128)(2,1)S(1)} %slice_bitcast_fusion.1), channel_id=1, source_target_pairs={{0,1},{1,2},{2,3},{3,0},{4,5},{5,6},{6,7},{7,4},{8,9},{9,10},{10,1... | collective-permute-start | bytes 663560 | tf_op jit(solution)/shard_map/ppermute | solution.py:29
  143.5 23.4 %all-to-all-start.7 = ((bf16[16,8,384]{2,1,0:T(8,128)(2,1)}), bf16[16,8,384]{2,1,0:T(8,128)(2,1)S(1)}, u32[]{:S(2)}, u32[]{:S(2)}) async-start(bf16[16,8,384]{2,1,0:T(8,128)(2,1)} %shard_map.101), calls=%async_computation.7 | async-start | bytes 196608 | tf_op jit(solution)/shard_map/all_to_all | solution.py:20
  154.2 12.7 %copy-start = (f32[3]{0:T(128)S(1)}, f32[3]{0:T(128)}, u32[]{:S(2)}) copy-start(f32[3]{0:T(128)} %cheb_ref.1) | copy-start | bytes 40
